TPU v7x, 512 devices: a whole 4x8x8 slice. The times are simulated.
512 devices in a mesh: brick: 32 (over z_hi, y), stack: 16 (over x, z_lo, core).
Axes of the slice: x: 4, y: 8, z: 8 (z_hi: 4, z_lo: 2; z = z_hi * 2 + z_lo), core: 2. Of those that a mesh axis runs over, the one named last changes fastest.
Arguments:
- estimate: float32 [256, 1024, 128], P('stack', 'brick'), may hold values from 0.5 to 2
- view_data: float32 [6, 256, 1024, 128], P(None, 'stack', 'brick'), may hold values from 0.25 to 4
- psf_taps: float32 [6, 3, 31], replicated, may hold values from 0.05 to 1
- offsets: int32 [6], replicated, may hold values from 0 to 31, as said below
- coverage: int32 [6, 32], P(None, 'brick'), may hold values from 0 to 1, as said below
Outputs:
- updated: float32 [256, 1024, 128], P('stack', 'brick')
Inputs may be any that keep to these rules, and one draw needn't show every extreme that they name: Tile j of view v images brick (j + offsets[v]) mod 32. `coverage`: every brick is covered by at least one view.
All inputs are finite; a program needn't handle non-finite values.
Results may differ from a plain program's by a relative error of at most 0.0001.
Values sent between devices are 32-bit elements; how exact they have to be, the bound alone decides.
No kernel may reach another device: no remote copies, remote signals or barrier semaphores. Data moves between devices by JAX's collectives and lax.ppermute only.
A program may use at most 128 MiB of HBM per device.

v0:
```python
import jax
import jax.numpy as jnp
from jax import lax
from jax.sharding import PartitionSpec as P


def from_behind(array, axis, by):
    peers = lax.axis_size(axis)
    return lax.ppermute(array, axis, [(i, (i + by) % peers) for i in range(peers)])


def padded_2(cells, sides, width):
    for axis, dim in sides:
        count = lax.axis_size(axis)
        ends = count - 1
        head = lax.slice_in_dim(cells, 0, width, axis=dim)
        tail = lax.slice_in_dim(cells, cells.shape[dim] - width, cells.shape[dim], axis=dim)
        cells = jnp.concatenate(
            [
                lax.ppermute(tail, axis, [(i, (i + 1) % count) for i in range(ends)]),
                cells,
                lax.ppermute(head, axis, [((i + 1) % count, i) for i in range(ends)]),
            ],
            axis=dim,
        )
    return cells


def band_matrix(taps, out_count, in_count, lead):
    out_index = jnp.arange(out_count)[:, None]
    in_index = jnp.arange(in_count)[None, :]
    distance = in_index - out_index + lead
    matrix = jnp.zeros((taps.shape[0], out_count, in_count), jnp.float32)
    for tap_index in range(taps.shape[1]):
        matrix = matrix + jnp.where(
            distance[None] == tap_index, taps[:, tap_index, None, None], jnp.float32(0.0)
        )
    return matrix


def shards(estimate, view_data, psf_taps, offsets, coverage):
    depth_cells, brick_rows, width_cells = estimate.shape
    half_width = (psf_taps.shape[2] - 1) // 2
    kernels = psf_taps / jnp.sum(psf_taps, axis=-1, keepdims=True)
    flipped = kernels[..., ::-1]
    view_tiles = view_data
    for bit_index in range((lax.axis_size("brick") - 1).bit_length()):
        shifted = from_behind(view_tiles, "brick", 1 << bit_index)
        bit_set = offsets // (1 << bit_index) % 2
        view_tiles = jnp.where((bit_set == 1)[:, None, None, None], shifted, view_tiles)
    axial_band = band_matrix(kernels[:, 0], depth_cells, depth_cells + 2 * half_width, 0)
    lateral_band = band_matrix(kernels[:, 1], brick_rows, brick_rows + 2 * half_width, 0)
    across_band = band_matrix(kernels[:, 2], width_cells, width_cells, half_width)
    across_back = band_matrix(flipped[:, 2], width_cells, width_cells, half_width)
    lateral_back = band_matrix(flipped[:, 1], brick_rows, brick_rows + 2 * half_width, 0)
    axial_back = band_matrix(flipped[:, 0], depth_cells, depth_cells + 2 * half_width, 0)
    highest = lax.Precision.HIGHEST
    padded = padded_2(estimate, (("stack", 0),), half_width)
    axial_blur = jnp.einsum("vij,jyx->viyx", axial_band, padded, precision=highest)
    lateral = padded_2(axial_blur, (("brick", 2),), half_width)
    sideways = jnp.einsum("vij,vzjx->vzix", lateral_band, lateral, precision=highest)
    cover_mask = coverage[:, 0].astype(jnp.float32)
    blurred = jnp.einsum("vzyj,vij->vzyi", sideways, across_band, precision=highest)
    ratio_field = cover_mask[:, None, None, None] * view_tiles / blurred
    across = jnp.einsum("vzyj,vij->vzyi", ratio_field, across_back, precision=highest)
    wide_ratio = padded_2(across, (("brick", 2),), half_width)
    back_lateral = jnp.einsum("vij,vzjx->vzix", lateral_back, wide_ratio, precision=highest)
    tall_ratio = padded_2(back_lateral, (("stack", 1),), half_width)
    back_axial = jnp.einsum("vij,vjyx->viyx", axial_back, tall_ratio, precision=highest)
    summed = jnp.sum(back_axial, axis=0)
    cover_count = jnp.sum(cover_mask)
    return estimate * summed / cover_count


def solution(mesh):
    placed = (
        P("stack", "brick", None),
        P(None, "stack", "brick", None),
        P(),
        P(),
        P(None, "brick"),
    )
    return jax.shard_map(
        shards, mesh=mesh, in_specs=placed, out_specs=P("stack", "brick", None), check_vma=False
    )
```

profile of v0, /device:TPU:58, one launch (start us, length us, event | category | flops | bytes accessed | tf_op | source)
XLA Modules:
  0.0 588.8 jit_solution(15871637166853577632)
XLA Ops:
  4.0 4.5 collective-permute-start.6
  8.5 5.3 collective-permute-start
  14.9 64.0 %collective-permute-done = f32[6,16,32,128]{3,2,1,0:T(8,128)S(1)} collective-permute-done((f32[6,16,32,128]{3,2,1,0:T(8,128)S(1)}, f32[6,16,32,128]{3,2,1,0:T(8,128)S(1)}, u32[]{:S(2)}, u32[]{:S(2)}) %collective-permute-start) | collective-permute-done | bytes 1572896 | tf_op jit(solution)/shard_map/ppermute | solution.py:9
  84.4 66.8 %collective-permute-done.1 = f32[6,16,32,128]{3,2,1,0:T(8,128)S(1)} collective-permute-done((f32[6,16,32,128]{3,2,1,0:T(8,128)S(1)}, f32[6,16,32,128]{3,2,1,0:T(8,128)S(1)}, u32[]{:S(2)}, u32[]{:S(2)}) %collective-permute-start.1) | collective-permute-done | bytes 1572896 | tf_op jit(solution)/shard_map/ppermute | solution.py:9
  156.0 70.1 %collective-permute-done.2 = f32[6,16,32,128]{3,2,1,0:T(8,128)S(1)} collective-permute-done((f32[6,16,32,128]{3,2,1,0:T(8,128)S(1)}, f32[6,16,32,128]{3,2,1,0:T(8,128)S(1)}, u32[]{:S(2)}, u32[]{:S(2)}) %collective-permute-start.2) | collective-permute-done | bytes 1572896 | tf_op jit(solution)/shard_map/ppermute | solution.py:9
  226.5 3.0 collective-permute-start.3
  230.2 2.8 fusion.28
  233.2 70.6 %collective-permute-start.7 = (f32[6,16,15,128]{3,1,2,0:T(8,128)S(1)}, f32[6,16,15,128]{3,1,2,0:T(8,128)S(1)}, u32[]{:S(2)}, u32[]{:S(2)}) collective-permute-start(f32[6,16,15,128]{3,1,2,0:T(8,128)S(1)} %get-tuple-element.195), channel_id=1, source_target_pairs={{0,16},{16,32},{32,48},{48,64},{64,80},{80,96},{96,112},{112,128},... | collective-permute-start | bytes 2211848 | tf_op jit(solution)/shard_map/ppermute | solution.py:20
  303.8 7.6 %collective-permute-start.8 = (f32[6,16,15,128]{3,1,2,0:T(8,128)S(1)}, f32[6,16,15,128]{3,1,2,0:T(8,128)S(1)}, u32[]{:S(2)}, u32[]{:S(2)}) collective-permute-start(f32[6,16,15,128]{3,1,2,0:T(8,128)S(1)} %get-tuple-element.196), channel_id=1, source_target_pairs={{16,0},{32,16},{48,32},{64,48},{80,64},{96,80},{112,96},{128,112},... | collective-permute-start | bytes 2211848 | tf_op jit(solution)/shard_map/ppermute | solution.py:22
  315.3 17.0 %collective-permute-done.7 = f32[6,16,15,128]{3,1,2,0:T(8,128)S(1)} collective-permute-done((f32[6,16,15,128]{3,1,2,0:T(8,128)S(1)}, f32[6,16,15,128]{3,1,2,0:T(8,128)S(1)}, u32[]{:S(2)}, u32[]{:S(2)}) %collective-permute-start.7) | collective-permute-done | bytes 737312 | tf_op jit(solution)/shard_map/ppermute | solution.py:20
  332.3 7.0 %collective-permute-done.8 = f32[6,16,15,128]{3,1,2,0:T(8,128)S(1)} collective-permute-done((f32[6,16,15,128]{3,1,2,0:T(8,128)S(1)}, f32[6,16,15,128]{3,1,2,0:T(8,128)S(1)}, u32[]{:S(2)}, u32[]{:S(2)}) %collective-permute-start.8) | collective-permute-done | bytes 737312 | tf_op jit(solution)/shard_map/ppermute | solution.py:22
  339.9 3.4 fusion.8
  343.3 2.9 fusion.10
  346.2 33.5 %collective-permute-done.4 = f32[6,16,32,128]{3,2,1,0:T(8,128)S(1)} collective-permute-done((f32[6,16,32,128]{3,2,1,0:T(8,128)S(1)}, f32[6,16,32,128]{3,2,1,0:T(8,128)S(1)}, u32[]{:S(2)}, u32[]{:S(2)}) %collective-permute-start.4) | collective-permute-done | bytes 1572896 | tf_op jit(solution)/shard_map/ppermute | solution.py:9
  379.8 3.1 fusion.12
  383.3 132.5 %collective-permute-start.9 = (f32[6,16,15,128]{3,1,2,0:T(8,128)S(1)}, f32[6,16,15,128]{3,1,2,0:T(8,128)S(1)}, u32[]{:S(2)}, u32[]{:S(2)}) collective-permute-start(f32[6,16,15,128]{3,1,2,0:T(8,128)S(1)} %copy.25), channel_id=1, source_target_pairs={{0,16},{16,32},{32,48},{48,64},{64,80},{80,96},{96,112},{112,128},... | collective-permute-start | bytes 2211848 | tf_op jit(solution)/shard_map/ppermute | solution.py:20
  516.9 2.1 collective-permute-start.10
  520.2 11.5 %collective-permute-done.9 = f32[6,16,15,128]{3,1,2,0:T(8,128)S(1)} collective-permute-done((f32[6,16,15,128]{3,1,2,0:T(8,128)S(1)}, f32[6,16,15,128]{3,1,2,0:T(8,128)S(1)}, u32[]{:S(2)}, u32[]{:S(2)}) %collective-permute-start.9) | collective-permute-done | bytes 737312 | tf_op jit(solution)/shard_map/ppermute | solution.py:20
  532.0 8.2 %collective-permute-done.10 = f32[6,16,15,128]{3,1,2,0:T(8,128)} collective-permute-done((f32[6,16,15,128]{3,1,2,0:T(8,128)}, f32[6,16,15,128]{3,1,2,0:T(8,128)}, u32[]{:S(2)}, u32[]{:S(2)}) %collective-permute-start.10) | collective-permute-done | bytes 737312 | tf_op jit(solution)/shard_map/ppermute | solution.py:22
  541.9 3.1 fusion.16
  549.0 4.5 collective-permute-start.12
  555.1 13.8 %collective-permute-done.11 = f32[6,15,32,128]{3,2,1,0:T(8,128)S(1)} collective-permute-done((f32[6,15,32,128]{3,2,1,0:T(8,128)}, f32[6,15,32,128]{3,2,1,0:T(8,128)S(1)}, u32[]{:S(2)}, u32[]{:S(2)}) %collective-permute-start.11) | collective-permute-done | bytes 1474592 | tf_op jit(solution)/shard_map/ppermute | solution.py:20
  568.8 11.3 %collective-permute-done.12 = f32[6,15,32,128]{3,2,1,0:T(8,128)} collective-permute-done((f32[6,15,32,128]{3,2,1,0:T(8,128)}, f32[6,15,32,128]{3,2,1,0:T(8,128)}, u32[]{:S(2)}, u32[]{:S(2)}) %collective-permute-start.12) | collective-permute-done | bytes 1474592 | tf_op jit(solution)/shard_map/ppermute | solution.py:22
  582.1 6.0 %fusion.25 = f32[16,32,128]{2,0,1:T(8,128)S(1)} fusion(f32[6,46,32,128]{3,2,1,0:T(8,128)S(1)} %pad_maximum_fusion, f32[]{:T(128)} %convert_reduce_fusion, f32[6]{0:T(128)S(1)} %get-tuple-element.6, f32[6]{0:T(128)S(1)} %get-tuple-element.7, f32[6]{0:T(128)S(1)} %get-tuple-element.8, f32[6]{0:T(128)S(1)} %get-tuple-element.9, f32[6]{0:T(128)S(1)} %get-tuple-element.10, ...), kind=kOutput, calls=%fused_computation.21 | convolution fusion | flops 217455680 | bytes 5069836 | tf_op jit(solution)/shard_map/vij,vjyx->viyx/dot_general | solution.py:69
  (218 shorter events, 32.7 us)
Async XLA Ops:
  2.1 228.2 %collective-permute-start.5 = (f32[15,32,128]{2,0,1:T(8,128)}, f32[15,32,128]{2,0,1:T(8,128)}, u32[]{:S(2)}, u32[]{:S(2)}) collective-permute-start(f32[15,32,128]{2,0,1:T(8,128)} %get-tuple-element.197), channel_id=1, source_target_pairs={{0,1},{1,2},{2,3},{3,4},{4,5},{5,6},{6,7},{7,8},{8,9},{9,10},{10,1... | collective-permute-start | bytes 737288 | tf_op jit(solution)/shard_map/ppermute | solution.py:20
  4.0 226.3 %collective-permute-start.6 = (f32[15,32,128]{2,0,1:T(8,128)}, f32[15,32,128]{2,0,1:T(8,128)}, u32[]{:S(2)}, u32[]{:S(2)}) collective-permute-start(f32[15,32,128]{2,0,1:T(8,128)} %get-tuple-element.198), channel_id=1, source_target_pairs={{1,0},{2,1},{3,2},{4,3},{5,4},{6,5},{7,6},{8,7},{9,8},{10,9},{11,1... | collective-permute-start | bytes 737288 | tf_op jit(solution)/shard_map/ppermute | solution.py:22
  8.5 70.4 %collective-permute-start = (f32[6,16,32,128]{3,2,1,0:T(8,128)S(1)}, f32[6,16,32,128]{3,2,1,0:T(8,128)S(1)}, u32[]{:S(2)}, u32[]{:S(2)}) collective-permute-start(f32[6,16,32,128]{3,2,1,0:T(8,128)S(1)} %copy-done), channel_id=1, source_target_pairs={{0,16},{16,32},{32,48},{48,64},{64,80},{80,96},{96,112},{112,128},... | collective-permute-start | bytes 4718600 | tf_op jit(solution)/shard_map/ppermute | solution.py:9
  81.9 69.3 %collective-permute-start.1 = (f32[6,16,32,128]{3,2,1,0:T(8,128)S(1)}, f32[6,16,32,128]{3,2,1,0:T(8,128)S(1)}, u32[]{:S(2)}, u32[]{:S(2)}) collective-permute-start(f32[6,16,32,128]{3,2,1,0:T(8,128)S(1)} %broadcast_select_fusion), channel_id=1, source_target_pairs={{0,32},{16,48},{32,64},{48,80},{64,96},{80,112},{96,128},{112,144}... | collective-permute-start | bytes 4718600 | tf_op jit(solution)/shard_map/ppermute | solution.py:9
  83.9 255.7 %copy-start.4 = (pred[32,62]{1,0:T(8,128)(4,1)}, pred[32,62]{1,0:T(8,128)(4,1)S(1)}, u32[]{:S(2)}) copy-start(pred[32,62]{1,0:T(8,128)(4,1)S(1)} %get-tuple-element.244) | copy-start | bytes 5956
  84.0 255.7 %copy-start.6 = (pred[32,62]{1,0:T(8,128)(4,1)}, pred[32,62]{1,0:T(8,128)(4,1)S(1)}, u32[]{:S(2)}) copy-start(pred[32,62]{1,0:T(8,128)(4,1)S(1)} %get-tuple-element.245) | copy-start | bytes 5956
  84.0 255.7 %copy-start.8 = (pred[32,62]{1,0:T(8,128)(4,1)}, pred[32,62]{1,0:T(8,128)(4,1)S(1)}, u32[]{:S(2)}) copy-start(pred[32,62]{1,0:T(8,128)(4,1)S(1)} %get-tuple-element.246) | copy-start | bytes 5956
  84.0 255.7 %copy-start.10 = (pred[32,62]{1,0:T(8,128)(4,1)}, pred[32,62]{1,0:T(8,128)(4,1)S(1)}, u32[]{:S(2)}) copy-start(pred[32,62]{1,0:T(8,128)(4,1)S(1)} %get-tuple-element.247) | copy-start | bytes 5956
  84.0 255.7 %copy-start.12 = (pred[32,62]{1,0:T(8,128)(4,1)}, pred[32,62]{1,0:T(8,128)(4,1)S(1)}, u32[]{:S(2)}) copy-start(pred[32,62]{1,0:T(8,128)(4,1)S(1)} %get-tuple-element.248) | copy-start | bytes 5956
  84.0 255.7 %copy-start.14 = (pred[32,62]{1,0:T(8,128)(4,1)}, pred[32,62]{1,0:T(8,128)(4,1)S(1)}, u32[]{:S(2)}) copy-start(pred[32,62]{1,0:T(8,128)(4,1)S(1)} %get-tuple-element.249) | copy-start | bytes 5956
  84.1 255.7 %copy-start.16 = (pred[32,62]{1,0:T(8,128)(4,1)}, pred[32,62]{1,0:T(8,128)(4,1)S(1)}, u32[]{:S(2)}) copy-start(pred[32,62]{1,0:T(8,128)(4,1)S(1)} %get-tuple-element.250) | copy-start | bytes 5956
  84.1 255.7 %copy-start.18 = (pred[32,62]{1,0:T(8,128)(4,1)}, pred[32,62]{1,0:T(8,128)(4,1)S(1)}, u32[]{:S(2)}) copy-start(pred[32,62]{1,0:T(8,128)(4,1)S(1)} %get-tuple-element.251) | copy-start | bytes 5956
  84.1 255.6 %copy-start.20 = (pred[32,62]{1,0:T(8,128)(4,1)}, pred[32,62]{1,0:T(8,128)(4,1)S(1)}, u32[]{:S(2)}) copy-start(pred[32,62]{1,0:T(8,128)(4,1)S(1)} %get-tuple-element.252) | copy-start | bytes 5956
  84.1 255.6 %copy-start.22 = (pred[32,62]{1,0:T(8,128)(4,1)}, pred[32,62]{1,0:T(8,128)(4,1)S(1)}, u32[]{:S(2)}) copy-start(pred[32,62]{1,0:T(8,128)(4,1)S(1)} %get-tuple-element.253) | copy-start | bytes 5956
  84.1 255.6 %copy-start.24 = (pred[32,62]{1,0:T(8,128)(4,1)}, pred[32,62]{1,0:T(8,128)(4,1)S(1)}, u32[]{:S(2)}) copy-start(pred[32,62]{1,0:T(8,128)(4,1)S(1)} %get-tuple-element.254) | copy-start | bytes 5956
  152.3 73.8 %collective-permute-start.2 = (f32[6,16,32,128]{3,2,1,0:T(8,128)S(1)}, f32[6,16,32,128]{3,2,1,0:T(8,128)S(1)}, u32[]{:S(2)}, u32[]{:S(2)}) collective-permute-start(f32[6,16,32,128]{3,2,1,0:T(8,128)S(1)} %broadcast_select_fusion.1), channel_id=1, source_target_pairs={{0,64},{16,80},{32,96},{48,112},{64,128},{80,144},{96,160},{112,17... | collective-permute-start | bytes 4718600 | tf_op jit(solution)/shard_map/ppermute | solution.py:9
  226.5 84.8 %collective-permute-start.3 = (f32[6,16,32,128]{3,2,1,0:T(8,128)S(1)}, f32[6,16,32,128]{3,2,1,0:T(8,128)S(1)}, u32[]{:S(2)}, u32[]{:S(2)}) collective-permute-start(f32[6,16,32,128]{3,2,1,0:T(8,128)S(1)} %broadcast_select_fusion.2), channel_id=1, source_target_pairs={{0,128},{16,144},{32,160},{48,176},{64,192},{80,208},{96,224},{112... | collective-permute-start | bytes 4718600 | tf_op jit(solution)/shard_map/ppermute | solution.py:9
  233.2 99.1 %collective-permute-start.7 = (f32[6,16,15,128]{3,1,2,0:T(8,128)S(1)}, f32[6,16,15,128]{3,1,2,0:T(8,128)S(1)}, u32[]{:S(2)}, u32[]{:S(2)}) collective-permute-start(f32[6,16,15,128]{3,1,2,0:T(8,128)S(1)} %get-tuple-element.195), channel_id=1, source_target_pairs={{0,16},{16,32},{32,48},{48,64},{64,80},{80,96},{96,112},{112,128},... | collective-permute-start | bytes 2211848 | tf_op jit(solution)/shard_map/ppermute | solution.py:20
  303.8 35.6 %collective-permute-start.8 = (f32[6,16,15,128]{3,1,2,0:T(8,128)S(1)}, f32[6,16,15,128]{3,1,2,0:T(8,128)S(1)}, u32[]{:S(2)}, u32[]{:S(2)}) collective-permute-start(f32[6,16,15,128]{3,1,2,0:T(8,128)S(1)} %get-tuple-element.196), channel_id=1, source_target_pairs={{16,0},{32,16},{48,32},{64,48},{80,64},{96,80},{112,96},{128,112},... | collective-permute-start | bytes 2211848 | tf_op jit(solution)/shard_map/ppermute | solution.py:22
  311.8 68.0 %collective-permute-start.4 = (f32[6,16,32,128]{3,2,1,0:T(8,128)S(1)}, f32[6,16,32,128]{3,2,1,0:T(8,128)S(1)}, u32[]{:S(2)}, u32[]{:S(2)}) collective-permute-start(f32[6,16,32,128]{3,2,1,0:T(8,128)S(1)} %broadcast_select_fusion.3), channel_id=1, source_target_pairs={{0,256},{16,272},{32,288},{48,304},{64,320},{80,336},{96,352},{112... | collective-permute-start | bytes 4718600 | tf_op jit(solution)/shard_map/ppermute | solution.py:9
  383.3 148.5 %collective-permute-start.9 = (f32[6,16,15,128]{3,1,2,0:T(8,128)S(1)}, f32[6,16,15,128]{3,1,2,0:T(8,128)S(1)}, u32[]{:S(2)}, u32[]{:S(2)}) collective-permute-start(f32[6,16,15,128]{3,1,2,0:T(8,128)S(1)} %copy.25), channel_id=1, source_target_pairs={{0,16},{16,32},{32,48},{48,64},{64,80},{80,96},{96,112},{112,128},... | collective-permute-start | bytes 2211848 | tf_op jit(solution)/shard_map/ppermute | solution.py:20
  516.9 23.3 %collective-permute-start.10 = (f32[6,16,15,128]{3,1,2,0:T(8,128)}, f32[6,16,15,128]{3,1,2,0:T(8,128)}, u32[]{:S(2)}, u32[]{:S(2)}) collective-permute-start(f32[6,16,15,128]{3,1,2,0:T(8,128)} %copy.26), channel_id=1, source_target_pairs={{16,0},{32,16},{48,32},{64,48},{80,64},{96,80},{112,96},{128,112},... | collective-permute-start | bytes 2211848 | tf_op jit(solution)/shard_map/ppermute | solution.py:22
  547.1 21.8 %collective-permute-start.11 = (f32[6,15,32,128]{3,2,1,0:T(8,128)}, f32[6,15,32,128]{3,2,1,0:T(8,128)S(1)}, u32[]{:S(2)}, u32[]{:S(2)}) collective-permute-start(f32[6,15,32,128]{3,2,1,0:T(8,128)} %get-tuple-element.191), channel_id=1, source_target_pairs={{0,1},{1,2},{2,3},{3,4},{4,5},{5,6},{6,7},{7,8},{8,9},{9,10},{10,1... | collective-permute-start | bytes 4423688 | tf_op jit(solution)/shard_map/ppermute | solution.py:20
  549.0 31.1 %collective-permute-start.12 = (f32[6,15,32,128]{3,2,1,0:T(8,128)}, f32[6,15,32,128]{3,2,1,0:T(8,128)}, u32[]{:S(2)}, u32[]{:S(2)}) collective-permute-start(f32[6,15,32,128]{3,2,1,0:T(8,128)} %get-tuple-element.192), channel_id=1, source_target_pairs={{1,0},{2,1},{3,2},{4,3},{5,4},{6,5},{7,6},{8,7},{9,8},{10,9},{11,1... | collective-permute-start | bytes 4423688 | tf_op jit(solution)/shard_map/ppermute | solution.py:22
  (51 other events, 4663.2 us)
where the time goes:
time: 594 us; the launch traced here: 589 us
  waiting for transfers between devices  303 us (51%)
  starting transfers between devices  240 us (40%)
  matrix products  21.3 us (4%)
  local copies, waits for them, and re-layouts  14.8 us (2%)
  other arithmetic  8.05 us (1%)
    ppermute x5, waiting for transfers between devices, from_behind(): lax.ppermute(array, axis, [(i, (i + by) % peers) for i in range(peers)])  234 us
    ppermute x4, starting transfers between devices, padded_2(): lax.ppermute(tail, axis, [(i, (i + 1) % count) for i in range(ends)])  207 us
    ppermute x4, waiting for transfers between devices, padded_2(): lax.ppermute(tail, axis, [(i, (i + 1) % count) for i in range(ends)])  42.3 us
    ppermute x4, waiting for transfers between devices, padded_2(): lax.ppermute(head, axis, [((i + 1) % count, i) for i in range(ends)])  26.5 us
    ppermute x4, starting transfers between devices, padded_2(): lax.ppermute(head, axis, [((i + 1) % count, i) for i in range(ends)])  18.8 us
    ppermute x5, starting transfers between devices, from_behind(): lax.ppermute(array, axis, [(i, (i + by) % peers) for i in range(peers)])  14.2 us
  transfers between devices with their start and end apart: 13, of which 10 were waited for; matrix products, arithmetic and copies ran while one was open for 4% of the time, Pallas kernels for 0%

commit v1 on v0

v1 whole, which is shorter than its diff:
```python
import functools

import jax
import jax.numpy as jnp
from jax import lax
from jax.experimental import pallas as pl
from jax.experimental.pallas import tpu as pltpu
from jax.sharding import PartitionSpec as P

F32, BF16 = jnp.float32, jnp.bfloat16


def split(values):
    high = values.astype(BF16)
    return high, (values - high.astype(F32)).astype(BF16)


def split_outside(values):
    high = lax.reduce_precision(values, 8, 7)
    return high.astype(BF16), (values - high).astype(BF16)


def dot(left, right):
    return jnp.dot(left, right, preferred_element_type=F32)


def band(taps, rows, columns, lead):
    count = taps.shape[1]
    tap = jnp.arange(columns)[None, :] - jnp.arange(rows)[:, None] + lead
    chosen = jnp.arange(count)[None, None, :] == tap[:, :, None]
    return jnp.sum(jnp.where(chosen[None], taps[:, None, None, :], 0.0), axis=-1)


def forward_kernel(half, taps_ref, low_ref, mid_ref, high_ref, lateral_ref, across_ref, out_ref, wide_ref):
    views, depth, rows, width = out_ref.shape
    refs = (low_ref, mid_ref, high_ref)
    for part in range(3):

        def lateral(pair, carry, part=part):
            z = pair * 2
            first_h, first_l = split(refs[part][z])
            second_h, second_l = split(refs[part][z + 1])
            upper = jnp.concatenate([first_h, second_h], axis=1)
            lower = jnp.concatenate([first_l, second_l], axis=1)
            stacked = jnp.concatenate([upper, lower, upper], axis=0)
            result = dot(lateral_ref[...], stacked)
            wide_ref[part * depth + z] = result[:, :width]
            wide_ref[part * depth + z + 1] = result[:, width:]
            return carry

        lax.fori_loop(0, depth // 2, lateral, 0)

    taps = taps_ref.shape[1]
    start = depth - half
    groups = rows // 8

    def axial(step, carry):
        view, group = step // groups, step % groups
        at = pl.ds(pl.multiple_of(view * rows + group * 8, 8), 8)
        field = [wide_ref[z, at, :] for z in range(start, start + depth + taps - 1)]
        for z in range(depth):
            total = taps_ref[view, 0] * field[z]
            for t in range(1, taps):
                total += taps_ref[view, t] * field[z + t]
            out_ref[view, z, pl.ds(pl.multiple_of(group * 8, 8), 8), :] = total
        return carry

    lax.fori_loop(0, views * groups, axial, 0)

    def across(view, carry):
        field = out_ref[view].reshape(depth * rows, width)
        upper, lower = split(field)
        both = dot(jnp.concatenate([upper, lower], axis=1), across_ref[view])
        out_ref[view] = (both[:, :width] + both[:, width:]).reshape(depth, rows, width)
        return carry

    lax.fori_loop(0, views, across, 0)


def back_kernel(half, taps_ref, cover_ref, tiles_ref, blurred_ref, across_ref, lateral_ref, low_ref, mid_ref, high_ref, near_ref, wide_ref):
    views, depth, rows, width = blurred_ref.shape
    halves = tiles_ref.shape[1]

    def across(view, carry):
        owned = jnp.concatenate([tiles_ref[:, part, view] for part in range(halves)], axis=1)
        ratio = (cover_ref[view].astype(F32) * owned / blurred_ref[view]).reshape(depth * rows, width)
        upper, lower = split(ratio)
        both = dot(jnp.concatenate([upper, lower], axis=1), across_ref[view])
        near_ref[view] = (both[:, :width] + both[:, width:]).reshape(depth, rows, width)
        return carry

    lax.fori_loop(0, views, across, 0)

    taps = taps_ref.shape[1]
    start = depth - half
    groups = rows // 8

    def axial(step, carry):
        view, group = step // groups, step % groups
        at = pl.ds(pl.multiple_of(group * 8, 8), 8)
        into = pl.ds(pl.multiple_of(view * rows + group * 8, 8), 8)
        field = [near_ref[view, z, at, :] for z in range(depth)]
        for z in range(3 * depth):
            total = None
            for source in range(depth):
                t = z - start - source
                if 0 <= t < taps:
                    term = taps_ref[view, t] * field[source]
                    total = term if total is None else total + term
            wide_ref[z, into, :] = jnp.zeros((8, width), F32) if total is None else total
        return carry

    lax.fori_loop(0, views * groups, axial, 0)

    outs = (low_ref, mid_ref, high_ref)
    for part in range(3):

        def lateral(pair, carry, part=part):
            z = part * depth + pair * 2
            first_h, first_l = split(wide_ref[z])
            second_h, second_l = split(wide_ref[z + 1])
            upper = jnp.concatenate([first_h, second_h], axis=1)
            lower = jnp.concatenate([first_l, second_l], axis=1)
            result = dot(lateral_ref[0], upper) + dot(lateral_ref[0], lower) + dot(lateral_ref[1], upper)
            outs[part][pair * 2] = result[:, :width]
            outs[part][pair * 2 + 1] = result[:, width:]
            return carry

        lax.fori_loop(0, depth // 2, lateral, 0)


def turn_kernel(ring, offsets_ref, in_ref, out_ref):
    views = in_ref.shape[1]

    def body(place, carry):
        for view in range(views):
            source = lax.rem(place + ring - lax.rem(offsets_ref[view], ring), ring)
            out_ref[place, view] = in_ref[source, view]
        return carry

    lax.fori_loop(0, ring, body, 0)


SMEM = pl.BlockSpec(memory_space=pltpu.SMEM)
VMEM = pl.BlockSpec(memory_space=pltpu.VMEM)
PARAMS = pltpu.CompilerParams(vmem_limit_bytes=48 << 20)


def shards(estimate, view_data, psf_taps, offsets, coverage):
    depth, rows, width = estimate.shape
    views = view_data.shape[0]
    half = (psf_taps.shape[2] - 1) // 2
    reach = half + 1
    ring = lax.axis_size("brick")
    stacks = lax.axis_size("stack")
    up = [(i, i + 1) for i in range(stacks - 1)]
    down = [(i + 1, i) for i in range(stacks - 1)]
    right = [(i, i + 1) for i in range(ring - 1)]
    left = [(i + 1, i) for i in range(ring - 1)]

    parts = ring // depth
    strip = rows // parts
    pieces = view_data.reshape(views, ring, strip, width).transpose(1, 0, 2, 3)
    spread = lax.all_to_all(pieces, "brick", 0, 0, tiled=True)

    head = lax.ppermute(estimate[:, rows - reach :], "brick", right)
    tail = lax.ppermute(estimate[:, :reach], "brick", left)
    mid = jnp.concatenate([head, estimate, tail], axis=1)
    low = lax.ppermute(mid, "stack", up)
    high = lax.ppermute(mid, "stack", down)

    kernels = psf_taps / jnp.sum(psf_taps, axis=-1, keepdims=True)
    flipped = kernels[..., ::-1]
    wide = rows + 2 * reach
    lateral = band(kernels[:, 1], rows, wide, half - reach)
    lateral_h, lateral_l = split_outside(lateral.reshape(views * rows, wide))
    lateral_on = jnp.concatenate([lateral_h, lateral_h, lateral_l], axis=1)
    lateral_back = lateral.transpose(2, 0, 1).reshape(wide, views * rows)
    lateral_back = jnp.stack(split_outside(lateral_back))

    def across_of(taps):
        high_part, low_part = split_outside(band(taps, width, width, half).transpose(0, 2, 1))
        top = jnp.concatenate([high_part, low_part], axis=2)
        return jnp.concatenate([top, jnp.concatenate([high_part, jnp.zeros_like(low_part)], axis=2)], axis=1)

    across_on, across_back = across_of(kernels[:, 2]), across_of(flipped[:, 2])

    blurred = pl.pallas_call(
        functools.partial(forward_kernel, half),
        out_shape=jax.ShapeDtypeStruct((views, depth, rows, width), F32),
        in_specs=[SMEM, VMEM, VMEM, VMEM, VMEM, VMEM],
        out_specs=VMEM,
        scratch_shapes=[pltpu.VMEM((3 * depth, views * rows, width), F32)],
        compiler_params=PARAMS,
        name="forward",
    )(kernels[:, 0], low, mid, high, lateral_on, across_on)

    turned = pl.pallas_call(
        functools.partial(turn_kernel, ring),
        out_shape=jax.ShapeDtypeStruct(spread.shape, F32),
        in_specs=[SMEM, VMEM],
        out_specs=VMEM,
        compiler_params=PARAMS,
        name="turn",
    )(offsets, spread)
    tiles = lax.all_to_all(turned, "brick", 0, 0, tiled=True)
    tiles = tiles.reshape(depth, parts, views, strip, width)

    slab = jax.ShapeDtypeStruct((depth, wide, width), F32)
    below, own, above = pl.pallas_call(
        functools.partial(back_kernel, half),
        out_shape=(slab, slab, slab),
        in_specs=[SMEM, SMEM, VMEM, VMEM, VMEM, VMEM],
        out_specs=(VMEM, VMEM, VMEM),
        scratch_shapes=[
            pltpu.VMEM((views, depth, rows, width), F32),
            pltpu.VMEM((3 * depth, views * rows, width), F32),
        ],
        compiler_params=PARAMS,
        name="back",
    )(kernels[:, 0], coverage[:, 0], tiles, blurred, across_back, lateral_back)

    total = own + lax.ppermute(below, "stack", down) + lax.ppermute(above, "stack", up)
    from_right = lax.ppermute(total[:, :reach], "brick", left)
    from_left = lax.ppermute(total[:, rows + reach :], "brick", right)
    summed = total[:, reach : rows + reach]
    gap = jnp.zeros((depth, rows - reach, width), F32)
    summed = summed + jnp.concatenate([from_left, gap], axis=1) + jnp.concatenate([gap, from_right], axis=1)
    cover_count = jnp.sum(coverage[:, 0].astype(F32))
    return estimate * summed / cover_count


def solution(mesh):
    placed = (
        P("stack", "brick", None),
        P(None, "stack", "brick", None),
        P(),
        P(),
        P(None, "brick"),
    )
    return jax.shard_map(
        shards, mesh=mesh, in_specs=placed, out_specs=P("stack", "brick", None), check_vma=False
    )
```

time: 594 us -> 189 us (0.32)
  the two profiles are of different devices: /device:TPU:58 before, /device:TPU:254 now
where the time goes in v1:
time: 189 us; the launch traced here: 188 us
  waiting for transfers between devices  84.5 us (45%)
  starting transfers between devices  46.7 us (25%)
  Pallas kernels  31.7 us (17%)
  local copies, waits for them, and re-layouts  13.6 us (7%)
  other arithmetic  11.4 us (6%)
    all_to_all x1, waiting for transfers between devices, shards(): spread = lax.all_to_all(pieces, 'brick', 0, 0, tiled=True)  34.3 us
    ppermute x1, waiting for transfers between devices, shards(): low = lax.ppermute(mid, 'stack', up)  27.6 us
    pallas_call x1, Pallas kernels, shards(): pl.pallas_call(functools.partial(forward_kernel, half), out_shape=jax.Sha...  15.2 us
    pallas_call x1, Pallas kernels, shards(): pl.pallas_call(functools.partial(back_kernel, half), out_shape=(slab, sla...  13.9 us
    all_to_all x1, starting transfers between devices, shards(): spread = lax.all_to_all(pieces, 'brick', 0, 0, tiled=True)  12.9 us
    ppermute x1, waiting for transfers between devices, shards(): from_right = lax.ppermute(total[:, :reach], 'brick', left)  9.74 us
    ppermute x1, waiting for transfers between devices, shards(): lax.ppermute(above, 'stack', up)  8.58 us
    all_to_all x1, starting transfers between devices, shards(): tiles = lax.all_to_all(turned, 'brick', 0, 0, tiled=True)  7.46 us
  transfers between devices with their start and end apart: 10, of which 5 were waited for; matrix products, arithmetic and copies ran while one was open for 8% of the time, Pallas kernels for 9%

profile of v1, /device:TPU:254, one launch (start us, length us, event | category | flops | bytes accessed | tf_op | source)
XLA Modules:
  0.0 188.2 jit_solution(3732127740057016543)
XLA Ops:
  0.0 2.8 %copy.26 = f32[6,32,16,128]{3,2,0,1:T(8,128)} copy(f32[6,32,16,128]{3,2,1,0:T(8,128)} %bitcast.28) | data formatting | bytes 3145728 | tf_op jit(solution)/shard_map/reshape | solution.py:163
  2.8 12.9 %all-to-all-start = ((f32[32,6,16,128]{3,2,1,0:T(8,128)}), f32[32,6,16,128]{3,2,1,0:T(8,128)S(1)}, u32[]{:S(2)}, u32[]{:S(2)}) async-start(f32[32,6,16,128]{3,2,1,0:T(8,128)} %bitcast.25), calls=%async_computation | async-start | bytes 3145728 | tf_op jit(solution)/shard_map/all_to_all | solution.py:164
  16.4 5.5 %collective-permute-start = (f32[16,16,128]{2,1,0:T(8,128)}, f32[16,16,128]{2,1,0:T(8,128)}, u32[]{:S(2)}, u32[]{:S(2)}) collective-permute-start(f32[16,16,128]{2,1,0:T(8,128)} %get-tuple-element.20), channel_id=1, source_target_pairs={{0,16},{16,32},{32,48},{48,64},{64,80},{80,96},{96,112},{112,128},... | collective-permute-start | bytes 393224 | tf_op jit(solution)/shard_map/ppermute | solution.py:166
  21.9 1.9 %collective-permute-start.1 = (f32[16,16,128]{2,1,0:T(8,128)}, f32[16,16,128]{2,1,0:T(8,128)}, u32[]{:S(2)}, u32[]{:S(2)}) collective-permute-start(f32[16,16,128]{2,1,0:T(8,128)} %get-tuple-element.19), channel_id=1, source_target_pairs={{16,0},{32,16},{48,32},{64,48},{80,64},{96,80},{112,96},{128,112},... | collective-permute-start | bytes 393224 | tf_op jit(solution)/shard_map/ppermute | solution.py:167
  24.2 34.3 %all-to-all-done.in_ref = f32[32,6,16,128]{3,2,1,0:T(8,128)S(1)} async-done(((f32[32,6,16,128]{3,2,1,0:T(8,128)}), f32[32,6,16,128]{3,2,1,0:T(8,128)S(1)}, u32[]{:S(2)}, u32[]{:S(2)}) %all-to-all-start) | async-done | bytes 1572896 | tf_op jit(solution)/shard_map/all_to_all | solution.py:164
  58.5 2.7 %turn.1 = f32[32,6,16,128]{3,2,1,0:T(8,128)} custom-call(s32[6]{0:T(128)S(1)} %copy-done.8, f32[32,6,16,128]{3,2,1,0:T(8,128)S(1)} %all-to-all-done.in_ref), custom_call_target="tpu_custom_call" | custom-call | tf_op jit(solution)/shard_map/turn/pallas_call | solution.py:198
  61.2 7.5 %all-to-all-start.1 = ((f32[32,6,16,128]{3,2,1,0:T(8,128)}), f32[32,6,16,128]{3,2,1,0:T(8,128)S(1)}, u32[]{:S(2)}, u32[]{:S(2)}) async-start(f32[32,6,16,128]{3,2,1,0:T(8,128)} %turn.1), calls=%async_computation.1 | async-start | bytes 3145728 | tf_op jit(solution)/shard_map/all_to_all | solution.py:206
  69.0 4.0 %select_reduce_fusion = (f32[6,128,128]{2,1,0:T(8,128)}, f32[6,128,128]{2,1,0:T(8,128)S(1)}) fusion(f32[6,31]{1,0:T(8,128)S(1)} %bitcast.30, pred[128,128,31]{1,0,2:T(8,128)(4,1)S(1)} %iota_compare_fusion, f32[6,31]{1,0:T(8,128)S(1)} %get-tuple-element.25), kind=kLoop, calls=%fused_computation | loop fusion | flops 11993088 | bytes 1295824 | tf_op jit(solution)/shard_map/reduce_sum | solution.py:31
  76.6 1.9 %collective-permute-start.2 = (f32[16,64,128]{2,1,0:T(8,128)S(1)}, f32[16,64,128]{2,1,0:T(8,128)S(1)}, u32[]{:S(2)}, u32[]{:S(2)}) collective-permute-start(f32[16,64,128]{2,1,0:T(8,128)S(1)} %constant_dynamic-update-slice_fusion.mid_ref), channel_id=1, source_target_pairs={{0,1},{1,2},{2,3},{3,4},{4,5},{5,6},{6,7},{7,8},{8,9},{9,10},{10,1... | collective-permute-start | bytes 1572872 | tf_op jit(solution)/shard_map/ppermute | solution.py:169
  78.6 3.8 %collective-permute-start.3 = (f32[16,64,128]{2,1,0:T(8,128)S(1)}, f32[16,64,128]{2,1,0:T(8,128)S(1)}, u32[]{:S(2)}, u32[]{:S(2)}) collective-permute-start(f32[16,64,128]{2,1,0:T(8,128)S(1)} %constant_dynamic-update-slice_fusion.mid_ref), channel_id=1, source_target_pairs={{1,0},{2,1},{3,2},{4,3},{5,4},{6,5},{7,6},{8,7},{9,8},{10,9},{11,1... | collective-permute-start | bytes 1572872 | tf_op jit(solution)/shard_map/ppermute | solution.py:170
  82.4 1.9 %copy.21 = f32[6,128,128]{1,2,0:T(8,128)} copy(f32[6,128,128]{2,1,0:T(8,128)} %get-tuple-element.11) | data formatting | bytes 786432 | tf_op jit(solution)/shard_map/reduce_sum | solution.py:31
  84.3 1.2 fusion.2.across_ref
  87.6 27.6 %collective-permute-done.2.low_ref = f32[16,64,128]{2,1,0:T(8,128)S(1)} collective-permute-done((f32[16,64,128]{2,1,0:T(8,128)S(1)}, f32[16,64,128]{2,1,0:T(8,128)S(1)}, u32[]{:S(2)}, u32[]{:S(2)}) %collective-permute-start.2) | collective-permute-done | bytes 524320 | tf_op jit(solution)/shard_map/ppermute | solution.py:169
  119.9 15.2 %forward.1.blurred_ref = f32[6,16,32,128]{3,2,1,0:T(8,128)S(1)} custom-call(f32[6,31]{1,0:T(8,128)S(1)} %get-tuple-element.28.taps_ref, f32[16,64,128]{2,1,0:T(8,128)S(1)} %copy-done.4, f32[16,64,128]{2,1,0:T(8,128)S(1)} %copy-done.2, f32[16,64,128]{2,1,0:T(8,128)S(1)} %copy-done.6, bf16[192,192]{1,0:T(8,128)(2,1)S(1)} %pad_maximum_fusion.lateral_ref, ...), custom_call_target="tpu_custom_call" | custom-call | tf_op jit(solution)/shard_map/forward/pallas_call | solution.py:188
  135.1 1.1 copy-done
  136.3 13.9 %back.1 = (f32[16,64,128]{2,1,0:T(8,128)S(1)}, f32[16,64,128]{2,1,0:T(8,128)S(1)}, f32[16,64,128]{2,1,0:T(8,128)S(1)}) custom-call(f32[6,31]{1,0:T(8,128)S(1)} %get-tuple-element.28.taps_ref, s32[6]{0:T(128)S(1)} %bitcast.27, f32[16,2,6,16,128]{4,3,2,1,0:T(8,128)S(1)} %bitcast.26, f32[6,16,32,128]{3,2,1,0:T(8,128)S(1)} %forward.1.blurred_ref, ...), custom_call_target="tpu_custom_call" | custom-call | tf_op jit(solution)/shard_map/back/pallas_call | solution.py:210
  150.2 2.1 %collective-permute-start.4 = (f32[16,64,128]{2,1,0:T(8,128)S(1)}, f32[16,64,128]{2,1,0:T(8,128)S(1)}, u32[]{:S(2)}, u32[]{:S(2)}) collective-permute-start(f32[16,64,128]{2,1,0:T(8,128)S(1)} %get-tuple-element.9), channel_id=1, source_target_pairs={{1,0},{2,1},{3,2},{4,3},{5,4},{6,5},{7,6},{8,7},{9,8},{10,9},{11,1... | collective-permute-start | bytes 1572872 | tf_op jit(solution)/shard_map/ppermute | solution.py:223
  152.2 2.4 %collective-permute-start.5 = (f32[16,64,128]{2,1,0:T(8,128)S(1)}, f32[16,64,128]{2,1,0:T(8,128)S(1)}, u32[]{:S(2)}, u32[]{:S(2)}) collective-permute-start(f32[16,64,128]{2,1,0:T(8,128)S(1)} %get-tuple-element.10), channel_id=1, source_target_pairs={{0,1},{1,2},{2,3},{3,4},{4,5},{5,6},{6,7},{7,8},{8,9},{9,10},{10,1... | collective-permute-start | bytes 1572872 | tf_op jit(solution)/shard_map/ppermute | solution.py:223
  154.7 4.2 %collective-permute-done.4 = f32[16,64,128]{2,1,0:T(8,128)S(1)} collective-permute-done((f32[16,64,128]{2,1,0:T(8,128)S(1)}, f32[16,64,128]{2,1,0:T(8,128)S(1)}, u32[]{:S(2)}, u32[]{:S(2)}) %collective-permute-start.4) | collective-permute-done | bytes 524320 | tf_op jit(solution)/shard_map/ppermute | solution.py:223
  158.9 8.6 %collective-permute-done.5 = f32[16,64,128]{2,1,0:T(8,128)S(1)} collective-permute-done((f32[16,64,128]{2,1,0:T(8,128)S(1)}, f32[16,64,128]{2,1,0:T(8,128)S(1)}, u32[]{:S(2)}, u32[]{:S(2)}) %collective-permute-start.5) | collective-permute-done | bytes 524320 | tf_op jit(solution)/shard_map/ppermute | solution.py:223
  167.6 6.7 %collective-permute-start.6 = (f32[16,16,128]{2,1,0:T(8,128)S(1)}, f32[16,16,128]{2,1,0:T(8,128)S(1)}, u32[]{:S(2)}, u32[]{:S(2)}) collective-permute-start(f32[16,16,128]{2,1,0:T(8,128)S(1)} %get-tuple-element.13), channel_id=1, source_target_pairs={{0,16},{16,32},{32,48},{48,64},{64,80},{80,96},{96,112},{112,128},... | collective-permute-start | bytes 393224 | tf_op jit(solution)/shard_map/ppermute | solution.py:225
  174.4 1.9 %collective-permute-start.7 = (f32[16,16,128]{2,1,0:T(8,128)S(1)}, f32[16,16,128]{2,1,0:T(8,128)S(1)}, u32[]{:S(2)}, u32[]{:S(2)}) collective-permute-start(f32[16,16,128]{2,1,0:T(8,128)S(1)} %get-tuple-element.14), channel_id=1, source_target_pairs={{16,0},{32,16},{48,32},{64,48},{80,64},{96,80},{112,96},{128,112},... | collective-permute-start | bytes 393224 | tf_op jit(solution)/shard_map/ppermute | solution.py:224
  177.0 9.7 %collective-permute-done.7 = f32[16,16,128]{2,1,0:T(8,128)S(1)} collective-permute-done((f32[16,16,128]{2,1,0:T(8,128)S(1)}, f32[16,16,128]{2,1,0:T(8,128)S(1)}, u32[]{:S(2)}, u32[]{:S(2)}) %collective-permute-start.7) | collective-permute-done | bytes 131104 | tf_op jit(solution)/shard_map/ppermute | solution.py:224
  186.7 1.4 fusion.8
  (54 shorter events, 12.5 us)
Async XLA Ops:
  2.8 12.9 %copy-start.9 = (f32[16,32,128]{2,1,0:T(8,128)S(1)}, f32[16,32,128]{2,1,0:T(8,128)}, u32[]{:S(2)}) copy-start(f32[16,32,128]{2,1,0:T(8,128)} %param.5) | copy-start | bytes 786436
  2.8 21.1 %copy-start.11 = (f32[6,3,31]{2,1,0:T(4,128)S(1)}, f32[6,3,31]{2,1,0:T(4,128)}, u32[]{:S(2)}) copy-start(f32[6,3,31]{2,1,0:T(4,128)} %param.7) | copy-start | bytes 6700
  2.8 55.7 %copy-start.8 = (s32[6]{0:T(128)S(1)}, s32[6]{0:T(128)}, u32[]{:S(2)}) copy-start(s32[6]{0:T(128)} %offsets_ref.1) | copy-start | bytes 76
  2.8 55.7 %all-to-all-start = ((f32[32,6,16,128]{3,2,1,0:T(8,128)}), f32[32,6,16,128]{3,2,1,0:T(8,128)S(1)}, u32[]{:S(2)}, u32[]{:S(2)}) async-start(f32[32,6,16,128]{3,2,1,0:T(8,128)} %bitcast.25), calls=%async_computation | async-start | bytes 3145728 | tf_op jit(solution)/shard_map/all_to_all | solution.py:164
  16.4 58.3 %collective-permute-start = (f32[16,16,128]{2,1,0:T(8,128)}, f32[16,16,128]{2,1,0:T(8,128)}, u32[]{:S(2)}, u32[]{:S(2)}) collective-permute-start(f32[16,16,128]{2,1,0:T(8,128)} %get-tuple-element.20), channel_id=1, source_target_pairs={{0,16},{16,32},{32,48},{48,64},{64,80},{80,96},{96,112},{112,128},... | collective-permute-start | bytes 393224 | tf_op jit(solution)/shard_map/ppermute | solution.py:166
  21.9 53.8 %collective-permute-start.1 = (f32[16,16,128]{2,1,0:T(8,128)}, f32[16,16,128]{2,1,0:T(8,128)}, u32[]{:S(2)}, u32[]{:S(2)}) collective-permute-start(f32[16,16,128]{2,1,0:T(8,128)} %get-tuple-element.19), channel_id=1, source_target_pairs={{16,0},{32,16},{48,32},{64,48},{80,64},{96,80},{112,96},{128,112},... | collective-permute-start | bytes 393224 | tf_op jit(solution)/shard_map/ppermute | solution.py:167
  61.2 73.9 %all-to-all-start.1 = ((f32[32,6,16,128]{3,2,1,0:T(8,128)}), f32[32,6,16,128]{3,2,1,0:T(8,128)S(1)}, u32[]{:S(2)}, u32[]{:S(2)}) async-start(f32[32,6,16,128]{3,2,1,0:T(8,128)} %turn.1), calls=%async_computation.1 | async-start | bytes 3145728 | tf_op jit(solution)/shard_map/all_to_all | solution.py:206
  76.6 11.0 %copy-start.1 = (f32[16,64,128]{2,1,0:T(8,128)}, f32[16,64,128]{2,1,0:T(8,128)S(1)}, u32[]{:S(2)}) copy-start(f32[16,64,128]{2,1,0:T(8,128)S(1)} %constant_dynamic-update-slice_fusion.mid_ref) | copy-start | bytes 1572868
  76.6 38.6 %collective-permute-start.2 = (f32[16,64,128]{2,1,0:T(8,128)S(1)}, f32[16,64,128]{2,1,0:T(8,128)S(1)}, u32[]{:S(2)}, u32[]{:S(2)}) collective-permute-start(f32[16,64,128]{2,1,0:T(8,128)S(1)} %constant_dynamic-update-slice_fusion.mid_ref), channel_id=1, source_target_pairs={{0,1},{1,2},{2,3},{3,4},{4,5},{5,6},{6,7},{7,8},{8,9},{9,10},{10,1... | collective-permute-start | bytes 1572872 | tf_op jit(solution)/shard_map/ppermute | solution.py:169
  78.6 37.4 %collective-permute-start.3 = (f32[16,64,128]{2,1,0:T(8,128)S(1)}, f32[16,64,128]{2,1,0:T(8,128)S(1)}, u32[]{:S(2)}, u32[]{:S(2)}) collective-permute-start(f32[16,64,128]{2,1,0:T(8,128)S(1)} %constant_dynamic-update-slice_fusion.mid_ref), channel_id=1, source_target_pairs={{1,0},{2,1},{3,2},{4,3},{5,4},{6,5},{7,6},{8,7},{9,8},{10,9},{11,1... | collective-permute-start | bytes 1572872 | tf_op jit(solution)/shard_map/ppermute | solution.py:170
  115.2 0.8 copy-start.3
  116.0 0.8 copy-start.5
  116.8 1.0 copy-start.2
  117.9 1.0 copy-start.4
  118.9 1.0 copy-start.6
  119.9 15.2 %copy-start.7 = (s32[6,1]{0,1:T(1,128)S(1)}, s32[6,1]{0,1:T(1,128)}, u32[]{:S(2)}) copy-start(s32[6,1]{0,1:T(1,128)} %param.9) | copy-start | bytes 76
  135.1 1.1 copy-start
  150.2 36.6 %copy-start.10 = (f32[16,32,128]{2,1,0:T(8,128)S(1)}, f32[16,32,128]{2,1,0:T(8,128)}, u32[]{:S(2)}) copy-start(f32[16,32,128]{2,1,0:T(8,128)} %param.5) | copy-start | bytes 786436
  150.2 8.7 %collective-permute-start.4 = (f32[16,64,128]{2,1,0:T(8,128)S(1)}, f32[16,64,128]{2,1,0:T(8,128)S(1)}, u32[]{:S(2)}, u32[]{:S(2)}) collective-permute-start(f32[16,64,128]{2,1,0:T(8,128)S(1)} %get-tuple-element.9), channel_id=1, source_target_pairs={{1,0},{2,1},{3,2},{4,3},{5,4},{6,5},{7,6},{8,7},{9,8},{10,9},{11,1... | collective-permute-start | bytes 1572872 | tf_op jit(solution)/shard_map/ppermute | solution.py:223
  152.2 15.3 %collective-permute-start.5 = (f32[16,64,128]{2,1,0:T(8,128)S(1)}, f32[16,64,128]{2,1,0:T(8,128)S(1)}, u32[]{:S(2)}, u32[]{:S(2)}) collective-permute-start(f32[16,64,128]{2,1,0:T(8,128)S(1)} %get-tuple-element.10), channel_id=1, source_target_pairs={{0,1},{1,2},{2,3},{3,4},{4,5},{5,6},{6,7},{7,8},{8,9},{9,10},{10,1... | collective-permute-start | bytes 1572872 | tf_op jit(solution)/shard_map/ppermute | solution.py:223
  167.6 9.4 %collective-permute-start.6 = (f32[16,16,128]{2,1,0:T(8,128)S(1)}, f32[16,16,128]{2,1,0:T(8,128)S(1)}, u32[]{:S(2)}, u32[]{:S(2)}) collective-permute-start(f32[16,16,128]{2,1,0:T(8,128)S(1)} %get-tuple-element.13), channel_id=1, source_target_pairs={{0,16},{16,32},{32,48},{48,64},{64,80},{80,96},{96,112},{112,128},... | collective-permute-start | bytes 393224 | tf_op jit(solution)/shard_map/ppermute | solution.py:225
  174.4 12.4 %collective-permute-start.7 = (f32[16,16,128]{2,1,0:T(8,128)S(1)}, f32[16,16,128]{2,1,0:T(8,128)S(1)}, u32[]{:S(2)}, u32[]{:S(2)}) collective-permute-start(f32[16,16,128]{2,1,0:T(8,128)S(1)} %get-tuple-element.14), channel_id=1, source_target_pairs={{16,0},{32,16},{48,32},{64,48},{80,64},{96,80},{112,96},{128,112},... | collective-permute-start | bytes 393224 | tf_op jit(solution)/shard_map/ppermute | solution.py:224

commit v2 on v1

--- a/solution.py
+++ b/solution.py
@@ -8,6 +8,8 @@
 from jax.sharding import PartitionSpec as P
 
 F32, BF16 = jnp.float32, jnp.bfloat16
+ROW = 8
+DIRECT = 3
 
 
 def split(values):
@@ -77,19 +79,24 @@
     lax.fori_loop(0, views, across, 0)
 
 
-def back_kernel(half, taps_ref, cover_ref, tiles_ref, blurred_ref, across_ref, lateral_ref, low_ref, mid_ref, high_ref, near_ref, wide_ref):
+def back_kernel(half, taps_ref, cover_ref, order_ref, *refs):
+    tiles_ref, *direct = refs[:-8]
+    blurred_ref, across_ref, lateral_ref, low_ref, mid_ref, high_ref, near_ref, wide_ref = refs[-8:]
     views, depth, rows, width = blurred_ref.shape
-    halves = tiles_ref.shape[1]
-
-    def across(view, carry):
-        owned = jnp.concatenate([tiles_ref[:, part, view] for part in range(halves)], axis=1)
+    halves, spread = tiles_ref.shape[1:3]
+
+    def across(slot, owned):
+        view = order_ref[slot]
         ratio = (cover_ref[view].astype(F32) * owned / blurred_ref[view]).reshape(depth * rows, width)
         upper, lower = split(ratio)
         both = dot(jnp.concatenate([upper, lower], axis=1), across_ref[view])
         near_ref[view] = (both[:, :width] + both[:, width:]).reshape(depth, rows, width)
-        return carry
-
-    lax.fori_loop(0, views, across, 0)
+
+    for slot in range(views):
+        if slot < spread:
+            across(slot, jnp.concatenate([tiles_ref[:, part, slot] for part in range(halves)], axis=1))
+        else:
+            across(slot, direct[slot - spread][...])
 
     taps = taps_ref.shape[1]
     start = depth - half
@@ -134,11 +141,39 @@
 
     def body(place, carry):
         for view in range(views):
-            source = lax.rem(place + ring - lax.rem(offsets_ref[view], ring), ring)
+            source = lax.rem(place + ring - offsets_ref[view], ring)
             out_ref[place, view] = in_ref[source, view]
         return carry
 
     lax.fori_loop(0, ring, body, 0)
+
+
+def pick_kernel(row, columns, offsets_ref, in_ref, order_ref, sorted_ref, pieces_ref, *direct):
+    views = in_ref.shape[0]
+    spread = pieces_ref.shape[1]
+    cost, moves = [], []
+    for view in range(views):
+        move = lax.rem(offsets_ref[view], row * columns)
+        across, along = lax.rem(move, row), move // row
+        near = 2 * jnp.minimum(along, columns - along)
+        far = 2 * jnp.minimum(along + 1, columns - 1 - along)
+        far = jnp.where(across > 0, far, 0)
+        cost.append(jnp.maximum(jnp.minimum(across, row - across), jnp.maximum(near, far)))
+        moves.append(move)
+    for view in range(views):
+        rank = jnp.int32(0)
+        for other in range(views):
+            if other != view:
+                ahead = cost[other] >= cost[view] if other < view else cost[other] > cost[view]
+                rank = rank + ahead.astype(jnp.int32)
+        order_ref[rank] = jnp.int32(view)
+        sorted_ref[rank] = moves[view]
+    for slot in range(views):
+        view = order_ref[slot]
+        if slot < spread:
+            pieces_ref[:, slot] = in_ref[view]
+        else:
+            direct[slot - spread][...] = in_ref[view].reshape(direct[slot - spread].shape)
 
 
 SMEM = pl.BlockSpec(memory_space=pltpu.SMEM)
@@ -160,8 +195,28 @@
 
     parts = ring // depth
     strip = rows // parts
-    pieces = view_data.reshape(views, ring, strip, width).transpose(1, 0, 2, 3)
+    tile = jax.ShapeDtypeStruct((depth, rows, width), F32)
+    order, moves, pieces, *straight = pl.pallas_call(
+        functools.partial(pick_kernel, ROW, ring // ROW),
+        out_shape=(
+            jax.ShapeDtypeStruct((views,), jnp.int32),
+            jax.ShapeDtypeStruct((views,), jnp.int32),
+            jax.ShapeDtypeStruct((ring, views - DIRECT, strip, width), F32),
+        )
+        + (tile,) * DIRECT,
+        in_specs=[SMEM, VMEM],
+        out_specs=(SMEM, SMEM, VMEM) + (VMEM,) * DIRECT,
+        compiler_params=PARAMS,
+        name="pick",
+    )(offsets, view_data.reshape(views, ring, strip, width))
     spread = lax.all_to_all(pieces, "brick", 0, 0, tiled=True)
+    hops = [functools.partial(lax.ppermute, axis_name="brick", perm=[(i, (i + by) % ring) for i in range(ring)]) for by in range(1, ring)]
+    hops = [lambda x: x] + hops
+
+    def send(slot, x):
+        return lax.switch(moves[views - DIRECT + slot], hops, x)
+
+    sent = [send(0, straight[0])]
 
     head = lax.ppermute(estimate[:, rows - reach :], "brick", right)
     tail = lax.ppermute(estimate[:, :reach], "brick", left)
@@ -184,6 +239,18 @@
         return jnp.concatenate([top, jnp.concatenate([high_part, jnp.zeros_like(low_part)], axis=2)], axis=1)
 
     across_on, across_back = across_of(kernels[:, 2]), across_of(flipped[:, 2])
+
+    turned = pl.pallas_call(
+        functools.partial(turn_kernel, ring),
+        out_shape=jax.ShapeDtypeStruct(spread.shape, F32),
+        in_specs=[SMEM, VMEM],
+        out_specs=VMEM,
+        compiler_params=PARAMS,
+        name="turn",
+    )(moves, spread)
+    turned, low, mid, high, *waiting = lax.optimization_barrier((turned, low, mid, high, *straight[1:]))
+    tiles = lax.all_to_all(turned, "brick", 0, 0, tiled=True)
+    sent += [send(slot + 1, x) for slot, x in enumerate(waiting)]
 
     blurred = pl.pallas_call(
         functools.partial(forward_kernel, half),
@@ -195,22 +262,13 @@
         name="forward",
     )(kernels[:, 0], low, mid, high, lateral_on, across_on)
 
-    turned = pl.pallas_call(
-        functools.partial(turn_kernel, ring),
-        out_shape=jax.ShapeDtypeStruct(spread.shape, F32),
-        in_specs=[SMEM, VMEM],
-        out_specs=VMEM,
-        compiler_params=PARAMS,
-        name="turn",
-    )(offsets, spread)
-    tiles = lax.all_to_all(turned, "brick", 0, 0, tiled=True)
-    tiles = tiles.reshape(depth, parts, views, strip, width)
+    tiles = tiles.reshape(depth, parts, views - DIRECT, strip, width)
 
     slab = jax.ShapeDtypeStruct((depth, wide, width), F32)
     below, own, above = pl.pallas_call(
         functools.partial(back_kernel, half),
         out_shape=(slab, slab, slab),
-        in_specs=[SMEM, SMEM, VMEM, VMEM, VMEM, VMEM],
+        in_specs=[SMEM, SMEM, SMEM] + [VMEM] * (4 + DIRECT),
         out_specs=(VMEM, VMEM, VMEM),
         scratch_shapes=[
             pltpu.VMEM((views, depth, rows, width), F32),
@@ -218,7 +276,7 @@
         ],
         compiler_params=PARAMS,
         name="back",
-    )(kernels[:, 0], coverage[:, 0], tiles, blurred, across_back, lateral_back)
+    )(kernels[:, 0], coverage[:, 0], order, tiles, *sent, blurred, across_back, lateral_back)
 
     total = own + lax.ppermute(below, "stack", down) + lax.ppermute(above, "stack", up)
     from_right = lax.ppermute(total[:, :reach], "brick", left)

time: 189 us -> 218 us (1.15)
  the two profiles are of different devices: /device:TPU:254 before, /device:TPU:258 now
where the time goes in v2:
time: 218 us; the launch traced here: 217 us
  waiting for transfers between devices  91.3 us (42%)
  starting transfers between devices  71.8 us (33%)
  Pallas kernels  32.4 us (15%)
  local copies, waits for them, and re-layouts  10.8 us (5%)
  other arithmetic  8.45 us (4%)
  between operations  2.31 us (1%)
    ppermute x3, waiting for transfers between devices, send(): return lax.switch(moves[views - DIRECT + slot], hops, x)  54.4 us
    pallas_call x1, Pallas kernels, shards(): pl.pallas_call(functools.partial(forward_kernel, half), out_shape=jax.Sha...  15.2 us
    pallas_call x1, Pallas kernels, shards(): pl.pallas_call(functools.partial(back_kernel, half), out_shape=(slab, sla...  13.6 us
    ppermute x1, waiting for transfers between devices, shards(): head = lax.ppermute(estimate[:, rows - reach:], 'brick', right)  13.4 us
    ppermute x1, starting transfers between devices, shards(): from_right = lax.ppermute(total[:, :reach], 'brick', left)  12.7 us
    ppermute x3, starting transfers between devices, send(): return lax.switch(moves[views - DIRECT + slot], hops, x)  12.7 us
    all_to_all x1, starting transfers between devices, shards(): spread = lax.all_to_all(pieces, 'brick', 0, 0, tiled=True)  12.7 us
    ppermute x1, waiting for transfers between devices, shards(): from_left = lax.ppermute(total[:, rows + reach:], 'brick', right)  10.4 us
  transfers between devices with their start and end apart: 13, of which 10 were waited for; matrix products, arithmetic and copies ran while one was open for 5% of the time, Pallas kernels for 8%

profile of v2, /device:TPU:258, one launch (start us, length us, event | category | flops | bytes accessed | tf_op | source)
XLA Modules:
  0.0 217.2 jit_solution(13719392713671678697)
XLA Ops:
  3.9 12.7 %all-to-all-start = ((f32[32,3,16,128]{3,2,1,0:T(8,128)}), f32[32,3,16,128]{3,2,1,0:T(8,128)S(1)}, u32[]{:S(2)}, u32[]{:S(2)}) async-start(f32[32,3,16,128]{3,2,1,0:T(8,128)} %get-tuple-element.217), calls=%async_computation | async-start | bytes 1572864 | tf_op jit(solution)/shard_map/all_to_all | solution.py:212
  16.6 3.4 %collective-permute-start.93 = (f32[16,16,128]{2,1,0:T(8,128)S(1)}, f32[16,16,128]{2,1,0:T(8,128)S(1)}, u32[]{:S(2)}, u32[]{:S(2)}) collective-permute-start(f32[16,16,128]{2,1,0:T(8,128)S(1)} %get-tuple-element.239), channel_id=1, source_target_pairs={{0,16},{16,32},{32,48},{48,64},{64,80},{80,96},{96,112},{112,128},... | collective-permute-start | bytes 393224 | tf_op jit(solution)/shard_map/ppermute | solution.py:221
  20.0 6.7 %collective-permute-start.94 = (f32[16,16,128]{2,1,0:T(8,128)S(1)}, f32[16,16,128]{2,1,0:T(8,128)S(1)}, u32[]{:S(2)}, u32[]{:S(2)}) collective-permute-start(f32[16,16,128]{2,1,0:T(8,128)S(1)} %get-tuple-element.238), channel_id=1, source_target_pairs={{16,0},{32,16},{48,32},{64,48},{80,64},{96,80},{112,96},{128,112},... | collective-permute-start | bytes 393224 | tf_op jit(solution)/shard_map/ppermute | solution.py:222
  27.8 13.4 %collective-permute-done.93 = f32[16,16,128]{2,1,0:T(8,128)S(1)} collective-permute-done((f32[16,16,128]{2,1,0:T(8,128)S(1)}, f32[16,16,128]{2,1,0:T(8,128)S(1)}, u32[]{:S(2)}, u32[]{:S(2)}) %collective-permute-start.93) | collective-permute-done | bytes 131104 | tf_op jit(solution)/shard_map/ppermute | solution.py:221
  41.3 1.9 collective-permute-start.95
  43.2 4.5 %collective-permute-start.96 = (f32[16,64,128]{2,1,0:T(8,128)S(1)}, f32[16,64,128]{2,1,0:T(8,128)S(1)}, u32[]{:S(2)}, u32[]{:S(2)}) collective-permute-start(f32[16,64,128]{2,1,0:T(8,128)S(1)} %constant_dynamic-update-slice_fusion.mid_ref), channel_id=1, source_target_pairs={{1,0},{2,1},{3,2},{4,3},{5,4},{6,5},{7,6},{8,7},{9,8},{10,9},{11,1... | collective-permute-start | bytes 1572872 | tf_op jit(solution)/shard_map/ppermute | solution.py:225
  47.8 4.0 %select_reduce_fusion = (f32[6,128,128]{2,1,0:T(8,128)}, f32[6,128,128]{2,1,0:T(8,128)S(1)}) fusion(f32[6,31]{1,0:T(8,128)S(1)} %bitcast.30, pred[128,128,31]{1,0,2:T(8,128)(4,1)S(1)} %iota_compare_fusion, f32[6,31]{1,0:T(8,128)S(1)} %get-tuple-element.244), kind=kLoop, calls=%fused_computation | loop fusion | flops 11993088 | bytes 1295824 | tf_op jit(solution)/shard_map/reduce_sum | solution.py:33
  56.4 8.7 %all-to-all-start.1 = ((f32[32,3,16,128]{3,2,1,0:T(8,128)}), f32[32,3,16,128]{3,2,1,0:T(8,128)S(1)}, u32[]{:S(2)}, u32[]{:S(2)}) async-start(f32[32,3,16,128]{3,2,1,0:T(8,128)} %turn.1), calls=%async_computation.1 | async-start | bytes 1572864 | tf_op jit(solution)/shard_map/all_to_all | solution.py:252
  69.2 28.7 %conditional.3 = (f32[16,32,128]{2,1,0:T(8,128)}) conditional(s32[]{:T(128)} %bitcast.4, f32[16,32,128]{2,1,0:T(8,128)} %get-tuple-element.221, f32[16,32,128]{2,1,0:T(8,128)} %get-tuple-element.221, f32[16,32,128]{2,1,0:T(8,128)} %get-tuple-element.221, f32[16,32,128]{2,1,0:T(8,128)} %get-tuple-element.221, ...), branch_computations={%region_1.0_spmd, %region_2.0_spmd, %region_3.0_spmd, %region_4.0_... | conditional | bytes 1572912 | solution.py:217
  69.2 5.5 %collective-permute-start.21 = (f32[16,32,128]{2,1,0:T(8,128)}, f32[16,32,128]{2,1,0:T(8,128)S(1)}, u32[]{:S(2)}, u32[]{:S(2)}) collective-permute-start(f32[16,32,128]{2,1,0:T(8,128)} %param.22), channel_id=1, source_target_pairs={{0,352},{16,368},{32,384},{48,400},{64,416},{80,432},{96,448},{112... | collective-permute-start | bytes 786440 | tf_op jit(solution)/shard_map/cond/branch_22_fun/ppermute | solution.py:217
  74.7 22.4 %collective-permute-done.21 = f32[16,32,128]{2,1,0:T(8,128)S(1)} collective-permute-done((f32[16,32,128]{2,1,0:T(8,128)}, f32[16,32,128]{2,1,0:T(8,128)S(1)}, u32[]{:S(2)}, u32[]{:S(2)}) %collective-permute-start.21) | collective-permute-done | bytes 262176 | tf_op jit(solution)/shard_map/cond/branch_22_fun/ppermute | solution.py:217
  99.2 28.9 %conditional.4 = (f32[16,32,128]{2,1,0:T(8,128)S(1)}) conditional(s32[]{:T(128)} %bitcast.5, f32[16,32,128]{2,1,0:T(8,128)S(1)} %get-tuple-element.222, f32[16,32,128]{2,1,0:T(8,128)S(1)} %get-tuple-element.222, f32[16,32,128]{2,1,0:T(8,128)S(1)} %get-tuple-element.222, ...), branch_computations={%region_33.34_spmd, %region_34.35_spmd, %region_35.36_spmd, %regio... | conditional | bytes 1572912 | solution.py:217
  99.2 5.3 %collective-permute-start.33 = (f32[16,32,128]{2,1,0:T(8,128)S(1)}, f32[16,32,128]{2,1,0:T(8,128)S(1)}, u32[]{:S(2)}, u32[]{:S(2)}) collective-permute-start(f32[16,32,128]{2,1,0:T(8,128)S(1)} %param.35), channel_id=1, source_target_pairs={{0,48},{16,64},{32,80},{48,96},{64,112},{80,128},{96,144},{112,160... | collective-permute-start | bytes 786440 | tf_op jit(solution)/shard_map/cond/branch_3_fun/ppermute | solution.py:217
  104.5 23.5 %collective-permute-done.33 = f32[16,32,128]{2,1,0:T(8,128)S(1)} collective-permute-done((f32[16,32,128]{2,1,0:T(8,128)S(1)}, f32[16,32,128]{2,1,0:T(8,128)S(1)}, u32[]{:S(2)}, u32[]{:S(2)}) %collective-permute-start.33) | collective-permute-done | bytes 262176 | tf_op jit(solution)/shard_map/cond/branch_3_fun/ppermute | solution.py:217
  128.8 11.1 %conditional.5 = (f32[16,32,128]{2,1,0:T(8,128)}) conditional(s32[]{:T(128)} %bitcast.6, f32[16,32,128]{2,1,0:T(8,128)} %get-tuple-element.223, f32[16,32,128]{2,1,0:T(8,128)} %get-tuple-element.223, f32[16,32,128]{2,1,0:T(8,128)} %get-tuple-element.223, f32[16,32,128]{2,1,0:T(8,128)} %get-tuple-element.223, ...), branch_computations={%region_65.66_spmd, %region_66.67_spmd, %region_67.68_spmd, %regio... | conditional | bytes 1572912 | solution.py:217
  130.7 8.4 %collective-permute-done.92 = f32[16,32,128]{2,1,0:T(8,128)S(1)} collective-permute-done((f32[16,32,128]{2,1,0:T(8,128)}, f32[16,32,128]{2,1,0:T(8,128)S(1)}, u32[]{:S(2)}, u32[]{:S(2)}) %collective-permute-start.92) | collective-permute-done | bytes 262176 | tf_op jit(solution)/shard_map/cond/branch_31_fun/ppermute | solution.py:217
  143.0 15.2 %forward.1.refs_4_ = f32[6,16,32,128]{3,2,1,0:T(8,128)S(1)} custom-call(f32[6,31]{1,0:T(8,128)S(1)} %get-tuple-element.247.taps_ref, f32[16,64,128]{2,1,0:T(8,128)S(1)} %copy-done.5, f32[16,64,128]{2,1,0:T(8,128)S(1)} %copy-done.3, f32[16,64,128]{2,1,0:T(8,128)S(1)} %copy-done.7, bf16[192,192]{1,0:T(8,128)(2,1)S(1)} %pad_maximum_fusion.lateral_ref, ...), custom_call_target="tpu_custom_call" | custom-call | tf_op jit(solution)/shard_map/forward/pallas_call | solution.py:255
  159.3 13.6 %back.1 = (f32[16,64,128]{2,1,0:T(8,128)S(1)}, f32[16,64,128]{2,1,0:T(8,128)S(1)}, f32[16,64,128]{2,1,0:T(8,128)S(1)}) custom-call(f32[6,31]{1,0:T(8,128)S(1)} %get-tuple-element.247.taps_ref, s32[6]{0:T(128)S(1)} %bitcast.28, s32[6]{0:T(128)S(1)} %get-tuple-element.215.order_ref, f32[16,2,3,16,128]{4,3,2,1,0:T(8,128)S(1)} %bitcast.26, ...), custom_call_target="tpu_custom_call" | custom-call | tf_op jit(solution)/shard_map/back/pallas_call | solution.py:268
  173.0 2.1 collective-permute-start.98
  175.0 4.5 %collective-permute-start.97 = (f32[16,64,128]{2,1,0:T(8,128)S(1)}, f32[16,64,128]{2,1,0:T(8,128)S(1)}, u32[]{:S(2)}, u32[]{:S(2)}) collective-permute-start(f32[16,64,128]{2,1,0:T(8,128)S(1)} %get-tuple-element.228), channel_id=1, source_target_pairs={{1,0},{2,1},{3,2},{4,3},{5,4},{6,5},{7,6},{8,7},{9,8},{10,9},{11,1... | collective-permute-start | bytes 1572872 | tf_op jit(solution)/shard_map/ppermute | solution.py:281
  179.6 8.5 %collective-permute-done.98 = f32[16,64,128]{2,1,0:T(8,128)S(1)} collective-permute-done((f32[16,64,128]{2,1,0:T(8,128)S(1)}, f32[16,64,128]{2,1,0:T(8,128)S(1)}, u32[]{:S(2)}, u32[]{:S(2)}) %collective-permute-start.98) | collective-permute-done | bytes 524320 | tf_op jit(solution)/shard_map/ppermute | solution.py:281
  188.6 12.7 %collective-permute-start.100 = (f32[16,16,128]{2,1,0:T(8,128)S(1)}, f32[16,16,128]{2,1,0:T(8,128)S(1)}, u32[]{:S(2)}, u32[]{:S(2)}) collective-permute-start(f32[16,16,128]{2,1,0:T(8,128)S(1)} %get-tuple-element.233), channel_id=1, source_target_pairs={{16,0},{32,16},{48,32},{64,48},{80,64},{96,80},{112,96},{128,112},... | collective-permute-start | bytes 393224 | tf_op jit(solution)/shard_map/ppermute | solution.py:282
  201.3 1.9 collective-permute-start.99
  205.4 10.4 %collective-permute-done.99 = f32[16,16,128]{2,1,0:T(8,128)S(1)} collective-permute-done((f32[16,16,128]{2,1,0:T(8,128)S(1)}, f32[16,16,128]{2,1,0:T(8,128)S(1)}, u32[]{:S(2)}, u32[]{:S(2)}) %collective-permute-start.99) | collective-permute-done | bytes 131104 | tf_op jit(solution)/shard_map/ppermute | solution.py:283
  (71 shorter events, 25.3 us)
Async XLA Ops:
  0.0 1.4 copy-start.1
  2.1 14.5 %copy-start.10 = (f32[16,32,128]{2,1,0:T(8,128)S(1)}, f32[16,32,128]{2,1,0:T(8,128)}, u32[]{:S(2)}) copy-start(f32[16,32,128]{2,1,0:T(8,128)} %param.101) | copy-start | bytes 786436
  2.1 24.6 %copy-start.13 = (f32[6,3,31]{2,1,0:T(4,128)S(1)}, f32[6,3,31]{2,1,0:T(4,128)}, u32[]{:S(2)}) copy-start(f32[6,3,31]{2,1,0:T(4,128)} %param.103) | copy-start | bytes 6700
  3.9 48.0 %all-to-all-start = ((f32[32,3,16,128]{3,2,1,0:T(8,128)}), f32[32,3,16,128]{3,2,1,0:T(8,128)S(1)}, u32[]{:S(2)}, u32[]{:S(2)}) async-start(f32[32,3,16,128]{3,2,1,0:T(8,128)} %get-tuple-element.217), calls=%async_computation | async-start | bytes 1572864 | tf_op jit(solution)/shard_map/all_to_all | solution.py:212
  16.6 24.7 %collective-permute-start.93 = (f32[16,16,128]{2,1,0:T(8,128)S(1)}, f32[16,16,128]{2,1,0:T(8,128)S(1)}, u32[]{:S(2)}, u32[]{:S(2)}) collective-permute-start(f32[16,16,128]{2,1,0:T(8,128)S(1)} %get-tuple-element.239), channel_id=1, source_target_pairs={{0,16},{16,32},{32,48},{48,64},{64,80},{80,96},{96,112},{112,128},... | collective-permute-start | bytes 393224 | tf_op jit(solution)/shard_map/ppermute | solution.py:221
  20.0 21.3 %collective-permute-start.94 = (f32[16,16,128]{2,1,0:T(8,128)S(1)}, f32[16,16,128]{2,1,0:T(8,128)S(1)}, u32[]{:S(2)}, u32[]{:S(2)}) collective-permute-start(f32[16,16,128]{2,1,0:T(8,128)S(1)} %get-tuple-element.238), channel_id=1, source_target_pairs={{16,0},{32,16},{48,32},{64,48},{80,64},{96,80},{112,96},{128,112},... | collective-permute-start | bytes 393224 | tf_op jit(solution)/shard_map/ppermute | solution.py:222
  41.3 15.1 %copy-start.2 = (f32[16,64,128]{2,1,0:T(8,128)}, f32[16,64,128]{2,1,0:T(8,128)S(1)}, u32[]{:S(2)}) copy-start(f32[16,64,128]{2,1,0:T(8,128)S(1)} %constant_dynamic-update-slice_fusion.mid_ref) | copy-start | bytes 1572868
  41.3 14.2 %collective-permute-start.95 = (f32[16,64,128]{2,1,0:T(8,128)S(1)}, f32[16,64,128]{2,1,0:T(8,128)S(1)}, u32[]{:S(2)}, u32[]{:S(2)}) collective-permute-start(f32[16,64,128]{2,1,0:T(8,128)S(1)} %constant_dynamic-update-slice_fusion.mid_ref), channel_id=1, source_target_pairs={{0,1},{1,2},{2,3},{3,4},{4,5},{5,6},{6,7},{7,8},{8,9},{9,10},{10,1... | collective-permute-start | bytes 1572872 | tf_op jit(solution)/shard_map/ppermute | solution.py:224
  43.2 13.1 %collective-permute-start.96 = (f32[16,64,128]{2,1,0:T(8,128)S(1)}, f32[16,64,128]{2,1,0:T(8,128)S(1)}, u32[]{:S(2)}, u32[]{:S(2)}) collective-permute-start(f32[16,64,128]{2,1,0:T(8,128)S(1)} %constant_dynamic-update-slice_fusion.mid_ref), channel_id=1, source_target_pairs={{1,0},{2,1},{3,2},{4,3},{5,4},{6,5},{7,6},{8,7},{9,8},{10,9},{11,1... | collective-permute-start | bytes 1572872 | tf_op jit(solution)/shard_map/ppermute | solution.py:225
  55.5 13.5 %copy-start.4 = (f32[16,64,128]{2,1,0:T(8,128)}, f32[16,64,128]{2,1,0:T(8,128)S(1)}, u32[]{:S(2)}) copy-start(f32[16,64,128]{2,1,0:T(8,128)S(1)} %collective-permute-done.95.low_ref) | copy-start | bytes 1572868
  56.4 12.7 %copy-start.6 = (f32[16,64,128]{2,1,0:T(8,128)}, f32[16,64,128]{2,1,0:T(8,128)S(1)}, u32[]{:S(2)}) copy-start(f32[16,64,128]{2,1,0:T(8,128)S(1)} %collective-permute-done.96.high_ref) | copy-start | bytes 1572868
  56.4 101.8 %all-to-all-start.1 = ((f32[32,3,16,128]{3,2,1,0:T(8,128)}), f32[32,3,16,128]{3,2,1,0:T(8,128)S(1)}, u32[]{:S(2)}, u32[]{:S(2)}) async-start(f32[32,3,16,128]{3,2,1,0:T(8,128)} %turn.1), calls=%async_computation.1 | async-start | bytes 1572864 | tf_op jit(solution)/shard_map/all_to_all | solution.py:252
  69.2 27.9 %collective-permute-start.21 = (f32[16,32,128]{2,1,0:T(8,128)}, f32[16,32,128]{2,1,0:T(8,128)S(1)}, u32[]{:S(2)}, u32[]{:S(2)}) collective-permute-start(f32[16,32,128]{2,1,0:T(8,128)} %param.22), channel_id=1, source_target_pairs={{0,352},{16,368},{32,384},{48,400},{64,416},{80,432},{96,448},{112... | collective-permute-start | bytes 786440 | tf_op jit(solution)/shard_map/cond/branch_22_fun/ppermute | solution.py:217
  99.2 28.8 %collective-permute-start.33 = (f32[16,32,128]{2,1,0:T(8,128)S(1)}, f32[16,32,128]{2,1,0:T(8,128)S(1)}, u32[]{:S(2)}, u32[]{:S(2)}) collective-permute-start(f32[16,32,128]{2,1,0:T(8,128)S(1)} %param.35), channel_id=1, source_target_pairs={{0,48},{16,64},{32,80},{48,96},{64,112},{80,128},{96,144},{112,160... | collective-permute-start | bytes 786440 | tf_op jit(solution)/shard_map/cond/branch_3_fun/ppermute | solution.py:217
  128.8 10.4 %collective-permute-start.92 = (f32[16,32,128]{2,1,0:T(8,128)}, f32[16,32,128]{2,1,0:T(8,128)S(1)}, u32[]{:S(2)}, u32[]{:S(2)}) collective-permute-start(f32[16,32,128]{2,1,0:T(8,128)} %param.95), channel_id=1, source_target_pairs={{0,496},{16,0},{32,16},{48,32},{64,48},{80,64},{96,80},{112,96},{1... | collective-permute-start | bytes 786440 | tf_op jit(solution)/shard_map/cond/branch_31_fun/ppermute | solution.py:217
  139.9 1.0 copy-start.3
  140.9 1.0 copy-start.5
  143.0 15.2 %copy-start.9 = (s32[6,1]{0,1:T(1,128)S(1)}, s32[6,1]{0,1:T(1,128)}, u32[]{:S(2)}) copy-start(s32[6,1]{0,1:T(1,128)} %param.105) | copy-start | bytes 76
  158.2 1.1 copy-start
  172.9 42.8 %copy-start.11 = (f32[16,32,128]{2,1,0:T(8,128)S(1)}, f32[16,32,128]{2,1,0:T(8,128)}, u32[]{:S(2)}) copy-start(f32[16,32,128]{2,1,0:T(8,128)} %param.101) | copy-start | bytes 786436
  173.0 15.1 %collective-permute-start.98 = (f32[16,64,128]{2,1,0:T(8,128)S(1)}, f32[16,64,128]{2,1,0:T(8,128)S(1)}, u32[]{:S(2)}, u32[]{:S(2)}) collective-permute-start(f32[16,64,128]{2,1,0:T(8,128)S(1)} %get-tuple-element.229), channel_id=1, source_target_pairs={{0,1},{1,2},{2,3},{3,4},{4,5},{5,6},{6,7},{7,8},{8,9},{9,10},{10,1... | collective-permute-start | bytes 1572872 | tf_op jit(solution)/shard_map/ppermute | solution.py:281
  175.0 13.4 %collective-permute-start.97 = (f32[16,64,128]{2,1,0:T(8,128)S(1)}, f32[16,64,128]{2,1,0:T(8,128)S(1)}, u32[]{:S(2)}, u32[]{:S(2)}) collective-permute-start(f32[16,64,128]{2,1,0:T(8,128)S(1)} %get-tuple-element.228), channel_id=1, source_target_pairs={{1,0},{2,1},{3,2},{4,3},{5,4},{6,5},{7,6},{8,7},{9,8},{10,9},{11,1... | collective-permute-start | bytes 1572872 | tf_op jit(solution)/shard_map/ppermute | solution.py:281
  188.6 16.8 %collective-permute-start.100 = (f32[16,16,128]{2,1,0:T(8,128)S(1)}, f32[16,16,128]{2,1,0:T(8,128)S(1)}, u32[]{:S(2)}, u32[]{:S(2)}) collective-permute-start(f32[16,16,128]{2,1,0:T(8,128)S(1)} %get-tuple-element.233), channel_id=1, source_target_pairs={{16,0},{32,16},{48,32},{64,48},{80,64},{96,80},{112,96},{128,112},... | collective-permute-start | bytes 393224 | tf_op jit(solution)/shard_map/ppermute | solution.py:282
  201.3 14.5 %collective-permute-start.99 = (f32[16,16,128]{2,1,0:T(8,128)S(1)}, f32[16,16,128]{2,1,0:T(8,128)S(1)}, u32[]{:S(2)}, u32[]{:S(2)}) collective-permute-start(f32[16,16,128]{2,1,0:T(8,128)S(1)} %get-tuple-element.232), channel_id=1, source_target_pairs={{0,16},{16,32},{32,48},{48,64},{64,80},{80,96},{96,112},{112,128},... | collective-permute-start | bytes 393224 | tf_op jit(solution)/shard_map/ppermute | solution.py:283
  (3 other events, 2.4 us)

commit v3 on v0

v3 whole, which is shorter than its diff:
```python
import functools

import jax
import jax.numpy as jnp
from jax import lax
from jax.experimental import pallas as pl
from jax.experimental.pallas import tpu as pltpu
from jax.sharding import PartitionSpec as P

F32, BF16 = jnp.float32, jnp.bfloat16
ROW = 8
DIRECT = 2


def split(values):
    high = values.astype(BF16)
    return high, (values - high.astype(F32)).astype(BF16)


def dot(left, right):
    return jnp.dot(left, right, preferred_element_type=F32)


def normal(taps_ref, view, dim):
    count = taps_ref.shape[2]
    total = taps_ref[view, dim, 0]
    for t in range(1, count):
        total = total + taps_ref[view, dim, t]
    scale = 1.0 / jnp.full((8, 128), total, F32)
    return [jnp.full((8, 128), taps_ref[view, dim, t], F32) * scale for t in range(count)]


def prepare_kernel(half, rows, wide, taps_ref, lateral_ref, lateral_back_ref, across_ref, across_back_ref):
    views, width = taps_ref.shape[0], 128

    def banded(taps, lane_of, count):
        lane = lax.broadcasted_iota(jnp.int32, (8, width), 1)
        first = jnp.zeros((8, width), F32)
        for t, tap in enumerate(taps):
            first = jnp.where(lane == lane_of(t) % width, tap, first)
        tall = jnp.concatenate([first] * (count // 8), axis=0)
        return pltpu.roll(tall, 0, 1, stride=1, stride_axis=0)

    row = lax.broadcasted_iota(jnp.int32, (width, width), 0)
    lane = lax.broadcasted_iota(jnp.int32, (width, width), 1)
    near = jnp.abs(row - lane) <= half
    back = [[jnp.zeros((wide, width), F32)] for _ in range(-(-views * rows // width))]
    for view in range(views):
        taps = normal(taps_ref, view, 2)
        for ref, lane_of in ((across_ref, lambda t: half - t), (across_back_ref, lambda t: t - half)):
            high, low = split(jnp.where(near, banded(taps, lane_of, width), 0.0))
            ref[view, :width, :width] = high
            ref[view, :width, width:] = low
            ref[view, width:, :width] = high
            ref[view, width:, width:] = jnp.zeros_like(low)
        taps = normal(taps_ref, view, 1)
        high, low = split(banded(taps, lambda t: t + 1, rows))
        high = high.astype(F32)
        at = slice(view * rows, (view + 1) * rows)
        lateral_ref[at, : 2 * wide] = (high + pltpu.roll(high, wide, 1)).astype(BF16)
        lateral_ref[at, 2 * wide :] = low[:, :wide]
        field = jnp.where(lane[:wide] < rows, banded(taps, lambda t: -1 - t, wide), 0.0)
        place = view * rows
        shift = place % width
        back[place // width].append(pltpu.roll(field, shift, 1) if shift else field)
    for block, fields in enumerate(back):
        total = fields[0]
        for field in fields[1:]:
            total = total + field
        high, low = split(total)
        size = min(width, views * rows - block * width)
        lateral_back_ref[:wide, block * width : block * width + size] = high[:, :size]
        lateral_back_ref[wide:, block * width : block * width + size] = low[:, :size]


def pair_of(ref, z):
    first_h, first_l = split(ref[z])
    second_h, second_l = split(ref[z + 1])
    return jnp.concatenate([first_h, second_h], axis=1), jnp.concatenate([first_l, second_l], axis=1)


def across_pass(field, matrix):
    depth, rows, width = field.shape
    upper, lower = split(field.reshape(depth * rows, width))
    both = dot(jnp.concatenate([upper, lower], axis=1), matrix)
    return (both[:, :width] + both[:, width:]).reshape(depth, rows, width)


def forward_kernel(half, taps_ref, low_ref, mid_ref, high_ref, lateral_ref, across_ref, out_ref, wide_ref):
    views, depth, rows, width = out_ref.shape
    for part, ref in enumerate((low_ref, mid_ref, high_ref)):

        def lateral(pair, carry, part=part, ref=ref):
            upper, lower = pair_of(ref, pair * 2)
            result = dot(lateral_ref[...], jnp.concatenate([upper, lower, upper], axis=0))
            wide_ref[part * depth + pair * 2] = result[:, :width]
            wide_ref[part * depth + pair * 2 + 1] = result[:, width:]
            return carry

        lax.fori_loop(0, depth // 2, lateral, 0, unroll=True)

    start, block = depth - half, 8

    def axial(view, carry):
        taps = normal(taps_ref, view, 0)
        for group in range(rows // 8):
            at = pl.ds(pl.multiple_of(view * rows + group * 8, 8), 8)
            for base in range(0, depth, block):
                totals = [None] * block
                for z in range(base, base + block + len(taps) - 1):
                    field = wide_ref[start + z, at, :]
                    for i in range(block):
                        t = z - base - i
                        if 0 <= t < len(taps):
                            term = taps[t] * field
                            totals[i] = term if totals[i] is None else totals[i] + term
                for i in range(block):
                    out_ref[view, base + i, group * 8 : group * 8 + 8, :] = totals[i]
        return carry

    lax.fori_loop(0, views, axial, 0)
    for view in range(views):
        out_ref[view] = across_pass(out_ref[view], across_ref[view])


def axial_back(half, taps_ref, near_ref, wide_ref, places):
    views, depth, rows, width = near_ref.shape
    start = depth - half

    def body(view, carry):
        taps = normal(taps_ref, view, 0)
        for group in range(rows // 8):
            into = pl.ds(pl.multiple_of(view * rows + group * 8, 8), 8)
            field = [near_ref[view, z, group * 8 : group * 8 + 8, :] for z in range(depth)]
            for slot, z in enumerate(places):
                total = None
                for source in range(depth):
                    t = z - start - source
                    if 0 <= t < len(taps):
                        term = taps[t] * field[source]
                        total = term if total is None else total + term
                wide_ref[slot, into, :] = jnp.zeros((8, width), F32) if total is None else total
        return carry

    lax.fori_loop(0, views, body, 0)


def lateral_back(lateral_ref, wide_ref, first, out_ref):
    depth, wide, width = out_ref.shape

    def body(pair, carry):
        upper, lower = pair_of(wide_ref, first + pair * 2)
        one = dot(lateral_ref[...], upper)
        result = one[:wide] + one[wide:] + dot(lateral_ref[:wide], lower)
        out_ref[pair * 2] = result[:, :width]
        out_ref[pair * 2 + 1] = result[:, width:]
        return carry

    lax.fori_loop(0, depth // 2, body, 0, unroll=True)


def outer_kernel(half, taps_ref, cover_ref, order_ref, *refs):
    tiles_ref, *direct = refs[:-7]
    blurred_ref, across_ref, lateral_ref, near_ref, low_ref, high_ref, wide_ref = refs[-7:]
    views, depth, rows, width = blurred_ref.shape
    halves, spread = tiles_ref.shape[1:3]
    for slot in range(views):
        view = order_ref[slot]
        if slot < spread:
            owned = jnp.concatenate([tiles_ref[:, part, slot] for part in range(halves)], axis=1)
        else:
            owned = direct[slot - spread][...]
        ratio = cover_ref[view].astype(F32) * owned / blurred_ref[view]
        near_ref[view] = across_pass(ratio, across_ref[view])
    axial_back(half, taps_ref, near_ref, wide_ref, list(range(depth)) + list(range(2 * depth, 3 * depth)))
    lateral_back(lateral_ref, wide_ref, 0, low_ref)
    lateral_back(lateral_ref, wide_ref, depth, high_ref)


def inner_kernel(half, taps_ref, near_ref, lateral_ref, mid_ref, wide_ref):
    depth = near_ref.shape[1]
    axial_back(half, taps_ref, near_ref, wide_ref, list(range(depth, 2 * depth)))
    lateral_back(lateral_ref, wide_ref, 0, mid_ref)


def turn_kernel(ring, offsets_ref, in_ref, out_ref):
    views = in_ref.shape[1]

    def body(place, carry):
        for view in range(views):
            source = lax.rem(place + ring - offsets_ref[view], ring)
            out_ref[place, view] = in_ref[source, view]
        return carry

    lax.fori_loop(0, ring, body, 0)


def pick_kernel(row, columns, offsets_ref, in_ref, order_ref, sorted_ref, pieces_ref, *direct):
    views = in_ref.shape[0]
    spread = pieces_ref.shape[1]
    cost, moves = [], []
    for view in range(views):
        move = lax.rem(offsets_ref[view], row * columns)
        across, along = lax.rem(move, row), move // row
        near = 2 * jnp.minimum(along, columns - along)
        far = 2 * jnp.minimum(along + 1, columns - 1 - along)
        far = jnp.where(across > 0, far, 0)
        cost.append(jnp.maximum(jnp.minimum(across, row - across), jnp.maximum(near, far)))
        moves.append(move)
    for view in range(views):
        rank = jnp.int32(0)
        for other in range(views):
            if other != view:
                ahead = cost[other] >= cost[view] if other < view else cost[other] > cost[view]
                rank = rank + ahead.astype(jnp.int32)
        order_ref[rank] = jnp.int32(view)
        sorted_ref[rank] = moves[view]
    for slot in range(views):
        view = order_ref[slot]
        if slot < spread:
            pieces_ref[:, slot] = in_ref[view]
        else:
            direct[slot - spread][...] = in_ref[view].reshape(direct[slot - spread].shape)


SMEM = pl.BlockSpec(memory_space=pltpu.SMEM)
VMEM = pl.BlockSpec(memory_space=pltpu.VMEM)
PARAMS = pltpu.CompilerParams(vmem_limit_bytes=48 << 20)


def call(kernel, name, outs, scalars, arrays, scratch=(), out_specs=None):
    return pl.pallas_call(
        kernel,
        out_shape=tuple(jax.ShapeDtypeStruct(shape, dtype) for shape, dtype in outs),
        in_specs=[SMEM] * len(scalars) + [VMEM] * len(arrays),
        out_specs=tuple(out_specs or [VMEM] * len(outs)),
        scratch_shapes=[pltpu.VMEM(shape, F32) for shape in scratch],
        compiler_params=PARAMS,
        name=name,
    )(*scalars, *arrays)


def shards(estimate, view_data, psf_taps, offsets, coverage):
    depth, rows, width = estimate.shape
    views = view_data.shape[0]
    half = (psf_taps.shape[2] - 1) // 2
    reach = half + 1
    wide = rows + 2 * reach
    ring = lax.axis_size("brick")
    stacks = lax.axis_size("stack")
    up = [(i, i + 1) for i in range(stacks - 1)]
    down = [(i + 1, i) for i in range(stacks - 1)]
    right = [(i, i + 1) for i in range(ring - 1)]
    left = [(i + 1, i) for i in range(ring - 1)]

    parts = ring // depth
    strip = rows // parts
    spread_views = views - DIRECT
    order, moves, pieces, *straight = call(
        functools.partial(pick_kernel, ROW, ring // ROW),
        "pick",
        [((views,), jnp.int32)] * 2 + [((ring, spread_views, strip, width), F32)] + [((depth, rows, width), F32)] * DIRECT,
        [offsets],
        [view_data.reshape(views, ring, strip, width)],
        out_specs=[SMEM, SMEM] + [VMEM] * (1 + DIRECT),
    )
    spread = lax.all_to_all(pieces, "brick", 0, 0, tiled=True)

    head = lax.ppermute(estimate[:, rows - reach :], "brick", right)
    tail = lax.ppermute(estimate[:, :reach], "brick", left)
    mid = jnp.concatenate([head, estimate, tail], axis=1)
    low = lax.ppermute(mid, "stack", up)
    high = lax.ppermute(mid, "stack", down)

    lateral_on, lateral_off, across_on, across_off = call(
        functools.partial(prepare_kernel, half, rows, wide),
        "prepare",
        [((views * rows, 3 * wide), BF16), ((2 * wide, views * rows), BF16)] + [((views, 2 * width, 2 * width), BF16)] * 2,
        [psf_taps],
        [],
    )

    hops = [lambda x: x]
    for by in range(1, ring):
        pairs = [(i, (i + by) % ring) for i in range(ring)]
        hops.append(functools.partial(lax.ppermute, axis_name="brick", perm=pairs))

    def send(slot, x):
        return lax.switch(moves[spread_views + slot], hops, x)

    first = send(0, straight[0])
    spread, first = lax.optimization_barrier((spread, first))
    (turned,) = call(functools.partial(turn_kernel, ring), "turn", [(spread.shape, F32)], [moves], [spread])
    turned, low, mid, high, *waiting = lax.optimization_barrier((turned, low, mid, high, *straight[1:]))
    tiles = lax.all_to_all(turned, "brick", 0, 0, tiled=True)
    tiles = tiles.reshape(depth, parts, spread_views, strip, width)
    sent = [first] + [send(slot + 1, x) for slot, x in enumerate(waiting)]

    (blurred,) = call(
        functools.partial(forward_kernel, half),
        "forward",
        [((views, depth, rows, width), F32)],
        [psf_taps],
        [low, mid, high, lateral_on, across_on],
        [(3 * depth, views * rows, width)],
    )

    slab = ((depth, wide, width), F32)
    near, below, above = call(
        functools.partial(outer_kernel, half),
        "outer",
        [((views, depth, rows, width), F32), slab, slab],
        [psf_taps, coverage[:, 0], order],
        [tiles, *sent, blurred, across_off, lateral_off],
        [(2 * depth, views * rows, width)],
    )
    from_above = lax.ppermute(below, "stack", down)
    from_below = lax.ppermute(above, "stack", up)
    (own,) = call(
        functools.partial(inner_kernel, half),
        "inner",
        [slab],
        [psf_taps],
        [near, lateral_off],
        [(depth, views * rows, width)],
    )

    total = own + from_above + from_below
    from_right = lax.ppermute(total[:, :reach], "brick", left)
    from_left = lax.ppermute(total[:, rows + reach :], "brick", right)
    summed = total[:, reach : rows + reach]
    gap = jnp.zeros((depth, rows - reach, width), F32)
    summed = summed + jnp.concatenate([from_left, gap], axis=1) + jnp.concatenate([gap, from_right], axis=1)
    cover_count = jnp.sum(coverage[:, 0].astype(F32))
    return estimate * summed / cover_count


def solution(mesh):
    placed = (
        P("stack", "brick", None),
        P(None, "stack", "brick", None),
        P(),
        P(),
        P(None, "brick"),
    )
    return jax.shard_map(
        shards, mesh=mesh, in_specs=placed, out_specs=P("stack", "brick", None), check_vma=False
    )
```

time: 594 us -> 173 us (0.29)
  the two profiles are of different devices: /device:TPU:58 before, /device:TPU:31 now
where the time goes in v3:
time: 173 us; the launch traced here: 172 us
  starting transfers between devices  73.4 us (42%)
  waiting for transfers between devices  65.9 us (38%)
  Pallas kernels  18.3 us (11%)
  local copies, waits for them, and re-layouts  11.1 us (6%)
  other arithmetic  2.01 us (1%)
    ppermute x2, waiting for transfers between devices, send(): return lax.switch(moves[spread_views + slot], hops, x)  32.1 us
    ppermute x1, waiting for transfers between devices, shards(): head = lax.ppermute(estimate[:, rows - reach:], 'brick', right)  20.4 us
    pallas_call x6, Pallas kernels, call(): pl.pallas_call(kernel, out_shape=tuple((jax.ShapeDtypeStruct(shape, dtype...  18.3 us
    all_to_all x1, starting transfers between devices, shards(): tiles = lax.all_to_all(turned, 'brick', 0, 0, tiled=True)  16 us
    all_to_all x1, starting transfers between devices, shards(): spread = lax.all_to_all(pieces, 'brick', 0, 0, tiled=True)  15.4 us
    ppermute x2, starting transfers between devices, send(): return lax.switch(moves[spread_views + slot], hops, x)  9.3 us
    ppermute x1, starting transfers between devices, shards(): from_left = lax.ppermute(total[:, rows + reach:], 'brick', right)  9.15 us
    unnamed x30, local copies, waits for them, and re-layouts  9.04 us
  transfers between devices with their start and end apart: 12, of which 8 were waited for; matrix products, arithmetic and copies ran while one was open for 2% of the time, Pallas kernels for 7%

profile of v3, /device:TPU:31, one launch (start us, length us, event | category | flops | bytes accessed | tf_op | source)
XLA Modules:
  0.0 172.4 jit_solution(14790670938374861985)
XLA Ops:
  2.1 1.9 %pick.1 = (s32[6]{0:T(128)S(1)}, s32[6]{0:T(128)S(1)}, f32[32,4,16,128]{3,2,1,0:T(8,128)}, f32[16,32,128]{2,1,0:T(8,128)}, f32[16,32,128]{2,1,0:T(8,128)}) custom-call(s32[6]{0:T(128)S(1)} %copy-done.10, f32[6,32,16,128]{3,2,1,0:T(8,128)S(1)} %bitcast.7), custom_call_target="tpu_custom_call" | custom-call | tf_op jit(solution)/shard_map/pick/pallas_call | solution.py:232
  4.0 15.4 %all-to-all-start = ((f32[32,4,16,128]{3,2,1,0:T(8,128)}), f32[32,4,16,128]{3,2,1,0:T(8,128)S(1)}, u32[]{:S(2)}, u32[]{:S(2)}) async-start(f32[32,4,16,128]{3,2,1,0:T(8,128)} %get-tuple-element.156), calls=%async_computation | async-start | bytes 2097152 | tf_op jit(solution)/shard_map/all_to_all | solution.py:267
  19.4 4.3 %collective-permute-start.62 = (f32[16,16,128]{2,1,0:T(8,128)S(1)}, f32[16,16,128]{2,1,0:T(8,128)S(1)}, u32[]{:S(2)}, u32[]{:S(2)}) collective-permute-start(f32[16,16,128]{2,1,0:T(8,128)S(1)} %get-tuple-element.176), channel_id=1, source_target_pairs={{0,16},{16,32},{32,48},{48,64},{64,80},{80,96},{96,112},{112,128},... | collective-permute-start | bytes 393224 | tf_op jit(solution)/shard_map/ppermute | solution.py:269
  23.7 1.9 %collective-permute-start.63 = (f32[16,16,128]{2,1,0:T(8,128)S(1)}, f32[16,16,128]{2,1,0:T(8,128)S(1)}, u32[]{:S(2)}, u32[]{:S(2)}) collective-permute-start(f32[16,16,128]{2,1,0:T(8,128)S(1)} %get-tuple-element.175), channel_id=1, source_target_pairs={{16,0},{32,16},{48,32},{64,48},{80,64},{96,80},{112,96},{128,112},... | collective-permute-start | bytes 393224 | tf_op jit(solution)/shard_map/ppermute | solution.py:270
  25.6 20.4 %collective-permute-done.62 = f32[16,16,128]{2,1,0:T(8,128)S(1)} collective-permute-done((f32[16,16,128]{2,1,0:T(8,128)S(1)}, f32[16,16,128]{2,1,0:T(8,128)S(1)}, u32[]{:S(2)}, u32[]{:S(2)}) %collective-permute-start.62) | collective-permute-done | bytes 131104 | tf_op jit(solution)/shard_map/ppermute | solution.py:269
  46.8 5.0 %collective-permute-start.64 = (f32[16,64,128]{2,1,0:T(8,128)S(1)}, f32[16,64,128]{2,1,0:T(8,128)S(1)}, u32[]{:S(2)}, u32[]{:S(2)}) collective-permute-start(f32[16,64,128]{2,1,0:T(8,128)S(1)} %constant_dynamic-update-slice_fusion.mid_ref), channel_id=1, source_target_pairs={{0,1},{1,2},{2,3},{3,4},{4,5},{5,6},{6,7},{7,8},{8,9},{9,10},{10,1... | collective-permute-start | bytes 1572872 | tf_op jit(solution)/shard_map/ppermute | solution.py:272
  51.8 1.9 %collective-permute-start.65 = (f32[16,64,128]{2,1,0:T(8,128)S(1)}, f32[16,64,128]{2,1,0:T(8,128)S(1)}, u32[]{:S(2)}, u32[]{:S(2)}) collective-permute-start(f32[16,64,128]{2,1,0:T(8,128)S(1)} %constant_dynamic-update-slice_fusion.mid_ref), channel_id=1, source_target_pairs={{1,0},{2,1},{3,2},{4,3},{5,4},{6,5},{7,6},{8,7},{9,8},{10,9},{11,1... | collective-permute-start | bytes 1572872 | tf_op jit(solution)/shard_map/ppermute | solution.py:273
  55.0 10.4 %conditional.2 = (f32[16,32,128]{2,1,0:T(8,128)}) conditional(s32[]{:T(128)} %bitcast.2, f32[16,32,128]{2,1,0:T(8,128)} %get-tuple-element.157, f32[16,32,128]{2,1,0:T(8,128)} %get-tuple-element.157, f32[16,32,128]{2,1,0:T(8,128)} %get-tuple-element.157, f32[16,32,128]{2,1,0:T(8,128)} %get-tuple-element.157, ...), branch_computations={%region_0.0_spmd, %region_1.0_spmd, %region_2.0_spmd, %region_3.0_... | conditional | bytes 1572912 | solution.py:289
  55.0 1.9 %collective-permute-start.30 = (f32[16,32,128]{2,1,0:T(8,128)}, f32[16,32,128]{2,1,0:T(8,128)S(1)}, u32[]{:S(2)}, u32[]{:S(2)}) collective-permute-start(f32[16,32,128]{2,1,0:T(8,128)} %param.31), channel_id=1, source_target_pairs={{0,496},{16,0},{32,16},{48,32},{64,48},{80,64},{96,80},{112,96},{1... | collective-permute-start | bytes 786440 | tf_op jit(solution)/shard_map/cond/branch_31_fun/ppermute | solution.py:289
  57.0 7.7 %collective-permute-done.30 = f32[16,32,128]{2,1,0:T(8,128)S(1)} collective-permute-done((f32[16,32,128]{2,1,0:T(8,128)}, f32[16,32,128]{2,1,0:T(8,128)S(1)}, u32[]{:S(2)}, u32[]{:S(2)}) %collective-permute-start.30) | collective-permute-done | bytes 262176 | tf_op jit(solution)/shard_map/cond/branch_31_fun/ppermute | solution.py:289
  65.4 2.0 %turn.1 = f32[32,4,16,128]{3,2,1,0:T(8,128)} custom-call(s32[6]{0:T(128)S(1)} %get-tuple-element.155.offsets_ref, f32[32,4,16,128]{3,2,1,0:T(8,128)S(1)} %all-to-all-done.in_ref), custom_call_target="tpu_custom_call" | custom-call | tf_op jit(solution)/shard_map/turn/pallas_call | solution.py:232
  68.2 16.0 %all-to-all-start.1 = ((f32[32,4,16,128]{3,2,1,0:T(8,128)}), f32[32,4,16,128]{3,2,1,0:T(8,128)S(1)}, u32[]{:S(2)}, u32[]{:S(2)}) async-start(f32[32,4,16,128]{3,2,1,0:T(8,128)} %turn.1), calls=%async_computation.1 | async-start | bytes 2097152 | tf_op jit(solution)/shard_map/all_to_all | solution.py:295
  88.3 32.5 %conditional.3 = (f32[16,32,128]{2,1,0:T(8,128)}) conditional(s32[]{:T(128)} %bitcast.4, f32[16,32,128]{2,1,0:T(8,128)} %get-tuple-element.162, f32[16,32,128]{2,1,0:T(8,128)} %get-tuple-element.162, f32[16,32,128]{2,1,0:T(8,128)} %get-tuple-element.162, f32[16,32,128]{2,1,0:T(8,128)} %get-tuple-element.162, ...), branch_computations={%region_32.0_spmd, %region_33.0_spmd, %region_34.0_spmd, %region_3... | conditional | bytes 1572912 | solution.py:289
  88.4 7.4 %collective-permute-start.55 = (f32[16,32,128]{2,1,0:T(8,128)}, f32[16,32,128]{2,1,0:T(8,128)S(1)}, u32[]{:S(2)}, u32[]{:S(2)}) collective-permute-start(f32[16,32,128]{2,1,0:T(8,128)} %param.57), channel_id=1, source_target_pairs={{0,400},{16,416},{32,432},{48,448},{64,464},{80,480},{96,496},{112... | collective-permute-start | bytes 786440 | tf_op jit(solution)/shard_map/cond/branch_25_fun/ppermute | solution.py:289
  95.8 24.3 %collective-permute-done.55 = f32[16,32,128]{2,1,0:T(8,128)S(1)} collective-permute-done((f32[16,32,128]{2,1,0:T(8,128)}, f32[16,32,128]{2,1,0:T(8,128)S(1)}, u32[]{:S(2)}, u32[]{:S(2)}) %collective-permute-start.55) | collective-permute-done | bytes 262176 | tf_op jit(solution)/shard_map/cond/branch_25_fun/ppermute | solution.py:289
  124.1 5.5 %forward.1.refs_3_ = f32[6,16,32,128]{3,2,1,0:T(8,128)S(1)} custom-call(f32[6,3,31]{2,1,0:T(4,128)S(1)} %copy-done.9, f32[16,64,128]{2,1,0:T(8,128)S(1)} %copy-done.6, f32[16,64,128]{2,1,0:T(8,128)S(1)} %constant_dynamic-update-slice_fusion.mid_ref, f32[16,64,128]{2,1,0:T(8,128)S(1)} %copy-done.8, bf16[192,192]{1,0:T(8,128)(2,1)S(1)} %get-tuple-element.166.lateral_ref, ...), custom_call_target="tpu_custom_call" | custom-call | tf_op jit(solution)/shard_map/forward/pallas_call | solution.py:232
  130.8 4.2 %outer.1 = (f32[6,16,32,128]{3,2,1,0:T(8,128)S(1)}, f32[16,64,128]{2,1,0:T(8,128)S(1)}, f32[16,64,128]{2,1,0:T(8,128)S(1)}) custom-call(f32[6,3,31]{2,1,0:T(4,128)S(1)} %copy-done.9, s32[6]{0:T(128)S(1)} %bitcast.8, s32[6]{0:T(128)S(1)} %get-tuple-element.154.order_ref, f32[16,2,4,16,128]{4,3,2,1,0:T(8,128)S(1)} %bitcast.6, ...), custom_call_target="tpu_custom_call" | custom-call | tf_op jit(solution)/shard_map/outer/pallas_call | solution.py:232
  134.9 6.6 %collective-permute-start.66 = (f32[16,64,128]{2,1,0:T(8,128)S(1)}, f32[16,64,128]{2,1,0:T(8,128)S(1)}, u32[]{:S(2)}, u32[]{:S(2)}) collective-permute-start(f32[16,64,128]{2,1,0:T(8,128)S(1)} %get-tuple-element.171), channel_id=1, source_target_pairs={{1,0},{2,1},{3,2},{4,3},{5,4},{6,5},{7,6},{8,7},{9,8},{10,9},{11,1... | collective-permute-start | bytes 1572872 | tf_op jit(solution)/shard_map/ppermute | solution.py:317
  141.5 1.9 %collective-permute-start.67 = (f32[16,64,128]{2,1,0:T(8,128)S(1)}, f32[16,64,128]{2,1,0:T(8,128)S(1)}, u32[]{:S(2)}, u32[]{:S(2)}) collective-permute-start(f32[16,64,128]{2,1,0:T(8,128)S(1)} %get-tuple-element.172), channel_id=1, source_target_pairs={{0,1},{1,2},{2,3},{3,4},{4,5},{5,6},{6,7},{7,8},{8,9},{9,10},{10,1... | collective-permute-start | bytes 1572872 | tf_op jit(solution)/shard_map/ppermute | solution.py:318
  143.4 3.1 %inner.1 = f32[16,64,128]{2,1,0:T(8,128)S(1)} custom-call(f32[6,3,31]{2,1,0:T(4,128)S(1)} %copy-done.9, f32[6,16,32,128]{3,2,1,0:T(8,128)S(1)} %get-tuple-element.170.near_ref, bf16[128,192]{1,0:T(8,128)(2,1)S(1)} %get-tuple-element.169.refs_5_.lateral_ref), custom_call_target="tpu_custom_call" | custom-call | tf_op jit(solution)/shard_map/inner/pallas_call | solution.py:232
  148.4 5.0 %collective-permute-done.67 = f32[16,64,128]{2,1,0:T(8,128)S(1)} collective-permute-done((f32[16,64,128]{2,1,0:T(8,128)S(1)}, f32[16,64,128]{2,1,0:T(8,128)S(1)}, u32[]{:S(2)}, u32[]{:S(2)}) %collective-permute-start.67) | collective-permute-done | bytes 524320 | tf_op jit(solution)/shard_map/ppermute | solution.py:318
  153.6 9.2 %collective-permute-start.68 = (f32[16,16,128]{2,1,0:T(8,128)S(1)}, f32[16,16,128]{2,1,0:T(8,128)S(1)}, u32[]{:S(2)}, u32[]{:S(2)}) collective-permute-start(f32[16,16,128]{2,1,0:T(8,128)S(1)} %get-tuple-element.173), channel_id=1, source_target_pairs={{0,16},{16,32},{32,48},{48,64},{64,80},{80,96},{96,112},{112,128},... | collective-permute-start | bytes 393224 | tf_op jit(solution)/shard_map/ppermute | solution.py:330
  162.7 1.9 %collective-permute-start.69 = (f32[16,16,128]{2,1,0:T(8,128)S(1)}, f32[16,16,128]{2,1,0:T(8,128)S(1)}, u32[]{:S(2)}, u32[]{:S(2)}) collective-permute-start(f32[16,16,128]{2,1,0:T(8,128)S(1)} %get-tuple-element.174), channel_id=1, source_target_pairs={{16,0},{32,16},{48,32},{64,48},{80,64},{96,80},{112,96},{128,112},... | collective-permute-start | bytes 393224 | tf_op jit(solution)/shard_map/ppermute | solution.py:329
  166.0 5.1 %collective-permute-done.69 = f32[16,16,128]{2,1,0:T(8,128)S(1)} collective-permute-done((f32[16,16,128]{2,1,0:T(8,128)S(1)}, f32[16,16,128]{2,1,0:T(8,128)S(1)}, u32[]{:S(2)}, u32[]{:S(2)}) %collective-permute-start.69) | collective-permute-done | bytes 131104 | tf_op jit(solution)/shard_map/ppermute | solution.py:329
  (47 shorter events, 18.1 us)
Async XLA Ops:
  0.0 1.4 copy-start
  2.1 17.3 %copy-start.12 = (f32[16,32,128]{2,1,0:T(8,128)S(1)}, f32[16,32,128]{2,1,0:T(8,128)}, u32[]{:S(2)}) copy-start(f32[16,32,128]{2,1,0:T(8,128)} %param.69) | copy-start | bytes 786436
  4.0 61.4 %all-to-all-start = ((f32[32,4,16,128]{3,2,1,0:T(8,128)}), f32[32,4,16,128]{3,2,1,0:T(8,128)S(1)}, u32[]{:S(2)}, u32[]{:S(2)}) async-start(f32[32,4,16,128]{3,2,1,0:T(8,128)} %get-tuple-element.156), calls=%async_computation | async-start | bytes 2097152 | tf_op jit(solution)/shard_map/all_to_all | solution.py:267
  19.4 26.6 %collective-permute-start.62 = (f32[16,16,128]{2,1,0:T(8,128)S(1)}, f32[16,16,128]{2,1,0:T(8,128)S(1)}, u32[]{:S(2)}, u32[]{:S(2)}) collective-permute-start(f32[16,16,128]{2,1,0:T(8,128)S(1)} %get-tuple-element.176), channel_id=1, source_target_pairs={{0,16},{16,32},{32,48},{48,64},{64,80},{80,96},{96,112},{112,128},... | collective-permute-start | bytes 393224 | tf_op jit(solution)/shard_map/ppermute | solution.py:269
  23.7 23.0 %collective-permute-start.63 = (f32[16,16,128]{2,1,0:T(8,128)S(1)}, f32[16,16,128]{2,1,0:T(8,128)S(1)}, u32[]{:S(2)}, u32[]{:S(2)}) collective-permute-start(f32[16,16,128]{2,1,0:T(8,128)S(1)} %get-tuple-element.175), channel_id=1, source_target_pairs={{16,0},{32,16},{48,32},{64,48},{80,64},{96,80},{112,96},{128,112},... | collective-permute-start | bytes 393224 | tf_op jit(solution)/shard_map/ppermute | solution.py:270
  46.8 20.6 %collective-permute-start.64 = (f32[16,64,128]{2,1,0:T(8,128)S(1)}, f32[16,64,128]{2,1,0:T(8,128)S(1)}, u32[]{:S(2)}, u32[]{:S(2)}) collective-permute-start(f32[16,64,128]{2,1,0:T(8,128)S(1)} %constant_dynamic-update-slice_fusion.mid_ref), channel_id=1, source_target_pairs={{0,1},{1,2},{2,3},{3,4},{4,5},{5,6},{6,7},{7,8},{8,9},{9,10},{10,1... | collective-permute-start | bytes 1572872 | tf_op jit(solution)/shard_map/ppermute | solution.py:272
  51.8 15.6 %collective-permute-start.65 = (f32[16,64,128]{2,1,0:T(8,128)S(1)}, f32[16,64,128]{2,1,0:T(8,128)S(1)}, u32[]{:S(2)}, u32[]{:S(2)}) collective-permute-start(f32[16,64,128]{2,1,0:T(8,128)S(1)} %constant_dynamic-update-slice_fusion.mid_ref), channel_id=1, source_target_pairs={{1,0},{2,1},{3,2},{4,3},{5,4},{6,5},{7,6},{8,7},{9,8},{10,9},{11,1... | collective-permute-start | bytes 1572872 | tf_op jit(solution)/shard_map/ppermute | solution.py:273
  55.0 9.7 %collective-permute-start.30 = (f32[16,32,128]{2,1,0:T(8,128)}, f32[16,32,128]{2,1,0:T(8,128)S(1)}, u32[]{:S(2)}, u32[]{:S(2)}) collective-permute-start(f32[16,32,128]{2,1,0:T(8,128)} %param.31), channel_id=1, source_target_pairs={{0,496},{16,0},{32,16},{48,32},{64,48},{80,64},{96,80},{112,96},{1... | collective-permute-start | bytes 786440 | tf_op jit(solution)/shard_map/cond/branch_31_fun/ppermute | solution.py:289
  67.4 16.9 %copy-start.9 = (f32[6,3,31]{2,1,0:T(4,128)S(1)}, f32[6,3,31]{2,1,0:T(4,128)}, u32[]{:S(2)}) copy-start(f32[6,3,31]{2,1,0:T(4,128)} %taps_ref.7) | copy-start | bytes 6700
  67.4 20.9 %copy-start.5 = (f32[16,64,128]{2,1,0:T(8,128)}, f32[16,64,128]{2,1,0:T(8,128)S(1)}, u32[]{:S(2)}) copy-start(f32[16,64,128]{2,1,0:T(8,128)S(1)} %collective-permute-done.64.low_ref) | copy-start | bytes 1572868
  68.2 61.4 %all-to-all-start.1 = ((f32[32,4,16,128]{3,2,1,0:T(8,128)}), f32[32,4,16,128]{3,2,1,0:T(8,128)S(1)}, u32[]{:S(2)}, u32[]{:S(2)}) async-start(f32[32,4,16,128]{3,2,1,0:T(8,128)} %turn.1), calls=%async_computation.1 | async-start | bytes 2097152 | tf_op jit(solution)/shard_map/all_to_all | solution.py:295
  85.9 0.9 copy-start.1
  86.8 0.9 copy-start.3
  88.4 31.7 %collective-permute-start.55 = (f32[16,32,128]{2,1,0:T(8,128)}, f32[16,32,128]{2,1,0:T(8,128)S(1)}, u32[]{:S(2)}, u32[]{:S(2)}) collective-permute-start(f32[16,32,128]{2,1,0:T(8,128)} %param.57), channel_id=1, source_target_pairs={{0,400},{16,416},{32,432},{48,448},{64,464},{80,480},{96,496},{112... | collective-permute-start | bytes 786440 | tf_op jit(solution)/shard_map/cond/branch_25_fun/ppermute | solution.py:289
  120.8 1.1 copy-start.2
  122.0 1.0 copy-start.6
  123.0 1.0 copy-start.8
  124.1 5.6 %copy-start.11 = (s32[6,1]{0,1:T(1,128)S(1)}, s32[6,1]{0,1:T(1,128)}, u32[]{:S(2)}) copy-start(s32[6,1]{0,1:T(1,128)} %param.73) | copy-start | bytes 76
  129.6 1.1 copy-start.4
  134.9 13.5 %collective-permute-start.66 = (f32[16,64,128]{2,1,0:T(8,128)S(1)}, f32[16,64,128]{2,1,0:T(8,128)S(1)}, u32[]{:S(2)}, u32[]{:S(2)}) collective-permute-start(f32[16,64,128]{2,1,0:T(8,128)S(1)} %get-tuple-element.171), channel_id=1, source_target_pairs={{1,0},{2,1},{3,2},{4,3},{5,4},{6,5},{7,6},{8,7},{9,8},{10,9},{11,1... | collective-permute-start | bytes 1572872 | tf_op jit(solution)/shard_map/ppermute | solution.py:317
  141.5 11.9 %collective-permute-start.67 = (f32[16,64,128]{2,1,0:T(8,128)S(1)}, f32[16,64,128]{2,1,0:T(8,128)S(1)}, u32[]{:S(2)}, u32[]{:S(2)}) collective-permute-start(f32[16,64,128]{2,1,0:T(8,128)S(1)} %get-tuple-element.172), channel_id=1, source_target_pairs={{0,1},{1,2},{2,3},{3,4},{4,5},{5,6},{6,7},{7,8},{8,9},{9,10},{10,1... | collective-permute-start | bytes 1572872 | tf_op jit(solution)/shard_map/ppermute | solution.py:318
  146.5 24.6 %copy-start.13 = (f32[16,32,128]{2,1,0:T(8,128)S(1)}, f32[16,32,128]{2,1,0:T(8,128)}, u32[]{:S(2)}) copy-start(f32[16,32,128]{2,1,0:T(8,128)} %param.69) | copy-start | bytes 786436
  153.6 12.4 %collective-permute-start.68 = (f32[16,16,128]{2,1,0:T(8,128)S(1)}, f32[16,16,128]{2,1,0:T(8,128)S(1)}, u32[]{:S(2)}, u32[]{:S(2)}) collective-permute-start(f32[16,16,128]{2,1,0:T(8,128)S(1)} %get-tuple-element.173), channel_id=1, source_target_pairs={{0,16},{16,32},{32,48},{48,64},{64,80},{80,96},{96,112},{112,128},... | collective-permute-start | bytes 393224 | tf_op jit(solution)/shard_map/ppermute | solution.py:330
  162.7 8.4 %collective-permute-start.69 = (f32[16,16,128]{2,1,0:T(8,128)S(1)}, f32[16,16,128]{2,1,0:T(8,128)S(1)}, u32[]{:S(2)}, u32[]{:S(2)}) collective-permute-start(f32[16,16,128]{2,1,0:T(8,128)S(1)} %get-tuple-element.174), channel_id=1, source_target_pairs={{16,0},{32,16},{48,32},{64,48},{80,64},{96,80},{112,96},{128,112},... | collective-permute-start | bytes 393224 | tf_op jit(solution)/shard_map/ppermute | solution.py:329
  (2 other events, 1.5 us)

commit v4 on v3

--- a/solution.py
+++ b/solution.py
@@ -8,8 +8,6 @@
 from jax.sharding import PartitionSpec as P
 
 F32, BF16 = jnp.float32, jnp.bfloat16
-ROW = 8
-DIRECT = 2
 
 
 def split(values):
@@ -159,17 +157,10 @@
     lax.fori_loop(0, depth // 2, body, 0, unroll=True)
 
 
-def outer_kernel(half, taps_ref, cover_ref, order_ref, *refs):
-    tiles_ref, *direct = refs[:-7]
-    blurred_ref, across_ref, lateral_ref, near_ref, low_ref, high_ref, wide_ref = refs[-7:]
+def outer_kernel(half, taps_ref, cover_ref, tiles_ref, blurred_ref, across_ref, lateral_ref, near_ref, low_ref, high_ref, wide_ref):
     views, depth, rows, width = blurred_ref.shape
-    halves, spread = tiles_ref.shape[1:3]
-    for slot in range(views):
-        view = order_ref[slot]
-        if slot < spread:
-            owned = jnp.concatenate([tiles_ref[:, part, slot] for part in range(halves)], axis=1)
-        else:
-            owned = direct[slot - spread][...]
+    for view in range(views):
+        owned = jnp.concatenate([tiles_ref[:, part, view] for part in range(tiles_ref.shape[1])], axis=1)
         ratio = cover_ref[view].astype(F32) * owned / blurred_ref[view]
         near_ref[view] = across_pass(ratio, across_ref[view])
     axial_back(half, taps_ref, near_ref, wide_ref, list(range(depth)) + list(range(2 * depth, 3 * depth)))
@@ -188,39 +179,19 @@
 
     def body(place, carry):
         for view in range(views):
-            source = lax.rem(place + ring - offsets_ref[view], ring)
+            source = lax.rem(place + ring - lax.rem(offsets_ref[view], ring), ring)
             out_ref[place, view] = in_ref[source, view]
         return carry
 
     lax.fori_loop(0, ring, body, 0)
 
 
-def pick_kernel(row, columns, offsets_ref, in_ref, order_ref, sorted_ref, pieces_ref, *direct):
-    views = in_ref.shape[0]
-    spread = pieces_ref.shape[1]
-    cost, moves = [], []
-    for view in range(views):
-        move = lax.rem(offsets_ref[view], row * columns)
-        across, along = lax.rem(move, row), move // row
-        near = 2 * jnp.minimum(along, columns - along)
-        far = 2 * jnp.minimum(along + 1, columns - 1 - along)
-        far = jnp.where(across > 0, far, 0)
-        cost.append(jnp.maximum(jnp.minimum(across, row - across), jnp.maximum(near, far)))
-        moves.append(move)
-    for view in range(views):
-        rank = jnp.int32(0)
-        for other in range(views):
-            if other != view:
-                ahead = cost[other] >= cost[view] if other < view else cost[other] > cost[view]
-                rank = rank + ahead.astype(jnp.int32)
-        order_ref[rank] = jnp.int32(view)
-        sorted_ref[rank] = moves[view]
-    for slot in range(views):
-        view = order_ref[slot]
-        if slot < spread:
-            pieces_ref[:, slot] = in_ref[view]
-        else:
-            direct[slot - spread][...] = in_ref[view].reshape(direct[slot - spread].shape)
+def pieces_kernel(in_ref, out_ref, sems):
+    copies = [pltpu.make_async_copy(in_ref.at[view], out_ref.at[:, view], sems.at[view]) for view in range(in_ref.shape[0])]
+    for copy in copies:
+        copy.start()
+    for copy in copies:
+        copy.wait()
 
 
 SMEM = pl.BlockSpec(memory_space=pltpu.SMEM)
@@ -255,19 +226,20 @@
 
     parts = ring // depth
     strip = rows // parts
-    spread_views = views - DIRECT
-    order, moves, pieces, *straight = call(
-        functools.partial(pick_kernel, ROW, ring // ROW),
-        "pick",
-        [((views,), jnp.int32)] * 2 + [((ring, spread_views, strip, width), F32)] + [((depth, rows, width), F32)] * DIRECT,
-        [offsets],
-        [view_data.reshape(views, ring, strip, width)],
-        out_specs=[SMEM, SMEM] + [VMEM] * (1 + DIRECT),
-    )
-    spread = lax.all_to_all(pieces, "brick", 0, 0, tiled=True)
+    pieces = pl.pallas_call(
+        pieces_kernel,
+        out_shape=jax.ShapeDtypeStruct((ring, views, strip, width), F32),
+        in_specs=[pl.BlockSpec(memory_space=pltpu.HBM)],
+        out_specs=VMEM,
+        scratch_shapes=[pltpu.SemaphoreType.DMA((views,))],
+        compiler_params=PARAMS,
+        name="pieces",
+    )(view_data.reshape(views, ring, strip, width))
 
     head = lax.ppermute(estimate[:, rows - reach :], "brick", right)
     tail = lax.ppermute(estimate[:, :reach], "brick", left)
+    pieces, head, tail = lax.optimization_barrier((pieces, head, tail))
+    spread = lax.all_to_all(pieces, "brick", 0, 0, tiled=True)
     mid = jnp.concatenate([head, estimate, tail], axis=1)
     low = lax.ppermute(mid, "stack", up)
     high = lax.ppermute(mid, "stack", down)
@@ -280,21 +252,10 @@
         [],
     )
 
-    hops = [lambda x: x]
-    for by in range(1, ring):
-        pairs = [(i, (i + by) % ring) for i in range(ring)]
-        hops.append(functools.partial(lax.ppermute, axis_name="brick", perm=pairs))
-
-    def send(slot, x):
-        return lax.switch(moves[spread_views + slot], hops, x)
-
-    first = send(0, straight[0])
-    spread, first = lax.optimization_barrier((spread, first))
-    (turned,) = call(functools.partial(turn_kernel, ring), "turn", [(spread.shape, F32)], [moves], [spread])
-    turned, low, mid, high, *waiting = lax.optimization_barrier((turned, low, mid, high, *straight[1:]))
+    spread, low, high = lax.optimization_barrier((spread, low, high))
+    (turned,) = call(functools.partial(turn_kernel, ring), "turn", [(spread.shape, F32)], [offsets], [spread])
     tiles = lax.all_to_all(turned, "brick", 0, 0, tiled=True)
-    tiles = tiles.reshape(depth, parts, spread_views, strip, width)
-    sent = [first] + [send(slot + 1, x) for slot, x in enumerate(waiting)]
+    tiles = tiles.reshape(depth, parts, views, strip, width)
 
     (blurred,) = call(
         functools.partial(forward_kernel, half),
@@ -310,8 +271,8 @@
         functools.partial(outer_kernel, half),
         "outer",
         [((views, depth, rows, width), F32), slab, slab],
-        [psf_taps, coverage[:, 0], order],
-        [tiles, *sent, blurred, across_off, lateral_off],
+        [psf_taps, coverage[:, 0]],
+        [tiles, blurred, across_off, lateral_off],
         [(2 * depth, views * rows, width)],
     )
     from_above = lax.ppermute(below, "stack", down)

time: 173 us -> 180 us (1.040)
  the two profiles are of different devices: /device:TPU:31 before, /device:TPU:58 now
where the time goes in v4:
time: 180 us
  waiting for transfers between devices  108 us (60%)
  starting transfers between devices  46.2 us (26%)
  Pallas kernels  18.7 us (10%)
  local copies, waits for them, and re-layouts  4.65 us (3%)
  other arithmetic  2.12 us (1%)
    all_to_all x1, waiting for transfers between devices, shards(): tiles = lax.all_to_all(turned, 'brick', 0, 0, tiled=True)  42.8 us
    ppermute x1, waiting for transfers between devices, shards(): low = lax.ppermute(mid, 'stack', up)  37.3 us
    pallas_call x5, Pallas kernels, call(): pl.pallas_call(kernel, out_shape=tuple((jax.ShapeDtypeStruct(shape, dtype...  17.4 us
    all_to_all x1, starting transfers between devices, shards(): spread = lax.all_to_all(pieces, 'brick', 0, 0, tiled=True)  13.1 us
    all_to_all x1, starting transfers between devices, shards(): tiles = lax.all_to_all(turned, 'brick', 0, 0, tiled=True)  8.73 us
    ppermute x1, waiting for transfers between devices, shards(): from_right = lax.ppermute(total[:, :reach], 'brick', left)  8.6 us
    ppermute x1, waiting for transfers between devices, shards(): tail = lax.ppermute(estimate[:, :reach], 'brick', left)  6.15 us
    ppermute x1, starting transfers between devices, shards(): head = lax.ppermute(estimate[:, rows - reach:], 'brick', right)  5.29 us
  transfers between devices with their start and end apart: 10, of which 8 were waited for; matrix products, arithmetic and copies ran while one was open for 0% of the time, Pallas kernels for 6%

profile of v4, /device:TPU:58, one launch (start us, length us, event | category | flops | bytes accessed | tf_op | source)
XLA Modules:
  0.0 179.5 jit_solution(11661274119384284076)
XLA Ops:
  1.0 5.3 %collective-permute-start = (f32[16,16,128]{2,1,0:T(8,128)S(1)}, f32[16,16,128]{2,1,0:T(8,128)S(1)}, u32[]{:S(2)}, u32[]{:S(2)}) collective-permute-start(f32[16,16,128]{2,1,0:T(8,128)S(1)} %get-tuple-element.34), channel_id=1, source_target_pairs={{0,16},{16,32},{32,48},{48,64},{64,80},{80,96},{96,112},{112,128},... | collective-permute-start | bytes 393224 | tf_op jit(solution)/shard_map/ppermute | solution.py:239
  6.3 1.9 %collective-permute-start.1 = (f32[16,16,128]{2,1,0:T(8,128)S(1)}, f32[16,16,128]{2,1,0:T(8,128)S(1)}, u32[]{:S(2)}, u32[]{:S(2)}) collective-permute-start(f32[16,16,128]{2,1,0:T(8,128)S(1)} %get-tuple-element.33), channel_id=1, source_target_pairs={{16,0},{32,16},{48,32},{64,48},{80,64},{96,80},{112,96},{128,112},... | collective-permute-start | bytes 393224 | tf_op jit(solution)/shard_map/ppermute | solution.py:240
  8.2 1.4 copy-done.1
  11.0 6.2 %collective-permute-done.1 = f32[16,16,128]{2,1,0:T(8,128)S(1)} collective-permute-done((f32[16,16,128]{2,1,0:T(8,128)S(1)}, f32[16,16,128]{2,1,0:T(8,128)S(1)}, u32[]{:S(2)}, u32[]{:S(2)}) %collective-permute-start.1) | collective-permute-done | bytes 131104 | tf_op jit(solution)/shard_map/ppermute | solution.py:240
  17.2 13.1 %all-to-all-start = ((f32[32,6,16,128]{3,2,1,0:T(8,128)}), f32[32,6,16,128]{3,2,1,0:T(8,128)S(1)}, u32[]{:S(2)}, u32[]{:S(2)}) async-start(f32[32,6,16,128]{3,2,1,0:T(8,128)} %pieces.1), calls=%async_computation | async-start | bytes 3145728 | tf_op jit(solution)/shard_map/all_to_all | solution.py:242
  30.4 1.9 %collective-permute-start.2 = (f32[16,64,128]{2,1,0:T(8,128)S(1)}, f32[16,64,128]{2,1,0:T(8,128)S(1)}, u32[]{:S(2)}, u32[]{:S(2)}) collective-permute-start(f32[16,64,128]{2,1,0:T(8,128)S(1)} %constant_dynamic-update-slice_fusion.mid_ref), channel_id=1, source_target_pairs={{0,1},{1,2},{2,3},{3,4},{4,5},{5,6},{6,7},{7,8},{8,9},{9,10},{10,1... | collective-permute-start | bytes 1572872 | tf_op jit(solution)/shard_map/ppermute | solution.py:244
  32.3 4.5 %collective-permute-start.3 = (f32[16,64,128]{2,1,0:T(8,128)S(1)}, f32[16,64,128]{2,1,0:T(8,128)S(1)}, u32[]{:S(2)}, u32[]{:S(2)}) collective-permute-start(f32[16,64,128]{2,1,0:T(8,128)S(1)} %constant_dynamic-update-slice_fusion.mid_ref), channel_id=1, source_target_pairs={{1,0},{2,1},{3,2},{4,3},{5,4},{6,5},{7,6},{8,7},{9,8},{10,9},{11,1... | collective-permute-start | bytes 1572872 | tf_op jit(solution)/shard_map/ppermute | solution.py:245
  36.8 37.3 %collective-permute-done.2.low_ref = f32[16,64,128]{2,1,0:T(8,128)S(1)} collective-permute-done((f32[16,64,128]{2,1,0:T(8,128)S(1)}, f32[16,64,128]{2,1,0:T(8,128)S(1)}, u32[]{:S(2)}, u32[]{:S(2)}) %collective-permute-start.2) | collective-permute-done | bytes 524320 | tf_op jit(solution)/shard_map/ppermute | solution.py:244
  74.1 2.9 %collective-permute-done.3.high_ref = f32[16,64,128]{2,1,0:T(8,128)S(1)} collective-permute-done((f32[16,64,128]{2,1,0:T(8,128)S(1)}, f32[16,64,128]{2,1,0:T(8,128)S(1)}, u32[]{:S(2)}, u32[]{:S(2)}) %collective-permute-start.3) | collective-permute-done | bytes 524320 | tf_op jit(solution)/shard_map/ppermute | solution.py:245
  77.1 2.7 %turn.1 = f32[32,6,16,128]{3,2,1,0:T(8,128)} custom-call(s32[6]{0:T(128)S(1)} %copy-done.6, f32[32,6,16,128]{3,2,1,0:T(8,128)S(1)} %all-to-all-done.in_ref), custom_call_target="tpu_custom_call" | custom-call | tf_op jit(solution)/shard_map/turn/pallas_call | solution.py:203
  79.7 8.7 %all-to-all-start.1 = ((f32[32,6,16,128]{3,2,1,0:T(8,128)}), f32[32,6,16,128]{3,2,1,0:T(8,128)S(1)}, u32[]{:S(2)}, u32[]{:S(2)}) async-start(f32[32,6,16,128]{3,2,1,0:T(8,128)} %turn.1), calls=%async_computation.1 | async-start | bytes 3145728 | tf_op jit(solution)/shard_map/all_to_all | solution.py:257
  88.5 1.6 prepare.1
  91.2 5.5 %forward.1.blurred_ref = f32[6,16,32,128]{3,2,1,0:T(8,128)S(1)} custom-call(f32[6,3,31]{2,1,0:T(4,128)S(1)} %copy-done.4, f32[16,64,128]{2,1,0:T(8,128)S(1)} %collective-permute-done.2.low_ref, f32[16,64,128]{2,1,0:T(8,128)S(1)} %constant_dynamic-update-slice_fusion.mid_ref, f32[16,64,128]{2,1,0:T(8,128)S(1)} %copy-done.3, ...), custom_call_target="tpu_custom_call" | custom-call | tf_op jit(solution)/shard_map/forward/pallas_call | solution.py:203
  97.9 42.8 %all-to-all-done.1 = f32[32,6,16,128]{3,2,1,0:T(8,128)S(1)} async-done(((f32[32,6,16,128]{3,2,1,0:T(8,128)}), f32[32,6,16,128]{3,2,1,0:T(8,128)S(1)}, u32[]{:S(2)}, u32[]{:S(2)}) %all-to-all-start.1) | async-done | bytes 1572896 | tf_op jit(solution)/shard_map/all_to_all | solution.py:257
  140.6 4.5 %outer.1 = (f32[6,16,32,128]{3,2,1,0:T(8,128)S(1)}, f32[16,64,128]{2,1,0:T(8,128)S(1)}, f32[16,64,128]{2,1,0:T(8,128)S(1)}) custom-call(f32[6,3,31]{2,1,0:T(4,128)S(1)} %copy-done.4, s32[6]{0:T(128)S(1)} %bitcast.6, f32[16,2,6,16,128]{4,3,2,1,0:T(8,128)S(1)} %bitcast.4, f32[6,16,32,128]{3,2,1,0:T(8,128)} %copy-done, ...), custom_call_target="tpu_custom_call" | custom-call | tf_op jit(solution)/shard_map/outer/pallas_call | solution.py:203
  145.1 1.9 %collective-permute-start.4 = (f32[16,64,128]{2,1,0:T(8,128)S(1)}, f32[16,64,128]{2,1,0:T(8,128)S(1)}, u32[]{:S(2)}, u32[]{:S(2)}) collective-permute-start(f32[16,64,128]{2,1,0:T(8,128)S(1)} %get-tuple-element.29), channel_id=1, source_target_pairs={{1,0},{2,1},{3,2},{4,3},{5,4},{6,5},{7,6},{8,7},{9,8},{10,9},{11,1... | collective-permute-start | bytes 1572872 | tf_op jit(solution)/shard_map/ppermute | solution.py:278
  147.0 2.4 %collective-permute-start.5 = (f32[16,64,128]{2,1,0:T(8,128)S(1)}, f32[16,64,128]{2,1,0:T(8,128)S(1)}, u32[]{:S(2)}, u32[]{:S(2)}) collective-permute-start(f32[16,64,128]{2,1,0:T(8,128)S(1)} %get-tuple-element.30), channel_id=1, source_target_pairs={{0,1},{1,2},{2,3},{3,4},{4,5},{5,6},{6,7},{7,8},{8,9},{9,10},{10,1... | collective-permute-start | bytes 1572872 | tf_op jit(solution)/shard_map/ppermute | solution.py:279
  149.4 3.1 %inner.1 = f32[16,64,128]{2,1,0:T(8,128)S(1)} custom-call(f32[6,3,31]{2,1,0:T(4,128)S(1)} %copy-done.4, f32[6,16,32,128]{3,2,1,0:T(8,128)S(1)} %get-tuple-element.28.near_ref, bf16[128,192]{1,0:T(8,128)(2,1)S(1)} %get-tuple-element.27.lateral_ref), custom_call_target="tpu_custom_call" | custom-call | tf_op jit(solution)/shard_map/inner/pallas_call | solution.py:203
  152.5 4.5 %collective-permute-done.4 = f32[16,64,128]{2,1,0:T(8,128)S(1)} collective-permute-done((f32[16,64,128]{2,1,0:T(8,128)S(1)}, f32[16,64,128]{2,1,0:T(8,128)S(1)}, u32[]{:S(2)}, u32[]{:S(2)}) %collective-permute-start.4) | collective-permute-done | bytes 524320 | tf_op jit(solution)/shard_map/ppermute | solution.py:278
  157.0 4.1 %collective-permute-done.5 = f32[16,64,128]{2,1,0:T(8,128)S(1)} collective-permute-done((f32[16,64,128]{2,1,0:T(8,128)S(1)}, f32[16,64,128]{2,1,0:T(8,128)S(1)}, u32[]{:S(2)}, u32[]{:S(2)}) %collective-permute-start.5) | collective-permute-done | bytes 524320 | tf_op jit(solution)/shard_map/ppermute | solution.py:279
  161.3 4.4 %collective-permute-start.6 = (f32[16,16,128]{2,1,0:T(8,128)S(1)}, f32[16,16,128]{2,1,0:T(8,128)S(1)}, u32[]{:S(2)}, u32[]{:S(2)}) collective-permute-start(f32[16,16,128]{2,1,0:T(8,128)S(1)} %get-tuple-element.31), channel_id=1, source_target_pairs={{0,16},{16,32},{32,48},{48,64},{64,80},{80,96},{96,112},{112,128},... | collective-permute-start | bytes 393224 | tf_op jit(solution)/shard_map/ppermute | solution.py:291
  165.7 1.9 %collective-permute-start.7 = (f32[16,16,128]{2,1,0:T(8,128)S(1)}, f32[16,16,128]{2,1,0:T(8,128)S(1)}, u32[]{:S(2)}, u32[]{:S(2)}) collective-permute-start(f32[16,16,128]{2,1,0:T(8,128)S(1)} %get-tuple-element.32), channel_id=1, source_target_pairs={{16,0},{32,16},{48,32},{64,48},{80,64},{96,80},{112,96},{128,112},... | collective-permute-start | bytes 393224 | tf_op jit(solution)/shard_map/ppermute | solution.py:290
  169.5 8.6 %collective-permute-done.7 = f32[16,16,128]{2,1,0:T(8,128)S(1)} collective-permute-done((f32[16,16,128]{2,1,0:T(8,128)S(1)}, f32[16,16,128]{2,1,0:T(8,128)S(1)}, u32[]{:S(2)}, u32[]{:S(2)}) %collective-permute-start.7) | collective-permute-done | bytes 131104 | tf_op jit(solution)/shard_map/ppermute | solution.py:290
  178.2 1.4 fusion.2
  (28 shorter events, 6.6 us)
Async XLA Ops:
  1.0 10.0 %collective-permute-start = (f32[16,16,128]{2,1,0:T(8,128)S(1)}, f32[16,16,128]{2,1,0:T(8,128)S(1)}, u32[]{:S(2)}, u32[]{:S(2)}) collective-permute-start(f32[16,16,128]{2,1,0:T(8,128)S(1)} %get-tuple-element.34), channel_id=1, source_target_pairs={{0,16},{16,32},{32,48},{48,64},{64,80},{80,96},{96,112},{112,128},... | collective-permute-start | bytes 393224 | tf_op jit(solution)/shard_map/ppermute | solution.py:239
  6.3 10.9 %collective-permute-start.1 = (f32[16,16,128]{2,1,0:T(8,128)S(1)}, f32[16,16,128]{2,1,0:T(8,128)S(1)}, u32[]{:S(2)}, u32[]{:S(2)}) collective-permute-start(f32[16,16,128]{2,1,0:T(8,128)S(1)} %get-tuple-element.33), channel_id=1, source_target_pairs={{16,0},{32,16},{48,32},{64,48},{80,64},{96,80},{112,96},{128,112},... | collective-permute-start | bytes 393224 | tf_op jit(solution)/shard_map/ppermute | solution.py:240
  8.2 1.4 copy-start.1
  11.0 19.3 %copy-start.7 = (f32[16,32,128]{2,1,0:T(8,128)S(1)}, f32[16,32,128]{2,1,0:T(8,128)}, u32[]{:S(2)}) copy-start(f32[16,32,128]{2,1,0:T(8,128)} %param.5) | copy-start | bytes 786436
  11.0 66.1 %copy-start.6 = (s32[6]{0:T(128)S(1)}, s32[6]{0:T(128)}, u32[]{:S(2)}) copy-start(s32[6]{0:T(128)} %offsets_ref.1) | copy-start | bytes 76
  17.2 59.9 %all-to-all-start = ((f32[32,6,16,128]{3,2,1,0:T(8,128)}), f32[32,6,16,128]{3,2,1,0:T(8,128)S(1)}, u32[]{:S(2)}, u32[]{:S(2)}) async-start(f32[32,6,16,128]{3,2,1,0:T(8,128)} %pieces.1), calls=%async_computation | async-start | bytes 3145728 | tf_op jit(solution)/shard_map/all_to_all | solution.py:242
  30.4 43.7 %collective-permute-start.2 = (f32[16,64,128]{2,1,0:T(8,128)S(1)}, f32[16,64,128]{2,1,0:T(8,128)S(1)}, u32[]{:S(2)}, u32[]{:S(2)}) collective-permute-start(f32[16,64,128]{2,1,0:T(8,128)S(1)} %constant_dynamic-update-slice_fusion.mid_ref), channel_id=1, source_target_pairs={{0,1},{1,2},{2,3},{3,4},{4,5},{5,6},{6,7},{7,8},{8,9},{9,10},{10,1... | collective-permute-start | bytes 1572872 | tf_op jit(solution)/shard_map/ppermute | solution.py:244
  32.3 44.8 %collective-permute-start.3 = (f32[16,64,128]{2,1,0:T(8,128)S(1)}, f32[16,64,128]{2,1,0:T(8,128)S(1)}, u32[]{:S(2)}, u32[]{:S(2)}) collective-permute-start(f32[16,64,128]{2,1,0:T(8,128)S(1)} %constant_dynamic-update-slice_fusion.mid_ref), channel_id=1, source_target_pairs={{1,0},{2,1},{3,2},{4,3},{5,4},{6,5},{7,6},{8,7},{9,8},{10,9},{11,1... | collective-permute-start | bytes 1572872 | tf_op jit(solution)/shard_map/ppermute | solution.py:245
  77.0 2.7 %copy-start.2 = (f32[16,64,128]{2,1,0:T(8,128)}, f32[16,64,128]{2,1,0:T(8,128)S(1)}, u32[]{:S(2)}) copy-start(f32[16,64,128]{2,1,0:T(8,128)S(1)} %collective-permute-done.3.high_ref) | copy-start | bytes 1572868
  79.7 8.7 %copy-start.4 = (f32[6,3,31]{2,1,0:T(4,128)S(1)}, f32[6,3,31]{2,1,0:T(4,128)}, u32[]{:S(2)}) copy-start(f32[6,3,31]{2,1,0:T(4,128)} %taps_ref.7) | copy-start | bytes 6700
  79.7 60.9 %all-to-all-start.1 = ((f32[32,6,16,128]{3,2,1,0:T(8,128)}), f32[32,6,16,128]{3,2,1,0:T(8,128)S(1)}, u32[]{:S(2)}, u32[]{:S(2)}) async-start(f32[32,6,16,128]{3,2,1,0:T(8,128)} %turn.1), calls=%async_computation.1 | async-start | bytes 3145728 | tf_op jit(solution)/shard_map/all_to_all | solution.py:257
  90.1 1.0 copy-start.3
  91.2 49.5 %copy-start.5 = (s32[6,1]{0,1:T(1,128)S(1)}, s32[6,1]{0,1:T(1,128)}, u32[]{:S(2)}) copy-start(s32[6,1]{0,1:T(1,128)} %param.9) | copy-start | bytes 76
  96.7 1.1 copy-start
  145.1 11.9 %collective-permute-start.4 = (f32[16,64,128]{2,1,0:T(8,128)S(1)}, f32[16,64,128]{2,1,0:T(8,128)S(1)}, u32[]{:S(2)}, u32[]{:S(2)}) collective-permute-start(f32[16,64,128]{2,1,0:T(8,128)S(1)} %get-tuple-element.29), channel_id=1, source_target_pairs={{1,0},{2,1},{3,2},{4,3},{5,4},{6,5},{7,6},{8,7},{9,8},{10,9},{11,1... | collective-permute-start | bytes 1572872 | tf_op jit(solution)/shard_map/ppermute | solution.py:278
  147.0 14.1 %collective-permute-start.5 = (f32[16,64,128]{2,1,0:T(8,128)S(1)}, f32[16,64,128]{2,1,0:T(8,128)S(1)}, u32[]{:S(2)}, u32[]{:S(2)}) collective-permute-start(f32[16,64,128]{2,1,0:T(8,128)S(1)} %get-tuple-element.30), channel_id=1, source_target_pairs={{0,1},{1,2},{2,3},{3,4},{4,5},{5,6},{6,7},{7,8},{8,9},{9,10},{10,1... | collective-permute-start | bytes 1572872 | tf_op jit(solution)/shard_map/ppermute | solution.py:279
  152.5 25.6 %copy-start.8 = (f32[16,32,128]{2,1,0:T(8,128)S(1)}, f32[16,32,128]{2,1,0:T(8,128)}, u32[]{:S(2)}) copy-start(f32[16,32,128]{2,1,0:T(8,128)} %param.5) | copy-start | bytes 786436
  161.3 8.3 %collective-permute-start.6 = (f32[16,16,128]{2,1,0:T(8,128)S(1)}, f32[16,16,128]{2,1,0:T(8,128)S(1)}, u32[]{:S(2)}, u32[]{:S(2)}) collective-permute-start(f32[16,16,128]{2,1,0:T(8,128)S(1)} %get-tuple-element.31), channel_id=1, source_target_pairs={{0,16},{16,32},{32,48},{48,64},{64,80},{80,96},{96,112},{112,128},... | collective-permute-start | bytes 393224 | tf_op jit(solution)/shard_map/ppermute | solution.py:291
  165.7 12.4 %collective-permute-start.7 = (f32[16,16,128]{2,1,0:T(8,128)S(1)}, f32[16,16,128]{2,1,0:T(8,128)S(1)}, u32[]{:S(2)}, u32[]{:S(2)}) collective-permute-start(f32[16,16,128]{2,1,0:T(8,128)S(1)} %get-tuple-element.32), channel_id=1, source_target_pairs={{16,0},{32,16},{48,32},{64,48},{80,64},{96,80},{112,96},{128,112},... | collective-permute-start | bytes 393224 | tf_op jit(solution)/shard_map/ppermute | solution.py:290

commit v5 on v3

--- a/solution.py
+++ b/solution.py
@@ -10,6 +10,7 @@
 F32, BF16 = jnp.float32, jnp.bfloat16
 ROW = 8
 DIRECT = 2
+EARLY = 1
 
 
 def split(values):
@@ -264,10 +265,10 @@
         [view_data.reshape(views, ring, strip, width)],
         out_specs=[SMEM, SMEM] + [VMEM] * (1 + DIRECT),
     )
-    spread = lax.all_to_all(pieces, "brick", 0, 0, tiled=True)
-
     head = lax.ppermute(estimate[:, rows - reach :], "brick", right)
     tail = lax.ppermute(estimate[:, :reach], "brick", left)
+    pieces, head, tail = lax.optimization_barrier((pieces, head, tail))
+    spread = lax.all_to_all(pieces, "brick", 0, 0, tiled=True)
     mid = jnp.concatenate([head, estimate, tail], axis=1)
     low = lax.ppermute(mid, "stack", up)
     high = lax.ppermute(mid, "stack", down)
@@ -288,13 +289,11 @@
     def send(slot, x):
         return lax.switch(moves[spread_views + slot], hops, x)
 
-    first = send(0, straight[0])
-    spread, first = lax.optimization_barrier((spread, first))
+    sent = [send(slot, straight[slot]) for slot in range(EARLY)]
+    spread, low, high, *sent = lax.optimization_barrier((spread, low, high, *sent))
     (turned,) = call(functools.partial(turn_kernel, ring), "turn", [(spread.shape, F32)], [moves], [spread])
-    turned, low, mid, high, *waiting = lax.optimization_barrier((turned, low, mid, high, *straight[1:]))
     tiles = lax.all_to_all(turned, "brick", 0, 0, tiled=True)
     tiles = tiles.reshape(depth, parts, spread_views, strip, width)
-    sent = [first] + [send(slot + 1, x) for slot, x in enumerate(waiting)]
 
     (blurred,) = call(
         functools.partial(forward_kernel, half),
@@ -304,6 +303,9 @@
         [low, mid, high, lateral_on, across_on],
         [(3 * depth, views * rows, width)],
     )
+
+    blurred, *waiting = lax.optimization_barrier((blurred, *straight[EARLY:]))
+    sent += [send(EARLY + slot, x) for slot, x in enumerate(waiting)]
 
     slab = ((depth, wide, width), F32)
     near, below, above = call(

time: 173 us -> 162 us (0.936)
  the two profiles are of different devices: /device:TPU:31 before, /device:TPU:62 now
where the time goes in v5:
time: 162 us; the launch traced here: 161 us
  waiting for transfers between devices  75.3 us (46%)
  starting transfers between devices  56.1 us (35%)
  Pallas kernels  18.2 us (11%)
  local copies, waits for them, and re-layouts  7.43 us (5%)
  other arithmetic  2.12 us (1%)
    ppermute x2, waiting for transfers between devices, send(): return lax.switch(moves[spread_views + slot], hops, x)  39.1 us
    pallas_call x6, Pallas kernels, call(): pl.pallas_call(kernel, out_shape=tuple((jax.ShapeDtypeStruct(shape, dtype...  18.2 us
    all_to_all x1, starting transfers between devices, shards(): spread = lax.all_to_all(pieces, 'brick', 0, 0, tiled=True)  13.1 us
    ppermute x1, waiting for transfers between devices, shards(): low = lax.ppermute(mid, 'stack', up)  11.7 us
    ppermute x2, starting transfers between devices, send(): return lax.switch(moves[spread_views + slot], hops, x)  8.67 us
    ppermute x1, waiting for transfers between devices, shards(): from_right = lax.ppermute(total[:, :reach], 'brick', left)  8.55 us
    all_to_all x1, starting transfers between devices, shards(): tiles = lax.all_to_all(turned, 'brick', 0, 0, tiled=True)  7.08 us
    ppermute x1, waiting for transfers between devices, shards(): from_above = lax.ppermute(below, 'stack', down)  5.59 us
  transfers between devices with their start and end apart: 12, of which 7 were waited for; matrix products, arithmetic and copies ran while one was open for 1% of the time, Pallas kernels for 7%

profile of v5, /device:TPU:62, one launch (start us, length us, event | category | flops | bytes accessed | tf_op | source)
XLA Modules:
  0.0 160.8 jit_solution(10766339640144313363)
XLA Ops:
  1.0 5.3 %collective-permute-start.62 = (f32[16,16,128]{2,1,0:T(8,128)S(1)}, f32[16,16,128]{2,1,0:T(8,128)S(1)}, u32[]{:S(2)}, u32[]{:S(2)}) collective-permute-start(f32[16,16,128]{2,1,0:T(8,128)S(1)} %get-tuple-element.180), channel_id=1, source_target_pairs={{0,16},{16,32},{32,48},{48,64},{64,80},{80,96},{96,112},{112,128},... | collective-permute-start | bytes 393224 | tf_op jit(solution)/shard_map/ppermute | solution.py:268
  6.3 1.9 %collective-permute-start.63 = (f32[16,16,128]{2,1,0:T(8,128)S(1)}, f32[16,16,128]{2,1,0:T(8,128)S(1)}, u32[]{:S(2)}, u32[]{:S(2)}) collective-permute-start(f32[16,16,128]{2,1,0:T(8,128)S(1)} %get-tuple-element.179), channel_id=1, source_target_pairs={{16,0},{32,16},{48,32},{64,48},{80,64},{96,80},{112,96},{128,112},... | collective-permute-start | bytes 393224 | tf_op jit(solution)/shard_map/ppermute | solution.py:269
  12.1 5.0 %collective-permute-done.63 = f32[16,16,128]{2,1,0:T(8,128)S(1)} collective-permute-done((f32[16,16,128]{2,1,0:T(8,128)S(1)}, f32[16,16,128]{2,1,0:T(8,128)S(1)}, u32[]{:S(2)}, u32[]{:S(2)}) %collective-permute-start.63) | collective-permute-done | bytes 131104 | tf_op jit(solution)/shard_map/ppermute | solution.py:269
  17.2 13.1 %all-to-all-start = ((f32[32,4,16,128]{3,2,1,0:T(8,128)}), f32[32,4,16,128]{3,2,1,0:T(8,128)S(1)}, u32[]{:S(2)}, u32[]{:S(2)}) async-start(f32[32,4,16,128]{3,2,1,0:T(8,128)} %get-tuple-element.159), calls=%async_computation | async-start | bytes 2097152 | tf_op jit(solution)/shard_map/all_to_all | solution.py:271
  30.4 1.9 %collective-permute-start.64 = (f32[16,64,128]{2,1,0:T(8,128)S(1)}, f32[16,64,128]{2,1,0:T(8,128)S(1)}, u32[]{:S(2)}, u32[]{:S(2)}) collective-permute-start(f32[16,64,128]{2,1,0:T(8,128)S(1)} %constant_dynamic-update-slice_fusion.mid_ref), channel_id=1, source_target_pairs={{0,1},{1,2},{2,3},{3,4},{4,5},{5,6},{6,7},{7,8},{8,9},{9,10},{10,1... | collective-permute-start | bytes 1572872 | tf_op jit(solution)/shard_map/ppermute | solution.py:273
  32.3 4.5 %collective-permute-start.65 = (f32[16,64,128]{2,1,0:T(8,128)S(1)}, f32[16,64,128]{2,1,0:T(8,128)S(1)}, u32[]{:S(2)}, u32[]{:S(2)}) collective-permute-start(f32[16,64,128]{2,1,0:T(8,128)S(1)} %constant_dynamic-update-slice_fusion.mid_ref), channel_id=1, source_target_pairs={{1,0},{2,1},{3,2},{4,3},{5,4},{6,5},{7,6},{8,7},{9,8},{10,9},{11,1... | collective-permute-start | bytes 1572872 | tf_op jit(solution)/shard_map/ppermute | solution.py:274
  38.1 27.5 %conditional.2 = (f32[16,32,128]{2,1,0:T(8,128)S(1)}) conditional(s32[]{:T(128)} %bitcast.2, f32[16,32,128]{2,1,0:T(8,128)S(1)} %get-tuple-element.162, f32[16,32,128]{2,1,0:T(8,128)S(1)} %get-tuple-element.162, f32[16,32,128]{2,1,0:T(8,128)S(1)} %get-tuple-element.162, ...), branch_computations={%region_0.0_spmd, %region_1.0_spmd, %region_2.0_spmd, %region_3.0_... | conditional | bytes 1572912 | solution.py:290
  38.1 3.4 %collective-permute-start.30 = (f32[16,32,128]{2,1,0:T(8,128)S(1)}, f32[16,32,128]{2,1,0:T(8,128)S(1)}, u32[]{:S(2)}, u32[]{:S(2)}) collective-permute-start(f32[16,32,128]{2,1,0:T(8,128)S(1)} %param.31), channel_id=1, source_target_pairs={{0,496},{16,0},{32,16},{48,32},{64,48},{80,64},{96,80},{112,96},{1... | collective-permute-start | bytes 786440 | tf_op jit(solution)/shard_map/cond/branch_31_fun/ppermute | solution.py:290
  41.5 24.0 %collective-permute-done.30 = f32[16,32,128]{2,1,0:T(8,128)S(1)} collective-permute-done((f32[16,32,128]{2,1,0:T(8,128)S(1)}, f32[16,32,128]{2,1,0:T(8,128)S(1)}, u32[]{:S(2)}, u32[]{:S(2)}) %collective-permute-start.30) | collective-permute-done | bytes 262176 | tf_op jit(solution)/shard_map/cond/branch_31_fun/ppermute | solution.py:290
  65.5 11.7 %collective-permute-done.64.low_ref = f32[16,64,128]{2,1,0:T(8,128)S(1)} collective-permute-done((f32[16,64,128]{2,1,0:T(8,128)S(1)}, f32[16,64,128]{2,1,0:T(8,128)S(1)}, u32[]{:S(2)}, u32[]{:S(2)}) %collective-permute-start.64) | collective-permute-done | bytes 524320 | tf_op jit(solution)/shard_map/ppermute | solution.py:273
  77.3 2.0 %turn.1 = f32[32,4,16,128]{3,2,1,0:T(8,128)} custom-call(s32[6]{0:T(128)S(1)} %get-tuple-element.157.offsets_ref, f32[32,4,16,128]{3,2,1,0:T(8,128)S(1)} %all-to-all-done.in_ref), custom_call_target="tpu_custom_call" | custom-call | tf_op jit(solution)/shard_map/turn/pallas_call | solution.py:233
  79.3 7.1 %all-to-all-start.1 = ((f32[32,4,16,128]{3,2,1,0:T(8,128)}), f32[32,4,16,128]{3,2,1,0:T(8,128)S(1)}, u32[]{:S(2)}, u32[]{:S(2)}) async-start(f32[32,4,16,128]{3,2,1,0:T(8,128)} %turn.1), calls=%async_computation.1 | async-start | bytes 2097152 | tf_op jit(solution)/shard_map/all_to_all | solution.py:295
  91.6 5.5 %forward.1.refs_3_ = f32[6,16,32,128]{3,2,1,0:T(8,128)S(1)} custom-call(f32[6,3,31]{2,1,0:T(4,128)S(1)} %copy-done.7, f32[16,64,128]{2,1,0:T(8,128)S(1)} %copy-done.4, f32[16,64,128]{2,1,0:T(8,128)S(1)} %constant_dynamic-update-slice_fusion.mid_ref, f32[16,64,128]{2,1,0:T(8,128)S(1)} %copy-done.6, bf16[192,192]{1,0:T(8,128)(2,1)S(1)} %get-tuple-element.167.lateral_ref, ...), custom_call_target="tpu_custom_call" | custom-call | tf_op jit(solution)/shard_map/forward/pallas_call | solution.py:233
  97.2 21.2 %conditional.3 = (f32[16,32,128]{2,1,0:T(8,128)}) conditional(s32[]{:T(128)} %bitcast.4, f32[16,32,128]{2,1,0:T(8,128)} %get-tuple-element.170, f32[16,32,128]{2,1,0:T(8,128)} %get-tuple-element.170, f32[16,32,128]{2,1,0:T(8,128)} %get-tuple-element.170, f32[16,32,128]{2,1,0:T(8,128)} %get-tuple-element.170, ...), branch_computations={%region_32.0_spmd, %region_33.0_spmd, %region_34.0_spmd, %region_3... | conditional | bytes 1572912 | solution.py:290
  97.3 5.3 %collective-permute-start.32 = (f32[16,32,128]{2,1,0:T(8,128)}, f32[16,32,128]{2,1,0:T(8,128)S(1)}, u32[]{:S(2)}, u32[]{:S(2)}) collective-permute-start(f32[16,32,128]{2,1,0:T(8,128)} %param.34), channel_id=1, source_target_pairs={{0,32},{16,48},{32,64},{48,80},{64,96},{80,112},{96,128},{112,144}... | collective-permute-start | bytes 786440 | tf_op jit(solution)/shard_map/cond/branch_2_fun/ppermute | solution.py:290
  102.6 15.1 %collective-permute-done.32 = f32[16,32,128]{2,1,0:T(8,128)S(1)} collective-permute-done((f32[16,32,128]{2,1,0:T(8,128)}, f32[16,32,128]{2,1,0:T(8,128)S(1)}, u32[]{:S(2)}, u32[]{:S(2)}) %collective-permute-start.32) | collective-permute-done | bytes 262176 | tf_op jit(solution)/shard_map/cond/branch_2_fun/ppermute | solution.py:290
  118.4 4.2 %outer.1 = (f32[6,16,32,128]{3,2,1,0:T(8,128)S(1)}, f32[16,64,128]{2,1,0:T(8,128)S(1)}, f32[16,64,128]{2,1,0:T(8,128)S(1)}) custom-call(f32[6,3,31]{2,1,0:T(4,128)S(1)} %copy-done.7, s32[6]{0:T(128)S(1)} %bitcast.8, s32[6]{0:T(128)S(1)} %get-tuple-element.156.order_ref, f32[16,2,4,16,128]{4,3,2,1,0:T(8,128)S(1)} %bitcast.6, f32[16,32,128]{2,1,0:T(8,128)} %copy-done.12, ...), custom_call_target="tpu_custom_call" | custom-call | tf_op jit(solution)/shard_map/outer/pallas_call | solution.py:233
  122.5 5.4 %collective-permute-start.66 = (f32[16,64,128]{2,1,0:T(8,128)S(1)}, f32[16,64,128]{2,1,0:T(8,128)S(1)}, u32[]{:S(2)}, u32[]{:S(2)}) collective-permute-start(f32[16,64,128]{2,1,0:T(8,128)S(1)} %get-tuple-element.175), channel_id=1, source_target_pairs={{1,0},{2,1},{3,2},{4,3},{5,4},{6,5},{7,6},{8,7},{9,8},{10,9},{11,1... | collective-permute-start | bytes 1572872 | tf_op jit(solution)/shard_map/ppermute | solution.py:319
  127.9 1.9 %collective-permute-start.67 = (f32[16,64,128]{2,1,0:T(8,128)S(1)}, f32[16,64,128]{2,1,0:T(8,128)S(1)}, u32[]{:S(2)}, u32[]{:S(2)}) collective-permute-start(f32[16,64,128]{2,1,0:T(8,128)S(1)} %get-tuple-element.176), channel_id=1, source_target_pairs={{0,1},{1,2},{2,3},{3,4},{4,5},{5,6},{6,7},{7,8},{8,9},{9,10},{10,1... | collective-permute-start | bytes 1572872 | tf_op jit(solution)/shard_map/ppermute | solution.py:320
  129.8 3.1 %inner.1 = f32[16,64,128]{2,1,0:T(8,128)S(1)} custom-call(f32[6,3,31]{2,1,0:T(4,128)S(1)} %copy-done.7, f32[6,16,32,128]{3,2,1,0:T(8,128)S(1)} %get-tuple-element.174.near_ref, bf16[128,192]{1,0:T(8,128)(2,1)S(1)} %get-tuple-element.173.refs_5_.lateral_ref), custom_call_target="tpu_custom_call" | custom-call | tf_op jit(solution)/shard_map/inner/pallas_call | solution.py:233
  132.9 5.6 %collective-permute-done.66 = f32[16,64,128]{2,1,0:T(8,128)S(1)} collective-permute-done((f32[16,64,128]{2,1,0:T(8,128)S(1)}, f32[16,64,128]{2,1,0:T(8,128)S(1)}, u32[]{:S(2)}, u32[]{:S(2)}) %collective-permute-start.66) | collective-permute-done | bytes 524320 | tf_op jit(solution)/shard_map/ppermute | solution.py:319
  138.5 5.3 %collective-permute-done.67 = f32[16,64,128]{2,1,0:T(8,128)S(1)} collective-permute-done((f32[16,64,128]{2,1,0:T(8,128)S(1)}, f32[16,64,128]{2,1,0:T(8,128)S(1)}, u32[]{:S(2)}, u32[]{:S(2)}) %collective-permute-start.67) | collective-permute-done | bytes 524320 | tf_op jit(solution)/shard_map/ppermute | solution.py:320
  143.9 4.4 %collective-permute-start.68 = (f32[16,16,128]{2,1,0:T(8,128)S(1)}, f32[16,16,128]{2,1,0:T(8,128)S(1)}, u32[]{:S(2)}, u32[]{:S(2)}) collective-permute-start(f32[16,16,128]{2,1,0:T(8,128)S(1)} %get-tuple-element.177), channel_id=1, source_target_pairs={{0,16},{16,32},{32,48},{48,64},{64,80},{80,96},{96,112},{112,128},... | collective-permute-start | bytes 393224 | tf_op jit(solution)/shard_map/ppermute | solution.py:332
  150.8 8.5 %collective-permute-done.69 = f32[16,16,128]{2,1,0:T(8,128)S(1)} collective-permute-done((f32[16,16,128]{2,1,0:T(8,128)S(1)}, f32[16,16,128]{2,1,0:T(8,128)S(1)}, u32[]{:S(2)}, u32[]{:S(2)}) %collective-permute-start.69) | collective-permute-done | bytes 131104 | tf_op jit(solution)/shard_map/ppermute | solution.py:331
  (45 shorter events, 14.9 us)
Async XLA Ops:
  1.0 11.1 %collective-permute-start.62 = (f32[16,16,128]{2,1,0:T(8,128)S(1)}, f32[16,16,128]{2,1,0:T(8,128)S(1)}, u32[]{:S(2)}, u32[]{:S(2)}) collective-permute-start(f32[16,16,128]{2,1,0:T(8,128)S(1)} %get-tuple-element.180), channel_id=1, source_target_pairs={{0,16},{16,32},{32,48},{48,64},{64,80},{80,96},{96,112},{112,128},... | collective-permute-start | bytes 393224 | tf_op jit(solution)/shard_map/ppermute | solution.py:268
  6.3 10.9 %collective-permute-start.63 = (f32[16,16,128]{2,1,0:T(8,128)S(1)}, f32[16,16,128]{2,1,0:T(8,128)S(1)}, u32[]{:S(2)}, u32[]{:S(2)}) collective-permute-start(f32[16,16,128]{2,1,0:T(8,128)S(1)} %get-tuple-element.179), channel_id=1, source_target_pairs={{16,0},{32,16},{48,32},{64,48},{80,64},{96,80},{112,96},{128,112},... | collective-permute-start | bytes 393224 | tf_op jit(solution)/shard_map/ppermute | solution.py:269
  8.2 1.4 copy-start
  12.1 18.2 %copy-start.10 = (f32[16,32,128]{2,1,0:T(8,128)S(1)}, f32[16,32,128]{2,1,0:T(8,128)}, u32[]{:S(2)}) copy-start(f32[16,32,128]{2,1,0:T(8,128)} %param.69) | copy-start | bytes 786436
  17.2 60.1 %all-to-all-start = ((f32[32,4,16,128]{3,2,1,0:T(8,128)}), f32[32,4,16,128]{3,2,1,0:T(8,128)S(1)}, u32[]{:S(2)}, u32[]{:S(2)}) async-start(f32[32,4,16,128]{3,2,1,0:T(8,128)} %get-tuple-element.159), calls=%async_computation | async-start | bytes 2097152 | tf_op jit(solution)/shard_map/all_to_all | solution.py:271
  30.4 46.9 %collective-permute-start.64 = (f32[16,64,128]{2,1,0:T(8,128)S(1)}, f32[16,64,128]{2,1,0:T(8,128)S(1)}, u32[]{:S(2)}, u32[]{:S(2)}) collective-permute-start(f32[16,64,128]{2,1,0:T(8,128)S(1)} %constant_dynamic-update-slice_fusion.mid_ref), channel_id=1, source_target_pairs={{0,1},{1,2},{2,3},{3,4},{4,5},{5,6},{6,7},{7,8},{8,9},{9,10},{10,1... | collective-permute-start | bytes 1572872 | tf_op jit(solution)/shard_map/ppermute | solution.py:273
  32.3 45.0 %collective-permute-start.65 = (f32[16,64,128]{2,1,0:T(8,128)S(1)}, f32[16,64,128]{2,1,0:T(8,128)S(1)}, u32[]{:S(2)}, u32[]{:S(2)}) collective-permute-start(f32[16,64,128]{2,1,0:T(8,128)S(1)} %constant_dynamic-update-slice_fusion.mid_ref), channel_id=1, source_target_pairs={{1,0},{2,1},{3,2},{4,3},{5,4},{6,5},{7,6},{8,7},{9,8},{10,9},{11,1... | collective-permute-start | bytes 1572872 | tf_op jit(solution)/shard_map/ppermute | solution.py:274
  38.1 27.4 %collective-permute-start.30 = (f32[16,32,128]{2,1,0:T(8,128)S(1)}, f32[16,32,128]{2,1,0:T(8,128)S(1)}, u32[]{:S(2)}, u32[]{:S(2)}) collective-permute-start(f32[16,32,128]{2,1,0:T(8,128)S(1)} %param.31), channel_id=1, source_target_pairs={{0,496},{16,0},{32,16},{48,32},{64,48},{80,64},{96,80},{112,96},{1... | collective-permute-start | bytes 786440 | tf_op jit(solution)/shard_map/cond/branch_31_fun/ppermute | solution.py:290
  65.5 13.7 %copy-start.12 = (f32[16,32,128]{2,1,0:T(8,128)}, f32[16,32,128]{2,1,0:T(8,128)S(1)}, u32[]{:S(2)}) copy-start(f32[16,32,128]{2,1,0:T(8,128)S(1)} %get-tuple-element.183.refs_1_) | copy-start | bytes 786436
  77.3 2.0 %copy-start.3 = (f32[16,64,128]{2,1,0:T(8,128)}, f32[16,64,128]{2,1,0:T(8,128)S(1)}, u32[]{:S(2)}) copy-start(f32[16,64,128]{2,1,0:T(8,128)S(1)} %collective-permute-done.64.low_ref) | copy-start | bytes 1572868
  77.3 2.0 %copy-start.5 = (f32[16,64,128]{2,1,0:T(8,128)}, f32[16,64,128]{2,1,0:T(8,128)S(1)}, u32[]{:S(2)}) copy-start(f32[16,64,128]{2,1,0:T(8,128)S(1)} %collective-permute-done.65.high_ref) | copy-start | bytes 1572868
  79.3 7.1 %copy-start.7 = (f32[6,3,31]{2,1,0:T(4,128)S(1)}, f32[6,3,31]{2,1,0:T(4,128)}, u32[]{:S(2)}) copy-start(f32[6,3,31]{2,1,0:T(4,128)} %taps_ref.7) | copy-start | bytes 6700
  79.3 39.1 %all-to-all-start.1 = ((f32[32,4,16,128]{3,2,1,0:T(8,128)}), f32[32,4,16,128]{3,2,1,0:T(8,128)S(1)}, u32[]{:S(2)}, u32[]{:S(2)}) async-start(f32[32,4,16,128]{3,2,1,0:T(8,128)} %turn.1), calls=%async_computation.1 | async-start | bytes 2097152 | tf_op jit(solution)/shard_map/all_to_all | solution.py:295
  88.0 0.9 copy-start.1
  89.5 1.0 copy-start.4
  90.6 1.0 copy-start.6
  97.2 21.2 %copy-start.2 = (bf16[6,256,256]{2,1,0:T(8,128)(2,1)S(1)}, bf16[6,256,256]{2,1,0:T(8,128)(2,1)}, u32[]{:S(2)}) copy-start(bf16[6,256,256]{2,1,0:T(8,128)(2,1)} %copy-done.1) | copy-start | bytes 2359300
  97.2 21.2 %copy-start.9 = (s32[6,1]{0,1:T(1,128)S(1)}, s32[6,1]{0,1:T(1,128)}, u32[]{:S(2)}) copy-start(s32[6,1]{0,1:T(1,128)} %param.73) | copy-start | bytes 76
  97.3 20.4 %collective-permute-start.32 = (f32[16,32,128]{2,1,0:T(8,128)}, f32[16,32,128]{2,1,0:T(8,128)S(1)}, u32[]{:S(2)}, u32[]{:S(2)}) collective-permute-start(f32[16,32,128]{2,1,0:T(8,128)} %param.34), channel_id=1, source_target_pairs={{0,32},{16,48},{32,64},{48,80},{64,96},{80,112},{96,128},{112,144}... | collective-permute-start | bytes 786440 | tf_op jit(solution)/shard_map/cond/branch_2_fun/ppermute | solution.py:290
  122.5 16.0 %collective-permute-start.66 = (f32[16,64,128]{2,1,0:T(8,128)S(1)}, f32[16,64,128]{2,1,0:T(8,128)S(1)}, u32[]{:S(2)}, u32[]{:S(2)}) collective-permute-start(f32[16,64,128]{2,1,0:T(8,128)S(1)} %get-tuple-element.175), channel_id=1, source_target_pairs={{1,0},{2,1},{3,2},{4,3},{5,4},{6,5},{7,6},{8,7},{9,8},{10,9},{11,1... | collective-permute-start | bytes 1572872 | tf_op jit(solution)/shard_map/ppermute | solution.py:319
  127.9 15.9 %collective-permute-start.67 = (f32[16,64,128]{2,1,0:T(8,128)S(1)}, f32[16,64,128]{2,1,0:T(8,128)S(1)}, u32[]{:S(2)}, u32[]{:S(2)}) collective-permute-start(f32[16,64,128]{2,1,0:T(8,128)S(1)} %get-tuple-element.176), channel_id=1, source_target_pairs={{0,1},{1,2},{2,3},{3,4},{4,5},{5,6},{6,7},{7,8},{8,9},{9,10},{10,1... | collective-permute-start | bytes 1572872 | tf_op jit(solution)/shard_map/ppermute | solution.py:320
  132.9 26.5 %copy-start.11 = (f32[16,32,128]{2,1,0:T(8,128)S(1)}, f32[16,32,128]{2,1,0:T(8,128)}, u32[]{:S(2)}) copy-start(f32[16,32,128]{2,1,0:T(8,128)} %param.69) | copy-start | bytes 786436
  143.9 6.9 %collective-permute-start.68 = (f32[16,16,128]{2,1,0:T(8,128)S(1)}, f32[16,16,128]{2,1,0:T(8,128)S(1)}, u32[]{:S(2)}, u32[]{:S(2)}) collective-permute-start(f32[16,16,128]{2,1,0:T(8,128)S(1)} %get-tuple-element.177), channel_id=1, source_target_pairs={{0,16},{16,32},{32,48},{48,64},{64,80},{80,96},{96,112},{112,128},... | collective-permute-start | bytes 393224 | tf_op jit(solution)/shard_map/ppermute | solution.py:332
  148.3 11.1 %collective-permute-start.69 = (f32[16,16,128]{2,1,0:T(8,128)S(1)}, f32[16,16,128]{2,1,0:T(8,128)S(1)}, u32[]{:S(2)}, u32[]{:S(2)}) collective-permute-start(f32[16,16,128]{2,1,0:T(8,128)S(1)} %get-tuple-element.178), channel_id=1, source_target_pairs={{16,0},{32,16},{48,32},{64,48},{80,64},{96,80},{112,96},{128,112},... | collective-permute-start | bytes 393224 | tf_op jit(solution)/shard_map/ppermute | solution.py:331
  (1 other events, 0.7 us)

commit v6 on v5

--- a/solution.py
+++ b/solution.py
@@ -10,7 +10,7 @@
 F32, BF16 = jnp.float32, jnp.bfloat16
 ROW = 8
 DIRECT = 2
-EARLY = 1
+EARLY = 2
 
 
 def split(values):
@@ -226,7 +226,7 @@
 
 SMEM = pl.BlockSpec(memory_space=pltpu.SMEM)
 VMEM = pl.BlockSpec(memory_space=pltpu.VMEM)
-PARAMS = pltpu.CompilerParams(vmem_limit_bytes=48 << 20)
+PARAMS = pltpu.CompilerParams(vmem_limit_bytes=12 << 20)
 
 
 def call(kernel, name, outs, scalars, arrays, scratch=(), out_specs=None):
@@ -327,10 +327,13 @@
         [(depth, views * rows, width)],
     )
 
-    total = own + from_above + from_below
-    from_right = lax.ppermute(total[:, :reach], "brick", left)
-    from_left = lax.ppermute(total[:, rows + reach :], "brick", right)
-    summed = total[:, reach : rows + reach]
+    def total(at):
+        return own[:, at] + from_above[:, at] + from_below[:, at]
+
+    faces = total(slice(0, reach)), total(slice(rows + reach, wide))
+    from_right = lax.ppermute(faces[0], "brick", left)
+    from_left = lax.ppermute(faces[1], "brick", right)
+    summed = total(slice(reach, rows + reach))
     gap = jnp.zeros((depth, rows - reach, width), F32)
     summed = summed + jnp.concatenate([from_left, gap], axis=1) + jnp.concatenate([gap, from_right], axis=1)
     cover_count = jnp.sum(coverage[:, 0].astype(F32))

time: 162 us -> 164 us (1.012)
  the two profiles are of different devices: /device:TPU:62 before, /device:TPU:60 now
where the time goes in v6:
time: 164 us; the launch traced here: 163 us
  waiting for transfers between devices  82.1 us (50%)
  starting transfers between devices  49.8 us (30%)
  Pallas kernels  18.3 us (11%)
  local copies, waits for them, and re-layouts  9.23 us (6%)
  other arithmetic  2.13 us (1%)
    ppermute x2, waiting for transfers between devices, send(): return lax.switch(moves[spread_views + slot], hops, x)  37.8 us
    all_to_all x1, waiting for transfers between devices, shards(): tiles = lax.all_to_all(turned, 'brick', 0, 0, tiled=True)  19.2 us
    pallas_call x6, Pallas kernels, call(): pl.pallas_call(kernel, out_shape=tuple((jax.ShapeDtypeStruct(shape, dtype...  18.3 us
    all_to_all x1, starting transfers between devices, shards(): spread = lax.all_to_all(pieces, 'brick', 0, 0, tiled=True)  13.1 us
    ppermute x1, waiting for transfers between devices, shards(): from_right = lax.ppermute(faces[0], 'brick', left)  7.62 us
    all_to_all x1, starting transfers between devices, shards(): tiles = lax.all_to_all(turned, 'brick', 0, 0, tiled=True)  7.21 us
    unnamed x24, local copies, waits for them, and re-layouts  6.21 us
    ppermute x1, starting transfers between devices, shards(): head = lax.ppermute(estimate[:, rows - reach:], 'brick', right)  5.29 us
  transfers between devices with their start and end apart: 12, of which 9 were waited for; matrix products, arithmetic and copies ran while one was open for 2% of the time, Pallas kernels for 7%

profile of v6, /device:TPU:60, one launch (start us, length us, event | category | flops | bytes accessed | tf_op | source)
XLA Modules:
  0.0 163.1 jit_solution(10550342998390969103)
XLA Ops:
  1.0 5.3 %collective-permute-start.62 = (f32[16,16,128]{2,1,0:T(8,128)S(1)}, f32[16,16,128]{2,1,0:T(8,128)S(1)}, u32[]{:S(2)}, u32[]{:S(2)}) collective-permute-start(f32[16,16,128]{2,1,0:T(8,128)S(1)} %get-tuple-element.178), channel_id=1, source_target_pairs={{0,16},{16,32},{32,48},{48,64},{64,80},{80,96},{96,112},{112,128},... | collective-permute-start | bytes 393224 | tf_op jit(solution)/shard_map/ppermute | solution.py:268
  6.3 1.9 %collective-permute-start.63 = (f32[16,16,128]{2,1,0:T(8,128)S(1)}, f32[16,16,128]{2,1,0:T(8,128)S(1)}, u32[]{:S(2)}, u32[]{:S(2)}) collective-permute-start(f32[16,16,128]{2,1,0:T(8,128)S(1)} %get-tuple-element.177), channel_id=1, source_target_pairs={{16,0},{32,16},{48,32},{64,48},{80,64},{96,80},{112,96},{128,112},... | collective-permute-start | bytes 393224 | tf_op jit(solution)/shard_map/ppermute | solution.py:269
  12.2 5.0 %collective-permute-done.63 = f32[16,16,128]{2,1,0:T(8,128)S(1)} collective-permute-done((f32[16,16,128]{2,1,0:T(8,128)S(1)}, f32[16,16,128]{2,1,0:T(8,128)S(1)}, u32[]{:S(2)}, u32[]{:S(2)}) %collective-permute-start.63) | collective-permute-done | bytes 131104 | tf_op jit(solution)/shard_map/ppermute | solution.py:269
  17.2 13.1 %all-to-all-start = ((f32[32,4,16,128]{3,2,1,0:T(8,128)}), f32[32,4,16,128]{3,2,1,0:T(8,128)S(1)}, u32[]{:S(2)}, u32[]{:S(2)}) async-start(f32[32,4,16,128]{3,2,1,0:T(8,128)} %get-tuple-element.158), calls=%async_computation | async-start | bytes 2097152 | tf_op jit(solution)/shard_map/all_to_all | solution.py:271
  30.4 1.9 %collective-permute-start.64 = (f32[16,64,128]{2,1,0:T(8,128)S(1)}, f32[16,64,128]{2,1,0:T(8,128)S(1)}, u32[]{:S(2)}, u32[]{:S(2)}) collective-permute-start(f32[16,64,128]{2,1,0:T(8,128)S(1)} %constant_dynamic-update-slice_fusion.mid_ref), channel_id=1, source_target_pairs={{0,1},{1,2},{2,3},{3,4},{4,5},{5,6},{6,7},{7,8},{8,9},{9,10},{10,1... | collective-permute-start | bytes 1572872 | tf_op jit(solution)/shard_map/ppermute | solution.py:273
  32.3 4.5 %collective-permute-start.65 = (f32[16,64,128]{2,1,0:T(8,128)S(1)}, f32[16,64,128]{2,1,0:T(8,128)S(1)}, u32[]{:S(2)}, u32[]{:S(2)}) collective-permute-start(f32[16,64,128]{2,1,0:T(8,128)S(1)} %constant_dynamic-update-slice_fusion.mid_ref), channel_id=1, source_target_pairs={{1,0},{2,1},{3,2},{4,3},{5,4},{6,5},{7,6},{8,7},{9,8},{10,9},{11,1... | collective-permute-start | bytes 1572872 | tf_op jit(solution)/shard_map/ppermute | solution.py:274
  38.7 27.3 %conditional.2 = (f32[16,32,128]{2,1,0:T(8,128)}) conditional(s32[]{:T(128)} %bitcast.2, f32[16,32,128]{2,1,0:T(8,128)} %get-tuple-element.161, f32[16,32,128]{2,1,0:T(8,128)} %get-tuple-element.161, f32[16,32,128]{2,1,0:T(8,128)} %get-tuple-element.161, f32[16,32,128]{2,1,0:T(8,128)} %get-tuple-element.161, ...), branch_computations={%region_0.0_spmd, %region_1.0_spmd, %region_2.0_spmd, %region_3.0_... | conditional | bytes 1572912 | solution.py:290
  38.8 3.4 %collective-permute-start.30 = (f32[16,32,128]{2,1,0:T(8,128)}, f32[16,32,128]{2,1,0:T(8,128)S(1)}, u32[]{:S(2)}, u32[]{:S(2)}) collective-permute-start(f32[16,32,128]{2,1,0:T(8,128)} %param.31), channel_id=1, source_target_pairs={{0,496},{16,0},{32,16},{48,32},{64,48},{80,64},{96,80},{112,96},{1... | collective-permute-start | bytes 786440 | tf_op jit(solution)/shard_map/cond/branch_31_fun/ppermute | solution.py:290
  42.2 23.2 %collective-permute-done.30 = f32[16,32,128]{2,1,0:T(8,128)S(1)} collective-permute-done((f32[16,32,128]{2,1,0:T(8,128)}, f32[16,32,128]{2,1,0:T(8,128)S(1)}, u32[]{:S(2)}, u32[]{:S(2)}) %collective-permute-start.30) | collective-permute-done | bytes 262176 | tf_op jit(solution)/shard_map/cond/branch_31_fun/ppermute | solution.py:290
  66.0 17.2 %conditional.3 = (f32[16,32,128]{2,1,0:T(8,128)}) conditional(s32[]{:T(128)} %bitcast.3, f32[16,32,128]{2,1,0:T(8,128)} %get-tuple-element.162, f32[16,32,128]{2,1,0:T(8,128)} %get-tuple-element.162, f32[16,32,128]{2,1,0:T(8,128)} %get-tuple-element.162, f32[16,32,128]{2,1,0:T(8,128)} %get-tuple-element.162, ...), branch_computations={%region_32.0_spmd, %region_33.0_spmd, %region_34.0_spmd, %region_3... | conditional | bytes 1572912 | solution.py:290
  67.9 14.6 %collective-permute-done.60 = f32[16,32,128]{2,1,0:T(8,128)S(1)} collective-permute-done((f32[16,32,128]{2,1,0:T(8,128)}, f32[16,32,128]{2,1,0:T(8,128)S(1)}, u32[]{:S(2)}, u32[]{:S(2)}) %collective-permute-start.60) | collective-permute-done | bytes 262176 | tf_op jit(solution)/shard_map/cond/branch_30_fun/ppermute | solution.py:290
  83.3 4.9 %collective-permute-done.64.low_ref = f32[16,64,128]{2,1,0:T(8,128)S(1)} collective-permute-done((f32[16,64,128]{2,1,0:T(8,128)S(1)}, f32[16,64,128]{2,1,0:T(8,128)S(1)}, u32[]{:S(2)}, u32[]{:S(2)}) %collective-permute-start.64) | collective-permute-done | bytes 524320 | tf_op jit(solution)/shard_map/ppermute | solution.py:273
  88.2 2.0 %turn.1 = f32[32,4,16,128]{3,2,1,0:T(8,128)} custom-call(s32[6]{0:T(128)S(1)} %get-tuple-element.156.offsets_ref, f32[32,4,16,128]{3,2,1,0:T(8,128)S(1)} %all-to-all-done.in_ref), custom_call_target="tpu_custom_call" | custom-call | tf_op jit(solution)/shard_map/turn/pallas_call | solution.py:233
  90.2 7.2 %all-to-all-start.1 = ((f32[32,4,16,128]{3,2,1,0:T(8,128)}), f32[32,4,16,128]{3,2,1,0:T(8,128)S(1)}, u32[]{:S(2)}, u32[]{:S(2)}) async-start(f32[32,4,16,128]{3,2,1,0:T(8,128)} %turn.1), calls=%async_computation.1 | async-start | bytes 2097152 | tf_op jit(solution)/shard_map/all_to_all | solution.py:295
  102.1 5.6 %forward.1.refs_3_ = f32[6,16,32,128]{3,2,1,0:T(8,128)S(1)} custom-call(f32[6,3,31]{2,1,0:T(4,128)S(1)} %copy-done.7, f32[16,64,128]{2,1,0:T(8,128)S(1)} %copy-done.4, f32[16,64,128]{2,1,0:T(8,128)S(1)} %constant_dynamic-update-slice_fusion.mid_ref, f32[16,64,128]{2,1,0:T(8,128)S(1)} %copy-done.6, bf16[192,192]{1,0:T(8,128)(2,1)S(1)} %get-tuple-element.168.lateral_ref, ...), custom_call_target="tpu_custom_call" | custom-call | tf_op jit(solution)/shard_map/forward/pallas_call | solution.py:233
  107.6 19.2 %all-to-all-done.1 = f32[32,4,16,128]{3,2,1,0:T(8,128)S(1)} async-done(((f32[32,4,16,128]{3,2,1,0:T(8,128)}), f32[32,4,16,128]{3,2,1,0:T(8,128)S(1)}, u32[]{:S(2)}, u32[]{:S(2)}) %all-to-all-start.1) | async-done | bytes 1048608 | tf_op jit(solution)/shard_map/all_to_all | solution.py:295
  128.0 4.2 %outer.1 = (f32[6,16,32,128]{3,2,1,0:T(8,128)S(1)}, f32[16,64,128]{2,1,0:T(8,128)S(1)}, f32[16,64,128]{2,1,0:T(8,128)S(1)}) custom-call(f32[6,3,31]{2,1,0:T(4,128)S(1)} %copy-done.7, s32[6]{0:T(128)S(1)} %bitcast.8, s32[6]{0:T(128)S(1)} %get-tuple-element.155.order_ref, f32[16,2,4,16,128]{4,3,2,1,0:T(8,128)S(1)} %bitcast.6, ...), custom_call_target="tpu_custom_call" | custom-call | tf_op jit(solution)/shard_map/outer/pallas_call | solution.py:233
  132.2 1.9 %collective-permute-start.66 = (f32[16,64,128]{2,1,0:T(8,128)S(1)}, f32[16,64,128]{2,1,0:T(8,128)S(1)}, u32[]{:S(2)}, u32[]{:S(2)}) collective-permute-start(f32[16,64,128]{2,1,0:T(8,128)S(1)} %get-tuple-element.173), channel_id=1, source_target_pairs={{1,0},{2,1},{3,2},{4,3},{5,4},{6,5},{7,6},{8,7},{9,8},{10,9},{11,1... | collective-permute-start | bytes 1572872 | tf_op jit(solution)/shard_map/ppermute | solution.py:319
  134.1 2.4 %collective-permute-start.67 = (f32[16,64,128]{2,1,0:T(8,128)S(1)}, f32[16,64,128]{2,1,0:T(8,128)S(1)}, u32[]{:S(2)}, u32[]{:S(2)}) collective-permute-start(f32[16,64,128]{2,1,0:T(8,128)S(1)} %get-tuple-element.174), channel_id=1, source_target_pairs={{0,1},{1,2},{2,3},{3,4},{4,5},{5,6},{6,7},{7,8},{8,9},{9,10},{10,1... | collective-permute-start | bytes 1572872 | tf_op jit(solution)/shard_map/ppermute | solution.py:320
  136.5 3.1 %inner.1 = f32[16,64,128]{2,1,0:T(8,128)S(1)} custom-call(f32[6,3,31]{2,1,0:T(4,128)S(1)} %copy-done.7, f32[6,16,32,128]{3,2,1,0:T(8,128)S(1)} %get-tuple-element.172.near_ref, bf16[128,192]{1,0:T(8,128)(2,1)S(1)} %get-tuple-element.171.refs_5_.lateral_ref), custom_call_target="tpu_custom_call" | custom-call | tf_op jit(solution)/shard_map/inner/pallas_call | solution.py:233
  139.6 5.0 %collective-permute-done.66 = f32[16,64,128]{2,1,0:T(8,128)S(1)} collective-permute-done((f32[16,64,128]{2,1,0:T(8,128)S(1)}, f32[16,64,128]{2,1,0:T(8,128)S(1)}, u32[]{:S(2)}, u32[]{:S(2)}) %collective-permute-start.66) | collective-permute-done | bytes 524320 | tf_op jit(solution)/shard_map/ppermute | solution.py:319
  146.4 3.5 %collective-permute-start.68 = (f32[16,16,128]{2,1,0:T(8,128)S(1)}, f32[16,16,128]{2,1,0:T(8,128)S(1)}, u32[]{:S(2)}, u32[]{:S(2)}) collective-permute-start(f32[16,16,128]{2,1,0:T(8,128)S(1)} %get-tuple-element.175), channel_id=1, source_target_pairs={{0,16},{16,32},{32,48},{48,64},{64,80},{80,96},{96,112},{112,128},... | collective-permute-start | bytes 393224 | tf_op jit(solution)/shard_map/ppermute | solution.py:335
  149.9 2.8 %collective-permute-start.69 = (f32[16,16,128]{2,1,0:T(8,128)S(1)}, f32[16,16,128]{2,1,0:T(8,128)S(1)}, u32[]{:S(2)}, u32[]{:S(2)}) collective-permute-start(f32[16,16,128]{2,1,0:T(8,128)S(1)} %get-tuple-element.176), channel_id=1, source_target_pairs={{16,0},{32,16},{48,32},{64,48},{80,64},{96,80},{112,96},{128,112},... | collective-permute-start | bytes 393224 | tf_op jit(solution)/shard_map/ppermute | solution.py:334
  154.0 7.6 %collective-permute-done.69 = f32[16,16,128]{2,1,0:T(8,128)S(1)} collective-permute-done((f32[16,16,128]{2,1,0:T(8,128)S(1)}, f32[16,16,128]{2,1,0:T(8,128)S(1)}, u32[]{:S(2)}, u32[]{:S(2)}) %collective-permute-start.69) | collective-permute-done | bytes 131104 | tf_op jit(solution)/shard_map/ppermute | solution.py:334
  (40 shorter events, 19.3 us)
Async XLA Ops:
  1.0 11.2 %collective-permute-start.62 = (f32[16,16,128]{2,1,0:T(8,128)S(1)}, f32[16,16,128]{2,1,0:T(8,128)S(1)}, u32[]{:S(2)}, u32[]{:S(2)}) collective-permute-start(f32[16,16,128]{2,1,0:T(8,128)S(1)} %get-tuple-element.178), channel_id=1, source_target_pairs={{0,16},{16,32},{32,48},{48,64},{64,80},{80,96},{96,112},{112,128},... | collective-permute-start | bytes 393224 | tf_op jit(solution)/shard_map/ppermute | solution.py:268
  6.3 10.9 %collective-permute-start.63 = (f32[16,16,128]{2,1,0:T(8,128)S(1)}, f32[16,16,128]{2,1,0:T(8,128)S(1)}, u32[]{:S(2)}, u32[]{:S(2)}) collective-permute-start(f32[16,16,128]{2,1,0:T(8,128)S(1)} %get-tuple-element.177), channel_id=1, source_target_pairs={{16,0},{32,16},{48,32},{64,48},{80,64},{96,80},{112,96},{128,112},... | collective-permute-start | bytes 393224 | tf_op jit(solution)/shard_map/ppermute | solution.py:269
  8.2 1.4 copy-start
  9.6 0.7 copy-start.8
  12.2 18.1 %copy-start.10 = (f32[16,32,128]{2,1,0:T(8,128)S(1)}, f32[16,32,128]{2,1,0:T(8,128)}, u32[]{:S(2)}) copy-start(f32[16,32,128]{2,1,0:T(8,128)} %param.69) | copy-start | bytes 786436
  17.2 71.0 %all-to-all-start = ((f32[32,4,16,128]{3,2,1,0:T(8,128)}), f32[32,4,16,128]{3,2,1,0:T(8,128)S(1)}, u32[]{:S(2)}, u32[]{:S(2)}) async-start(f32[32,4,16,128]{3,2,1,0:T(8,128)} %get-tuple-element.158), calls=%async_computation | async-start | bytes 2097152 | tf_op jit(solution)/shard_map/all_to_all | solution.py:271
  30.4 57.8 %collective-permute-start.64 = (f32[16,64,128]{2,1,0:T(8,128)S(1)}, f32[16,64,128]{2,1,0:T(8,128)S(1)}, u32[]{:S(2)}, u32[]{:S(2)}) collective-permute-start(f32[16,64,128]{2,1,0:T(8,128)S(1)} %constant_dynamic-update-slice_fusion.mid_ref), channel_id=1, source_target_pairs={{0,1},{1,2},{2,3},{3,4},{4,5},{5,6},{6,7},{7,8},{8,9},{9,10},{10,1... | collective-permute-start | bytes 1572872 | tf_op jit(solution)/shard_map/ppermute | solution.py:273
  32.3 55.9 %collective-permute-start.65 = (f32[16,64,128]{2,1,0:T(8,128)S(1)}, f32[16,64,128]{2,1,0:T(8,128)S(1)}, u32[]{:S(2)}, u32[]{:S(2)}) collective-permute-start(f32[16,64,128]{2,1,0:T(8,128)S(1)} %constant_dynamic-update-slice_fusion.mid_ref), channel_id=1, source_target_pairs={{1,0},{2,1},{3,2},{4,3},{5,4},{6,5},{7,6},{8,7},{9,8},{10,9},{11,1... | collective-permute-start | bytes 1572872 | tf_op jit(solution)/shard_map/ppermute | solution.py:274
  38.8 26.5 %collective-permute-start.30 = (f32[16,32,128]{2,1,0:T(8,128)}, f32[16,32,128]{2,1,0:T(8,128)S(1)}, u32[]{:S(2)}, u32[]{:S(2)}) collective-permute-start(f32[16,32,128]{2,1,0:T(8,128)} %param.31), channel_id=1, source_target_pairs={{0,496},{16,0},{32,16},{48,32},{64,48},{80,64},{96,80},{112,96},{1... | collective-permute-start | bytes 786440 | tf_op jit(solution)/shard_map/cond/branch_31_fun/ppermute | solution.py:290
  66.0 16.5 %collective-permute-start.60 = (f32[16,32,128]{2,1,0:T(8,128)}, f32[16,32,128]{2,1,0:T(8,128)S(1)}, u32[]{:S(2)}, u32[]{:S(2)}) collective-permute-start(f32[16,32,128]{2,1,0:T(8,128)} %param.62), channel_id=1, source_target_pairs={{0,480},{16,496},{32,0},{48,16},{64,32},{80,48},{96,64},{112,80},{... | collective-permute-start | bytes 786440 | tf_op jit(solution)/shard_map/cond/branch_30_fun/ppermute | solution.py:290
  88.2 2.0 %copy-start.3 = (f32[16,64,128]{2,1,0:T(8,128)}, f32[16,64,128]{2,1,0:T(8,128)S(1)}, u32[]{:S(2)}) copy-start(f32[16,64,128]{2,1,0:T(8,128)S(1)} %collective-permute-done.64.low_ref) | copy-start | bytes 1572868
  88.2 2.0 %copy-start.5 = (f32[16,64,128]{2,1,0:T(8,128)}, f32[16,64,128]{2,1,0:T(8,128)S(1)}, u32[]{:S(2)}) copy-start(f32[16,64,128]{2,1,0:T(8,128)S(1)} %collective-permute-done.65.high_ref) | copy-start | bytes 1572868
  90.2 7.2 %copy-start.7 = (f32[6,3,31]{2,1,0:T(4,128)S(1)}, f32[6,3,31]{2,1,0:T(4,128)}, u32[]{:S(2)}) copy-start(f32[6,3,31]{2,1,0:T(4,128)} %taps_ref.7) | copy-start | bytes 6700
  90.2 36.6 %all-to-all-start.1 = ((f32[32,4,16,128]{3,2,1,0:T(8,128)}), f32[32,4,16,128]{3,2,1,0:T(8,128)S(1)}, u32[]{:S(2)}, u32[]{:S(2)}) async-start(f32[32,4,16,128]{3,2,1,0:T(8,128)} %turn.1), calls=%async_computation.1 | async-start | bytes 2097152 | tf_op jit(solution)/shard_map/all_to_all | solution.py:295
  99.1 0.9 copy-start.1
  100.0 1.0 copy-start.4
  101.0 1.0 copy-start.6
  102.1 24.8 %copy-start.9 = (s32[6,1]{0,1:T(1,128)S(1)}, s32[6,1]{0,1:T(1,128)}, u32[]{:S(2)}) copy-start(s32[6,1]{0,1:T(1,128)} %param.73) | copy-start | bytes 76
  126.9 1.1 copy-start.2
  132.2 12.4 %collective-permute-start.66 = (f32[16,64,128]{2,1,0:T(8,128)S(1)}, f32[16,64,128]{2,1,0:T(8,128)S(1)}, u32[]{:S(2)}, u32[]{:S(2)}) collective-permute-start(f32[16,64,128]{2,1,0:T(8,128)S(1)} %get-tuple-element.173), channel_id=1, source_target_pairs={{1,0},{2,1},{3,2},{4,3},{5,4},{6,5},{7,6},{8,7},{9,8},{10,9},{11,1... | collective-permute-start | bytes 1572872 | tf_op jit(solution)/shard_map/ppermute | solution.py:319
  134.1 12.2 %collective-permute-start.67 = (f32[16,64,128]{2,1,0:T(8,128)S(1)}, f32[16,64,128]{2,1,0:T(8,128)S(1)}, u32[]{:S(2)}, u32[]{:S(2)}) collective-permute-start(f32[16,64,128]{2,1,0:T(8,128)S(1)} %get-tuple-element.174), channel_id=1, source_target_pairs={{0,1},{1,2},{2,3},{3,4},{4,5},{5,6},{6,7},{7,8},{8,9},{9,10},{10,1... | collective-permute-start | bytes 1572872 | tf_op jit(solution)/shard_map/ppermute | solution.py:320
  146.4 7.7 %collective-permute-start.68 = (f32[16,16,128]{2,1,0:T(8,128)S(1)}, f32[16,16,128]{2,1,0:T(8,128)S(1)}, u32[]{:S(2)}, u32[]{:S(2)}) collective-permute-start(f32[16,16,128]{2,1,0:T(8,128)S(1)} %get-tuple-element.175), channel_id=1, source_target_pairs={{0,16},{16,32},{32,48},{48,64},{64,80},{80,96},{96,112},{112,128},... | collective-permute-start | bytes 393224 | tf_op jit(solution)/shard_map/ppermute | solution.py:335
  149.9 11.8 %collective-permute-start.69 = (f32[16,16,128]{2,1,0:T(8,128)S(1)}, f32[16,16,128]{2,1,0:T(8,128)S(1)}, u32[]{:S(2)}, u32[]{:S(2)}) collective-permute-start(f32[16,16,128]{2,1,0:T(8,128)S(1)} %get-tuple-element.176), channel_id=1, source_target_pairs={{16,0},{32,16},{48,32},{64,48},{80,64},{96,80},{112,96},{128,112},... | collective-permute-start | bytes 393224 | tf_op jit(solution)/shard_map/ppermute | solution.py:334

commit v7 on v6

--- a/solution.py
+++ b/solution.py
@@ -124,15 +124,15 @@
         out_ref[view] = across_pass(out_ref[view], across_ref[view])
 
 
-def axial_back(half, taps_ref, near_ref, wide_ref, places):
-    views, depth, rows, width = near_ref.shape
+def axial_back(half, taps_ref, near_ref, wide_ref, places, count, view_of, place_of):
+    depth, rows, width = near_ref.shape[1:]
     start = depth - half
 
-    def body(view, carry):
-        taps = normal(taps_ref, view, 0)
+    def body(number, carry):
+        taps, place = normal(taps_ref, view_of(number), 0), place_of(number)
         for group in range(rows // 8):
-            into = pl.ds(pl.multiple_of(view * rows + group * 8, 8), 8)
-            field = [near_ref[view, z, group * 8 : group * 8 + 8, :] for z in range(depth)]
+            into = pl.ds(pl.multiple_of(place * rows + group * 8, 8), 8)
+            field = [near_ref[place, z, group * 8 : group * 8 + 8, :] for z in range(depth)]
             for slot, z in enumerate(places):
                 total = None
                 for source in range(depth):
@@ -143,7 +143,7 @@
                 wide_ref[slot, into, :] = jnp.zeros((8, width), F32) if total is None else total
         return carry
 
-    lax.fori_loop(0, views, body, 0)
+    lax.fori_loop(0, count, body, 0)
 
 
 def lateral_back(lateral_ref, wide_ref, first, out_ref):
@@ -160,27 +160,46 @@
     lax.fori_loop(0, depth // 2, body, 0, unroll=True)
 
 
+def outer_places(depth):
+    return list(range(depth)) + list(range(2 * depth, 3 * depth))
+
+
+def ahead_kernel(half, taps_ref, cover_ref, order_ref, *refs):
+    *direct, blurred_ref, across_ref, near_ref, wide_ref = refs
+    depth = blurred_ref.shape[1]
+    first = blurred_ref.shape[0] - len(direct)
+    for number, tile_ref in enumerate(direct):
+        view = order_ref[first + number]
+        near_ref[number] = across_pass(cover_ref[view].astype(F32) * tile_ref[...] / blurred_ref[view], across_ref[view])
+    view_of = lambda number: order_ref[first + number]
+    axial_back(half, taps_ref, near_ref, wide_ref, outer_places(depth), len(direct), view_of, lambda number: number)
+
+
 def outer_kernel(half, taps_ref, cover_ref, order_ref, *refs):
-    tiles_ref, *direct = refs[:-7]
-    blurred_ref, across_ref, lateral_ref, near_ref, low_ref, high_ref, wide_ref = refs[-7:]
+    tiles_ref, near_ahead_ref, wide_ahead_ref, blurred_ref, across_ref, lateral_ref, near_ref, low_ref, high_ref, wide_ref = refs
     views, depth, rows, width = blurred_ref.shape
     halves, spread = tiles_ref.shape[1:3]
     for slot in range(views):
         view = order_ref[slot]
         if slot < spread:
             owned = jnp.concatenate([tiles_ref[:, part, slot] for part in range(halves)], axis=1)
+            ratio = cover_ref[view].astype(F32) * owned / blurred_ref[view]
+            near_ref[view] = across_pass(ratio, across_ref[view])
         else:
-            owned = direct[slot - spread][...]
-        ratio = cover_ref[view].astype(F32) * owned / blurred_ref[view]
-        near_ref[view] = across_pass(ratio, across_ref[view])
-    axial_back(half, taps_ref, near_ref, wide_ref, list(range(depth)) + list(range(2 * depth, 3 * depth)))
+            number = slot - spread
+            near_ref[view] = near_ahead_ref[number]
+            at = pl.ds(pl.multiple_of(view * rows, 8), rows)
+            wide_ref[:, at, :] = wide_ahead_ref[:, number * rows : (number + 1) * rows, :]
+    view_of = lambda slot: order_ref[slot]
+    axial_back(half, taps_ref, near_ref, wide_ref, outer_places(depth), spread, view_of, view_of)
     lateral_back(lateral_ref, wide_ref, 0, low_ref)
     lateral_back(lateral_ref, wide_ref, depth, high_ref)
 
 
 def inner_kernel(half, taps_ref, near_ref, lateral_ref, mid_ref, wide_ref):
-    depth = near_ref.shape[1]
-    axial_back(half, taps_ref, near_ref, wide_ref, list(range(depth, 2 * depth)))
+    views, depth = near_ref.shape[:2]
+    same = lambda view: view
+    axial_back(half, taps_ref, near_ref, wide_ref, list(range(depth, 2 * depth)), views, same, same)
     lateral_back(lateral_ref, wide_ref, 0, mid_ref)
 
 
@@ -307,13 +326,20 @@
     blurred, *waiting = lax.optimization_barrier((blurred, *straight[EARLY:]))
     sent += [send(EARLY + slot, x) for slot, x in enumerate(waiting)]
 
+    near_ahead, wide_ahead = call(
+        functools.partial(ahead_kernel, half),
+        "ahead",
+        [((DIRECT, depth, rows, width), F32), ((2 * depth, DIRECT * rows, width), F32)],
+        [psf_taps, coverage[:, 0], order],
+        [*sent, blurred, across_off],
+    )
     slab = ((depth, wide, width), F32)
     near, below, above = call(
         functools.partial(outer_kernel, half),
         "outer",
         [((views, depth, rows, width), F32), slab, slab],
         [psf_taps, coverage[:, 0], order],
-        [tiles, *sent, blurred, across_off, lateral_off],
+        [tiles, near_ahead, wide_ahead, blurred, across_off, lateral_off],
         [(2 * depth, views * rows, width)],
     )
     from_above = lax.ppermute(below, "stack", down)

time: 164 us -> 164 us (level)
  waiting for transfers between devices: 82.1 us -> 77.3 us
  local copies, waits for them, and re-layouts: 9.23 us -> 11.7 us
  starting transfers between devices: 49.8 us -> 51.5 us
    unnamed x24 -> x42, local copies, waits for them, and re-layouts: 6.21 us -> 9.98 us
    all_to_all x1, waiting for transfers between devices: 19.2 us -> 15.6 us  [shards(): tiles = lax.all_to_all(turned, 'brick', 0, 0, tiled=True)]
    ppermute x2, waiting for transfers between devices: 37.8 us -> 34.2 us  [send(): return lax.switch(moves[spread_views + slot], hops, x)]
    ppermute x1, waiting for transfers between devices: 4.93 us -> 7.21 us  [shards(): low = lax.ppermute(mid, 'stack', up)]
    pallas_call x6 -> x7, Pallas kernels: 18.3 us -> 18.8 us  [call(): pl.pallas_call(kernel, out_shape=tuple((jax.ShapeDtypeStruct(shape, dtype...]
  transfers between devices with their start and end apart: 12 -> 12, of which waited for: 9 -> 9; matrix products, arithmetic and copies ran while one was open for 2% -> 1% of each run, Pallas kernels for 7% -> 8%
where the time goes in v7:
time: 164 us; the launch traced here: 163 us
  waiting for transfers between devices  77.3 us (47%)
  starting transfers between devices  51.5 us (31%)
  Pallas kernels  18.8 us (11%)
  local copies, waits for them, and re-layouts  11.7 us (7%)
  other arithmetic  2.21 us (1%)
  between operations  1.65 us (1%)
    ppermute x2, waiting for transfers between devices, send(): return lax.switch(moves[spread_views + slot], hops, x)  34.2 us
    pallas_call x7, Pallas kernels, call(): pl.pallas_call(kernel, out_shape=tuple((jax.ShapeDtypeStruct(shape, dtype...  18.8 us
    all_to_all x1, waiting for transfers between devices, shards(): tiles = lax.all_to_all(turned, 'brick', 0, 0, tiled=True)  15.6 us
    all_to_all x1, starting transfers between devices, shards(): spread = lax.all_to_all(pieces, 'brick', 0, 0, tiled=True)  13.1 us
    unnamed x42, local copies, waits for them, and re-layouts  9.98 us
    all_to_all x1, starting transfers between devices, shards(): tiles = lax.all_to_all(turned, 'brick', 0, 0, tiled=True)  7.96 us
    ppermute x1, waiting for transfers between devices, shards(): from_right = lax.ppermute(faces[0], 'brick', left)  7.62 us
    ppermute x1, waiting for transfers between devices, shards(): low = lax.ppermute(mid, 'stack', up)  7.21 us
  transfers between devices with their start and end apart: 12, of which 9 were waited for; matrix products, arithmetic and copies ran while one was open for 1% of the time, Pallas kernels for 8%

profile of v7, /device:TPU:60, one launch (start us, length us, event | category | flops | bytes accessed | tf_op | source)
XLA Modules:
  0.0 163.2 jit_solution(1377177082631560003)
XLA Ops:
  1.0 5.3 %collective-permute-start.62 = (f32[16,16,128]{2,1,0:T(8,128)S(1)}, f32[16,16,128]{2,1,0:T(8,128)S(1)}, u32[]{:S(2)}, u32[]{:S(2)}) collective-permute-start(f32[16,16,128]{2,1,0:T(8,128)S(1)} %get-tuple-element.182), channel_id=1, source_target_pairs={{0,16},{16,32},{32,48},{48,64},{64,80},{80,96},{96,112},{112,128},... | collective-permute-start | bytes 393224 | tf_op jit(solution)/shard_map/ppermute | solution.py:287
  6.3 1.9 %collective-permute-start.63 = (f32[16,16,128]{2,1,0:T(8,128)S(1)}, f32[16,16,128]{2,1,0:T(8,128)S(1)}, u32[]{:S(2)}, u32[]{:S(2)}) collective-permute-start(f32[16,16,128]{2,1,0:T(8,128)S(1)} %get-tuple-element.181), channel_id=1, source_target_pairs={{16,0},{32,16},{48,32},{64,48},{80,64},{96,80},{112,96},{128,112},... | collective-permute-start | bytes 393224 | tf_op jit(solution)/shard_map/ppermute | solution.py:288
  12.0 5.1 %collective-permute-done.63 = f32[16,16,128]{2,1,0:T(8,128)S(1)} collective-permute-done((f32[16,16,128]{2,1,0:T(8,128)S(1)}, f32[16,16,128]{2,1,0:T(8,128)S(1)}, u32[]{:S(2)}, u32[]{:S(2)}) %collective-permute-start.63) | collective-permute-done | bytes 131104 | tf_op jit(solution)/shard_map/ppermute | solution.py:288
  17.2 13.1 %all-to-all-start = ((f32[32,4,16,128]{3,2,1,0:T(8,128)}), f32[32,4,16,128]{3,2,1,0:T(8,128)S(1)}, u32[]{:S(2)}, u32[]{:S(2)}) async-start(f32[32,4,16,128]{3,2,1,0:T(8,128)} %get-tuple-element.160), calls=%async_computation | async-start | bytes 2097152 | tf_op jit(solution)/shard_map/all_to_all | solution.py:290
  30.4 1.9 %collective-permute-start.64 = (f32[16,64,128]{2,1,0:T(8,128)S(1)}, f32[16,64,128]{2,1,0:T(8,128)S(1)}, u32[]{:S(2)}, u32[]{:S(2)}) collective-permute-start(f32[16,64,128]{2,1,0:T(8,128)S(1)} %constant_dynamic-update-slice_fusion.mid_ref), channel_id=1, source_target_pairs={{0,1},{1,2},{2,3},{3,4},{4,5},{5,6},{6,7},{7,8},{8,9},{9,10},{10,1... | collective-permute-start | bytes 1572872 | tf_op jit(solution)/shard_map/ppermute | solution.py:292
  32.3 4.5 %collective-permute-start.65 = (f32[16,64,128]{2,1,0:T(8,128)S(1)}, f32[16,64,128]{2,1,0:T(8,128)S(1)}, u32[]{:S(2)}, u32[]{:S(2)}) collective-permute-start(f32[16,64,128]{2,1,0:T(8,128)S(1)} %constant_dynamic-update-slice_fusion.mid_ref), channel_id=1, source_target_pairs={{1,0},{2,1},{3,2},{4,3},{5,4},{6,5},{7,6},{8,7},{9,8},{10,9},{11,1... | collective-permute-start | bytes 1572872 | tf_op jit(solution)/shard_map/ppermute | solution.py:293
  38.9 25.9 %conditional.2 = (f32[16,32,128]{2,1,0:T(8,128)S(1)}) conditional(s32[]{:T(128)} %bitcast.2, f32[16,32,128]{2,1,0:T(8,128)S(1)} %get-tuple-element.163, f32[16,32,128]{2,1,0:T(8,128)S(1)} %get-tuple-element.163, f32[16,32,128]{2,1,0:T(8,128)S(1)} %get-tuple-element.163, ...), branch_computations={%region_0.0_spmd, %region_1.0_spmd, %region_2.0_spmd, %region_3.0_... | conditional | bytes 1572912 | solution.py:309
  38.9 4.3 %collective-permute-start.29 = (f32[16,32,128]{2,1,0:T(8,128)S(1)}, f32[16,32,128]{2,1,0:T(8,128)S(1)}, u32[]{:S(2)}, u32[]{:S(2)}) collective-permute-start(f32[16,32,128]{2,1,0:T(8,128)S(1)} %param.30), channel_id=1, source_target_pairs={{0,480},{16,496},{32,0},{48,16},{64,32},{80,48},{96,64},{112,80},{... | collective-permute-start | bytes 786440 | tf_op jit(solution)/shard_map/cond/branch_30_fun/ppermute | solution.py:309
  43.2 21.5 %collective-permute-done.29 = f32[16,32,128]{2,1,0:T(8,128)S(1)} collective-permute-done((f32[16,32,128]{2,1,0:T(8,128)S(1)}, f32[16,32,128]{2,1,0:T(8,128)S(1)}, u32[]{:S(2)}, u32[]{:S(2)}) %collective-permute-start.29) | collective-permute-done | bytes 262176 | tf_op jit(solution)/shard_map/cond/branch_30_fun/ppermute | solution.py:309
  65.4 14.7 %conditional.3 = (f32[16,32,128]{2,1,0:T(8,128)S(1)}) conditional(s32[]{:T(128)} %bitcast.3, f32[16,32,128]{2,1,0:T(8,128)S(1)} %get-tuple-element.164, f32[16,32,128]{2,1,0:T(8,128)S(1)} %get-tuple-element.164, f32[16,32,128]{2,1,0:T(8,128)S(1)} %get-tuple-element.164, ...), branch_computations={%region_32.0_spmd, %region_33.0_spmd, %region_34.0_spmd, %region_3... | conditional | bytes 1572912 | solution.py:309
  67.3 12.7 %collective-permute-done.55 = f32[16,32,128]{2,1,0:T(8,128)S(1)} collective-permute-done((f32[16,32,128]{2,1,0:T(8,128)S(1)}, f32[16,32,128]{2,1,0:T(8,128)S(1)}, u32[]{:S(2)}, u32[]{:S(2)}) %collective-permute-start.55) | collective-permute-done | bytes 262176 | tf_op jit(solution)/shard_map/cond/branch_25_fun/ppermute | solution.py:309
  80.1 7.2 %collective-permute-done.64.low_ref = f32[16,64,128]{2,1,0:T(8,128)S(1)} collective-permute-done((f32[16,64,128]{2,1,0:T(8,128)S(1)}, f32[16,64,128]{2,1,0:T(8,128)S(1)}, u32[]{:S(2)}, u32[]{:S(2)}) %collective-permute-start.64) | collective-permute-done | bytes 524320 | tf_op jit(solution)/shard_map/ppermute | solution.py:292
  87.3 2.0 %turn.1 = f32[32,4,16,128]{3,2,1,0:T(8,128)} custom-call(s32[6]{0:T(128)S(1)} %get-tuple-element.158.offsets_ref, f32[32,4,16,128]{3,2,1,0:T(8,128)S(1)} %all-to-all-done.in_ref), custom_call_target="tpu_custom_call" | custom-call | tf_op jit(solution)/shard_map/turn/pallas_call | solution.py:252
  89.4 8.0 %all-to-all-start.1 = ((f32[32,4,16,128]{3,2,1,0:T(8,128)}), f32[32,4,16,128]{3,2,1,0:T(8,128)S(1)}, u32[]{:S(2)}, u32[]{:S(2)}) async-start(f32[32,4,16,128]{3,2,1,0:T(8,128)} %turn.1), calls=%async_computation.1 | async-start | bytes 2097152 | tf_op jit(solution)/shard_map/all_to_all | solution.py:314
  102.1 5.5 %forward.1.refs_2_.refs_3_ = f32[6,16,32,128]{3,2,1,0:T(8,128)S(1)} custom-call(f32[6,3,31]{2,1,0:T(4,128)S(1)} %copy-done.11, f32[16,64,128]{2,1,0:T(8,128)S(1)} %copy-done.6, f32[16,64,128]{2,1,0:T(8,128)S(1)} %copy-done.4, f32[16,64,128]{2,1,0:T(8,128)S(1)} %copy-done.8, bf16[192,192]{1,0:T(8,128)(2,1)S(1)} %get-tuple-element.170.lateral_ref, ...), custom_call_target="tpu_custom_call" | custom-call | tf_op jit(solution)/shard_map/forward/pallas_call | solution.py:252
  111.1 15.6 %all-to-all-done.1 = f32[32,4,16,128]{3,2,1,0:T(8,128)S(1)} async-done(((f32[32,4,16,128]{3,2,1,0:T(8,128)}), f32[32,4,16,128]{3,2,1,0:T(8,128)S(1)}, u32[]{:S(2)}, u32[]{:S(2)}) %all-to-all-start.1) | async-done | bytes 1048608 | tf_op jit(solution)/shard_map/all_to_all | solution.py:314
  129.0 3.2 %outer.1 = (f32[6,16,32,128]{3,2,1,0:T(8,128)S(1)}, f32[16,64,128]{2,1,0:T(8,128)S(1)}, f32[16,64,128]{2,1,0:T(8,128)S(1)}) custom-call(f32[6,3,31]{2,1,0:T(4,128)S(1)} %copy-done.11, s32[6]{0:T(128)S(1)} %bitcast.9, s32[6]{0:T(128)S(1)} %get-tuple-element.157.order_ref, f32[16,2,4,16,128]{4,3,2,1,0:T(8,128)S(1)} %bitcast.6, ...), custom_call_target="tpu_custom_call" | custom-call | tf_op jit(solution)/shard_map/outer/pallas_call | solution.py:252
  132.2 1.9 %collective-permute-start.66 = (f32[16,64,128]{2,1,0:T(8,128)S(1)}, f32[16,64,128]{2,1,0:T(8,128)S(1)}, u32[]{:S(2)}, u32[]{:S(2)}) collective-permute-start(f32[16,64,128]{2,1,0:T(8,128)S(1)} %get-tuple-element.177), channel_id=1, source_target_pairs={{1,0},{2,1},{3,2},{4,3},{5,4},{6,5},{7,6},{8,7},{9,8},{10,9},{11,1... | collective-permute-start | bytes 1572872 | tf_op jit(solution)/shard_map/ppermute | solution.py:345
  134.1 2.4 %collective-permute-start.67 = (f32[16,64,128]{2,1,0:T(8,128)S(1)}, f32[16,64,128]{2,1,0:T(8,128)S(1)}, u32[]{:S(2)}, u32[]{:S(2)}) collective-permute-start(f32[16,64,128]{2,1,0:T(8,128)S(1)} %get-tuple-element.178), channel_id=1, source_target_pairs={{0,1},{1,2},{2,3},{3,4},{4,5},{5,6},{6,7},{7,8},{8,9},{9,10},{10,1... | collective-permute-start | bytes 1572872 | tf_op jit(solution)/shard_map/ppermute | solution.py:346
  136.6 3.1 %inner.1 = f32[16,64,128]{2,1,0:T(8,128)S(1)} custom-call(f32[6,3,31]{2,1,0:T(4,128)S(1)} %copy-done.11, f32[6,16,32,128]{3,2,1,0:T(8,128)S(1)} %get-tuple-element.176.near_ref, bf16[128,192]{1,0:T(8,128)(2,1)S(1)} %get-tuple-element.175.refs_5_.lateral_ref), custom_call_target="tpu_custom_call" | custom-call | tf_op jit(solution)/shard_map/inner/pallas_call | solution.py:252
  139.6 5.0 %collective-permute-done.66 = f32[16,64,128]{2,1,0:T(8,128)S(1)} collective-permute-done((f32[16,64,128]{2,1,0:T(8,128)S(1)}, f32[16,64,128]{2,1,0:T(8,128)S(1)}, u32[]{:S(2)}, u32[]{:S(2)}) %collective-permute-start.66) | collective-permute-done | bytes 524320 | tf_op jit(solution)/shard_map/ppermute | solution.py:345
  146.4 3.5 %collective-permute-start.68 = (f32[16,16,128]{2,1,0:T(8,128)S(1)}, f32[16,16,128]{2,1,0:T(8,128)S(1)}, u32[]{:S(2)}, u32[]{:S(2)}) collective-permute-start(f32[16,16,128]{2,1,0:T(8,128)S(1)} %get-tuple-element.179), channel_id=1, source_target_pairs={{0,16},{16,32},{32,48},{48,64},{64,80},{80,96},{96,112},{112,128},... | collective-permute-start | bytes 393224 | tf_op jit(solution)/shard_map/ppermute | solution.py:361
  149.9 2.7 %collective-permute-start.69 = (f32[16,16,128]{2,1,0:T(8,128)S(1)}, f32[16,16,128]{2,1,0:T(8,128)S(1)}, u32[]{:S(2)}, u32[]{:S(2)}) collective-permute-start(f32[16,16,128]{2,1,0:T(8,128)S(1)} %get-tuple-element.180), channel_id=1, source_target_pairs={{16,0},{32,16},{48,32},{64,48},{80,64},{96,80},{112,96},{128,112},... | collective-permute-start | bytes 393224 | tf_op jit(solution)/shard_map/ppermute | solution.py:360
  154.1 7.6 %collective-permute-done.69 = f32[16,16,128]{2,1,0:T(8,128)S(1)} collective-permute-done((f32[16,16,128]{2,1,0:T(8,128)S(1)}, f32[16,16,128]{2,1,0:T(8,128)S(1)}, u32[]{:S(2)}, u32[]{:S(2)}) %collective-permute-start.69) | collective-permute-done | bytes 131104 | tf_op jit(solution)/shard_map/ppermute | solution.py:360
  (59 shorter events, 23.3 us)
Async XLA Ops:
  1.0 11.0 %collective-permute-start.62 = (f32[16,16,128]{2,1,0:T(8,128)S(1)}, f32[16,16,128]{2,1,0:T(8,128)S(1)}, u32[]{:S(2)}, u32[]{:S(2)}) collective-permute-start(f32[16,16,128]{2,1,0:T(8,128)S(1)} %get-tuple-element.182), channel_id=1, source_target_pairs={{0,16},{16,32},{32,48},{48,64},{64,80},{80,96},{96,112},{112,128},... | collective-permute-start | bytes 393224 | tf_op jit(solution)/shard_map/ppermute | solution.py:287
  6.3 10.9 %collective-permute-start.63 = (f32[16,16,128]{2,1,0:T(8,128)S(1)}, f32[16,16,128]{2,1,0:T(8,128)S(1)}, u32[]{:S(2)}, u32[]{:S(2)}) collective-permute-start(f32[16,16,128]{2,1,0:T(8,128)S(1)} %get-tuple-element.181), channel_id=1, source_target_pairs={{16,0},{32,16},{48,32},{64,48},{80,64},{96,80},{112,96},{128,112},... | collective-permute-start | bytes 393224 | tf_op jit(solution)/shard_map/ppermute | solution.py:288
  8.2 1.4 copy-start
  12.0 18.3 %copy-start.14 = (f32[16,32,128]{2,1,0:T(8,128)S(1)}, f32[16,32,128]{2,1,0:T(8,128)}, u32[]{:S(2)}) copy-start(f32[16,32,128]{2,1,0:T(8,128)} %param.69) | copy-start | bytes 786436
  17.2 70.2 %all-to-all-start = ((f32[32,4,16,128]{3,2,1,0:T(8,128)}), f32[32,4,16,128]{3,2,1,0:T(8,128)S(1)}, u32[]{:S(2)}, u32[]{:S(2)}) async-start(f32[32,4,16,128]{3,2,1,0:T(8,128)} %get-tuple-element.160), calls=%async_computation | async-start | bytes 2097152 | tf_op jit(solution)/shard_map/all_to_all | solution.py:290
  30.4 8.5 %copy-start.3 = (f32[16,64,128]{2,1,0:T(8,128)}, f32[16,64,128]{2,1,0:T(8,128)S(1)}, u32[]{:S(2)}) copy-start(f32[16,64,128]{2,1,0:T(8,128)S(1)} %constant_dynamic-update-slice_fusion.mid_ref) | copy-start | bytes 1572868
  30.4 57.0 %collective-permute-start.64 = (f32[16,64,128]{2,1,0:T(8,128)S(1)}, f32[16,64,128]{2,1,0:T(8,128)S(1)}, u32[]{:S(2)}, u32[]{:S(2)}) collective-permute-start(f32[16,64,128]{2,1,0:T(8,128)S(1)} %constant_dynamic-update-slice_fusion.mid_ref), channel_id=1, source_target_pairs={{0,1},{1,2},{2,3},{3,4},{4,5},{5,6},{6,7},{7,8},{8,9},{9,10},{10,1... | collective-permute-start | bytes 1572872 | tf_op jit(solution)/shard_map/ppermute | solution.py:292
  32.3 55.0 %collective-permute-start.65 = (f32[16,64,128]{2,1,0:T(8,128)S(1)}, f32[16,64,128]{2,1,0:T(8,128)S(1)}, u32[]{:S(2)}, u32[]{:S(2)}) collective-permute-start(f32[16,64,128]{2,1,0:T(8,128)S(1)} %constant_dynamic-update-slice_fusion.mid_ref), channel_id=1, source_target_pairs={{1,0},{2,1},{3,2},{4,3},{5,4},{6,5},{7,6},{8,7},{9,8},{10,9},{11,1... | collective-permute-start | bytes 1572872 | tf_op jit(solution)/shard_map/ppermute | solution.py:293
  38.9 25.8 %collective-permute-start.29 = (f32[16,32,128]{2,1,0:T(8,128)S(1)}, f32[16,32,128]{2,1,0:T(8,128)S(1)}, u32[]{:S(2)}, u32[]{:S(2)}) collective-permute-start(f32[16,32,128]{2,1,0:T(8,128)S(1)} %param.30), channel_id=1, source_target_pairs={{0,480},{16,496},{32,0},{48,16},{64,32},{80,48},{96,64},{112,80},{... | collective-permute-start | bytes 786440 | tf_op jit(solution)/shard_map/cond/branch_30_fun/ppermute | solution.py:309
  65.4 14.6 %collective-permute-start.55 = (f32[16,32,128]{2,1,0:T(8,128)S(1)}, f32[16,32,128]{2,1,0:T(8,128)S(1)}, u32[]{:S(2)}, u32[]{:S(2)}) collective-permute-start(f32[16,32,128]{2,1,0:T(8,128)S(1)} %param.57), channel_id=1, source_target_pairs={{0,400},{16,416},{32,432},{48,448},{64,464},{80,480},{96,496},{112... | collective-permute-start | bytes 786440 | tf_op jit(solution)/shard_map/cond/branch_25_fun/ppermute | solution.py:309
  80.1 9.2 %copy-start.16 = (f32[16,32,128]{2,1,0:T(8,128)}, f32[16,32,128]{2,1,0:T(8,128)S(1)}, u32[]{:S(2)}) copy-start(f32[16,32,128]{2,1,0:T(8,128)S(1)} %get-tuple-element.186.refs_1_) | copy-start | bytes 786436
  87.3 2.0 %copy-start.5 = (f32[16,64,128]{2,1,0:T(8,128)}, f32[16,64,128]{2,1,0:T(8,128)S(1)}, u32[]{:S(2)}) copy-start(f32[16,64,128]{2,1,0:T(8,128)S(1)} %collective-permute-done.64.low_ref) | copy-start | bytes 1572868
  87.3 2.0 %copy-start.7 = (f32[16,64,128]{2,1,0:T(8,128)}, f32[16,64,128]{2,1,0:T(8,128)S(1)}, u32[]{:S(2)}) copy-start(f32[16,64,128]{2,1,0:T(8,128)S(1)} %collective-permute-done.65.high_ref) | copy-start | bytes 1572868
  89.3 8.0 %copy-start.11 = (f32[6,3,31]{2,1,0:T(4,128)S(1)}, f32[6,3,31]{2,1,0:T(4,128)}, u32[]{:S(2)}) copy-start(f32[6,3,31]{2,1,0:T(4,128)} %taps_ref.9) | copy-start | bytes 6700
  89.4 37.4 %all-to-all-start.1 = ((f32[32,4,16,128]{3,2,1,0:T(8,128)}), f32[32,4,16,128]{3,2,1,0:T(8,128)S(1)}, u32[]{:S(2)}, u32[]{:S(2)}) async-start(f32[32,4,16,128]{3,2,1,0:T(8,128)} %turn.1), calls=%async_computation.1 | async-start | bytes 2097152 | tf_op jit(solution)/shard_map/all_to_all | solution.py:314
  102.1 5.6 %copy-start.12 = (s32[6,1]{0,1:T(1,128)S(1)}, s32[6,1]{0,1:T(1,128)}, u32[]{:S(2)}) copy-start(s32[6,1]{0,1:T(1,128)} %param.73) | copy-start | bytes 76
  102.1 5.6 %copy-start.17 = (f32[16,32,128]{2,1,0:T(8,128)S(1)}, f32[16,32,128]{2,1,0:T(8,128)}, u32[]{:S(2)}) copy-start(f32[16,32,128]{2,1,0:T(8,128)} %copy-done.16) | copy-start | bytes 786436
  102.1 5.6 %copy-start.19 = (f32[16,32,128]{2,1,0:T(8,128)S(1)}, f32[16,32,128]{2,1,0:T(8,128)}, u32[]{:S(2)}) copy-start(f32[16,32,128]{2,1,0:T(8,128)} %copy-done.18) | copy-start | bytes 786436
  126.7 1.2 copy-start.2
  132.2 12.4 %collective-permute-start.66 = (f32[16,64,128]{2,1,0:T(8,128)S(1)}, f32[16,64,128]{2,1,0:T(8,128)S(1)}, u32[]{:S(2)}, u32[]{:S(2)}) collective-permute-start(f32[16,64,128]{2,1,0:T(8,128)S(1)} %get-tuple-element.177), channel_id=1, source_target_pairs={{1,0},{2,1},{3,2},{4,3},{5,4},{6,5},{7,6},{8,7},{9,8},{10,9},{11,1... | collective-permute-start | bytes 1572872 | tf_op jit(solution)/shard_map/ppermute | solution.py:345
  134.1 12.2 %collective-permute-start.67 = (f32[16,64,128]{2,1,0:T(8,128)S(1)}, f32[16,64,128]{2,1,0:T(8,128)S(1)}, u32[]{:S(2)}, u32[]{:S(2)}) collective-permute-start(f32[16,64,128]{2,1,0:T(8,128)S(1)} %get-tuple-element.178), channel_id=1, source_target_pairs={{0,1},{1,2},{2,3},{3,4},{4,5},{5,6},{6,7},{7,8},{8,9},{9,10},{10,1... | collective-permute-start | bytes 1572872 | tf_op jit(solution)/shard_map/ppermute | solution.py:346
  136.6 25.2 %copy-start.15 = (f32[16,32,128]{2,1,0:T(8,128)S(1)}, f32[16,32,128]{2,1,0:T(8,128)}, u32[]{:S(2)}) copy-start(f32[16,32,128]{2,1,0:T(8,128)} %param.69) | copy-start | bytes 786436
  146.4 7.7 %collective-permute-start.68 = (f32[16,16,128]{2,1,0:T(8,128)S(1)}, f32[16,16,128]{2,1,0:T(8,128)S(1)}, u32[]{:S(2)}, u32[]{:S(2)}) collective-permute-start(f32[16,16,128]{2,1,0:T(8,128)S(1)} %get-tuple-element.179), channel_id=1, source_target_pairs={{0,16},{16,32},{32,48},{48,64},{64,80},{80,96},{96,112},{112,128},... | collective-permute-start | bytes 393224 | tf_op jit(solution)/shard_map/ppermute | solution.py:361
  149.9 11.8 %collective-permute-start.69 = (f32[16,16,128]{2,1,0:T(8,128)S(1)}, f32[16,16,128]{2,1,0:T(8,128)S(1)}, u32[]{:S(2)}, u32[]{:S(2)}) collective-permute-start(f32[16,16,128]{2,1,0:T(8,128)S(1)} %get-tuple-element.180), channel_id=1, source_target_pairs={{16,0},{32,16},{48,32},{64,48},{80,64},{96,80},{112,96},{128,112},... | collective-permute-start | bytes 393224 | tf_op jit(solution)/shard_map/ppermute | solution.py:360
  (8 other events, 7.3 us)

commit v8 on v6

--- a/solution.py
+++ b/solution.py
@@ -10,7 +10,7 @@
 F32, BF16 = jnp.float32, jnp.bfloat16
 ROW = 8
 DIRECT = 2
-EARLY = 2
+EARLY = 1
 
 
 def split(values):

time: 164 us -> 163 us (level)
  the two profiles are of different devices: /device:TPU:60 before, /device:TPU:58 now
where the time goes in v8:
time: 163 us; the launch traced here: 160 us
  waiting for transfers between devices  80.2 us (49%)
  starting transfers between devices  50.9 us (31%)
  Pallas kernels  18.2 us (11%)
  local copies, waits for them, and re-layouts  7.41 us (5%)
  other arithmetic  2.12 us (1%)
    ppermute x2, waiting for transfers between devices, send(): return lax.switch(moves[spread_views + slot], hops, x)  47.5 us
    pallas_call x6, Pallas kernels, call(): pl.pallas_call(kernel, out_shape=tuple((jax.ShapeDtypeStruct(shape, dtype...  18.2 us
    all_to_all x1, starting transfers between devices, shards(): spread = lax.all_to_all(pieces, 'brick', 0, 0, tiled=True)  13.1 us
    ppermute x1, waiting for transfers between devices, shards(): low = lax.ppermute(mid, 'stack', up)  11.6 us
    all_to_all x1, starting transfers between devices, shards(): tiles = lax.all_to_all(turned, 'brick', 0, 0, tiled=True)  7.07 us
    ppermute x2, starting transfers between devices, send(): return lax.switch(moves[spread_views + slot], hops, x)  6.88 us
    ppermute x1, waiting for transfers between devices, shards(): from_right = lax.ppermute(faces[0], 'brick', left)  5.69 us
    ppermute x1, starting transfers between devices, shards(): head = lax.ppermute(estimate[:, rows - reach:], 'brick', right)  5.29 us
  transfers between devices with their start and end apart: 12, of which 8 were waited for; matrix products, arithmetic and copies ran while one was open for 1% of the time, Pallas kernels for 7%

profile of v8, /device:TPU:58, one launch (start us, length us, event | category | flops | bytes accessed | tf_op | source)
XLA Modules:
  0.0 160.5 jit_solution(8525539304176642251)
XLA Ops:
  1.0 5.3 %collective-permute-start.62 = (f32[16,16,128]{2,1,0:T(8,128)S(1)}, f32[16,16,128]{2,1,0:T(8,128)S(1)}, u32[]{:S(2)}, u32[]{:S(2)}) collective-permute-start(f32[16,16,128]{2,1,0:T(8,128)S(1)} %get-tuple-element.180), channel_id=1, source_target_pairs={{0,16},{16,32},{32,48},{48,64},{64,80},{80,96},{96,112},{112,128},... | collective-permute-start | bytes 393224 | tf_op jit(solution)/shard_map/ppermute | solution.py:268
  6.3 1.9 %collective-permute-start.63 = (f32[16,16,128]{2,1,0:T(8,128)S(1)}, f32[16,16,128]{2,1,0:T(8,128)S(1)}, u32[]{:S(2)}, u32[]{:S(2)}) collective-permute-start(f32[16,16,128]{2,1,0:T(8,128)S(1)} %get-tuple-element.179), channel_id=1, source_target_pairs={{16,0},{32,16},{48,32},{64,48},{80,64},{96,80},{112,96},{128,112},... | collective-permute-start | bytes 393224 | tf_op jit(solution)/shard_map/ppermute | solution.py:269
  12.1 5.0 %collective-permute-done.63 = f32[16,16,128]{2,1,0:T(8,128)S(1)} collective-permute-done((f32[16,16,128]{2,1,0:T(8,128)S(1)}, f32[16,16,128]{2,1,0:T(8,128)S(1)}, u32[]{:S(2)}, u32[]{:S(2)}) %collective-permute-start.63) | collective-permute-done | bytes 131104 | tf_op jit(solution)/shard_map/ppermute | solution.py:269
  17.2 13.1 %all-to-all-start = ((f32[32,4,16,128]{3,2,1,0:T(8,128)}), f32[32,4,16,128]{3,2,1,0:T(8,128)S(1)}, u32[]{:S(2)}, u32[]{:S(2)}) async-start(f32[32,4,16,128]{3,2,1,0:T(8,128)} %get-tuple-element.159), calls=%async_computation | async-start | bytes 2097152 | tf_op jit(solution)/shard_map/all_to_all | solution.py:271
  30.4 1.9 %collective-permute-start.64 = (f32[16,64,128]{2,1,0:T(8,128)S(1)}, f32[16,64,128]{2,1,0:T(8,128)S(1)}, u32[]{:S(2)}, u32[]{:S(2)}) collective-permute-start(f32[16,64,128]{2,1,0:T(8,128)S(1)} %constant_dynamic-update-slice_fusion.mid_ref), channel_id=1, source_target_pairs={{0,1},{1,2},{2,3},{3,4},{4,5},{5,6},{6,7},{7,8},{8,9},{9,10},{10,1... | collective-permute-start | bytes 1572872 | tf_op jit(solution)/shard_map/ppermute | solution.py:273
  32.3 4.5 %collective-permute-start.65 = (f32[16,64,128]{2,1,0:T(8,128)S(1)}, f32[16,64,128]{2,1,0:T(8,128)S(1)}, u32[]{:S(2)}, u32[]{:S(2)}) collective-permute-start(f32[16,64,128]{2,1,0:T(8,128)S(1)} %constant_dynamic-update-slice_fusion.mid_ref), channel_id=1, source_target_pairs={{1,0},{2,1},{3,2},{4,3},{5,4},{6,5},{7,6},{8,7},{9,8},{10,9},{11,1... | collective-permute-start | bytes 1572872 | tf_op jit(solution)/shard_map/ppermute | solution.py:274
  38.1 27.3 %conditional.2 = (f32[16,32,128]{2,1,0:T(8,128)S(1)}) conditional(s32[]{:T(128)} %bitcast.2, f32[16,32,128]{2,1,0:T(8,128)S(1)} %get-tuple-element.162, f32[16,32,128]{2,1,0:T(8,128)S(1)} %get-tuple-element.162, f32[16,32,128]{2,1,0:T(8,128)S(1)} %get-tuple-element.162, ...), branch_computations={%region_0.0_spmd, %region_1.0_spmd, %region_2.0_spmd, %region_3.0_... | conditional | bytes 1572912 | solution.py:290
  38.1 3.4 %collective-permute-start.30 = (f32[16,32,128]{2,1,0:T(8,128)S(1)}, f32[16,32,128]{2,1,0:T(8,128)S(1)}, u32[]{:S(2)}, u32[]{:S(2)}) collective-permute-start(f32[16,32,128]{2,1,0:T(8,128)S(1)} %param.31), channel_id=1, source_target_pairs={{0,496},{16,0},{32,16},{48,32},{64,48},{80,64},{96,80},{112,96},{1... | collective-permute-start | bytes 786440 | tf_op jit(solution)/shard_map/cond/branch_31_fun/ppermute | solution.py:290
  41.5 23.8 %collective-permute-done.30 = f32[16,32,128]{2,1,0:T(8,128)S(1)} collective-permute-done((f32[16,32,128]{2,1,0:T(8,128)S(1)}, f32[16,32,128]{2,1,0:T(8,128)S(1)}, u32[]{:S(2)}, u32[]{:S(2)}) %collective-permute-start.30) | collective-permute-done | bytes 262176 | tf_op jit(solution)/shard_map/cond/branch_31_fun/ppermute | solution.py:290
  65.4 11.6 %collective-permute-done.64.low_ref = f32[16,64,128]{2,1,0:T(8,128)S(1)} collective-permute-done((f32[16,64,128]{2,1,0:T(8,128)S(1)}, f32[16,64,128]{2,1,0:T(8,128)S(1)}, u32[]{:S(2)}, u32[]{:S(2)}) %collective-permute-start.64) | collective-permute-done | bytes 524320 | tf_op jit(solution)/shard_map/ppermute | solution.py:273
  77.0 2.0 %turn.1 = f32[32,4,16,128]{3,2,1,0:T(8,128)} custom-call(s32[6]{0:T(128)S(1)} %get-tuple-element.157.offsets_ref, f32[32,4,16,128]{3,2,1,0:T(8,128)S(1)} %all-to-all-done.in_ref), custom_call_target="tpu_custom_call" | custom-call | tf_op jit(solution)/shard_map/turn/pallas_call | solution.py:233
  79.0 7.1 %all-to-all-start.1 = ((f32[32,4,16,128]{3,2,1,0:T(8,128)}), f32[32,4,16,128]{3,2,1,0:T(8,128)S(1)}, u32[]{:S(2)}, u32[]{:S(2)}) async-start(f32[32,4,16,128]{3,2,1,0:T(8,128)} %turn.1), calls=%async_computation.1 | async-start | bytes 2097152 | tf_op jit(solution)/shard_map/all_to_all | solution.py:295
  91.3 5.5 %forward.1.refs_3_ = f32[6,16,32,128]{3,2,1,0:T(8,128)S(1)} custom-call(f32[6,3,31]{2,1,0:T(4,128)S(1)} %copy-done.7, f32[16,64,128]{2,1,0:T(8,128)S(1)} %copy-done.4, f32[16,64,128]{2,1,0:T(8,128)S(1)} %constant_dynamic-update-slice_fusion.mid_ref, f32[16,64,128]{2,1,0:T(8,128)S(1)} %copy-done.6, bf16[192,192]{1,0:T(8,128)(2,1)S(1)} %get-tuple-element.167.lateral_ref, ...), custom_call_target="tpu_custom_call" | custom-call | tf_op jit(solution)/shard_map/forward/pallas_call | solution.py:233
  96.9 27.9 %conditional.3 = (f32[16,32,128]{2,1,0:T(8,128)}) conditional(s32[]{:T(128)} %bitcast.4, f32[16,32,128]{2,1,0:T(8,128)} %get-tuple-element.170, f32[16,32,128]{2,1,0:T(8,128)} %get-tuple-element.170, f32[16,32,128]{2,1,0:T(8,128)} %get-tuple-element.170, f32[16,32,128]{2,1,0:T(8,128)} %get-tuple-element.170, ...), branch_computations={%region_32.0_spmd, %region_33.0_spmd, %region_34.0_spmd, %region_3... | conditional | bytes 1572912 | solution.py:290
  97.0 3.5 %collective-permute-start.61 = (f32[16,32,128]{2,1,0:T(8,128)}, f32[16,32,128]{2,1,0:T(8,128)S(1)}, u32[]{:S(2)}, u32[]{:S(2)}) collective-permute-start(f32[16,32,128]{2,1,0:T(8,128)} %param.63), channel_id=1, source_target_pairs={{0,496},{16,0},{32,16},{48,32},{64,48},{80,64},{96,80},{112,96},{1... | collective-permute-start | bytes 786440 | tf_op jit(solution)/shard_map/cond/branch_31_fun/ppermute | solution.py:290
  100.5 23.6 %collective-permute-done.61 = f32[16,32,128]{2,1,0:T(8,128)S(1)} collective-permute-done((f32[16,32,128]{2,1,0:T(8,128)}, f32[16,32,128]{2,1,0:T(8,128)S(1)}, u32[]{:S(2)}, u32[]{:S(2)}) %collective-permute-start.61) | collective-permute-done | bytes 262176 | tf_op jit(solution)/shard_map/cond/branch_31_fun/ppermute | solution.py:290
  124.9 4.2 %outer.1 = (f32[6,16,32,128]{3,2,1,0:T(8,128)S(1)}, f32[16,64,128]{2,1,0:T(8,128)S(1)}, f32[16,64,128]{2,1,0:T(8,128)S(1)}) custom-call(f32[6,3,31]{2,1,0:T(4,128)S(1)} %copy-done.7, s32[6]{0:T(128)S(1)} %bitcast.8, s32[6]{0:T(128)S(1)} %get-tuple-element.156.order_ref, f32[16,2,4,16,128]{4,3,2,1,0:T(8,128)S(1)} %bitcast.6, f32[16,32,128]{2,1,0:T(8,128)} %copy-done.12, ...), custom_call_target="tpu_custom_call" | custom-call | tf_op jit(solution)/shard_map/outer/pallas_call | solution.py:233
  129.0 1.9 %collective-permute-start.66 = (f32[16,64,128]{2,1,0:T(8,128)S(1)}, f32[16,64,128]{2,1,0:T(8,128)S(1)}, u32[]{:S(2)}, u32[]{:S(2)}) collective-permute-start(f32[16,64,128]{2,1,0:T(8,128)S(1)} %get-tuple-element.175), channel_id=1, source_target_pairs={{1,0},{2,1},{3,2},{4,3},{5,4},{6,5},{7,6},{8,7},{9,8},{10,9},{11,1... | collective-permute-start | bytes 1572872 | tf_op jit(solution)/shard_map/ppermute | solution.py:319
  130.9 2.4 %collective-permute-start.67 = (f32[16,64,128]{2,1,0:T(8,128)S(1)}, f32[16,64,128]{2,1,0:T(8,128)S(1)}, u32[]{:S(2)}, u32[]{:S(2)}) collective-permute-start(f32[16,64,128]{2,1,0:T(8,128)S(1)} %get-tuple-element.176), channel_id=1, source_target_pairs={{0,1},{1,2},{2,3},{3,4},{4,5},{5,6},{6,7},{7,8},{8,9},{9,10},{10,1... | collective-permute-start | bytes 1572872 | tf_op jit(solution)/shard_map/ppermute | solution.py:320
  133.4 3.1 %inner.1 = f32[16,64,128]{2,1,0:T(8,128)S(1)} custom-call(f32[6,3,31]{2,1,0:T(4,128)S(1)} %copy-done.7, f32[6,16,32,128]{3,2,1,0:T(8,128)S(1)} %get-tuple-element.174.near_ref, bf16[128,192]{1,0:T(8,128)(2,1)S(1)} %get-tuple-element.173.refs_5_.lateral_ref), custom_call_target="tpu_custom_call" | custom-call | tf_op jit(solution)/shard_map/inner/pallas_call | solution.py:233
  136.4 4.9 %collective-permute-done.66 = f32[16,64,128]{2,1,0:T(8,128)S(1)} collective-permute-done((f32[16,64,128]{2,1,0:T(8,128)S(1)}, f32[16,64,128]{2,1,0:T(8,128)S(1)}, u32[]{:S(2)}, u32[]{:S(2)}) %collective-permute-start.66) | collective-permute-done | bytes 524320 | tf_op jit(solution)/shard_map/ppermute | solution.py:319
  141.4 5.1 %collective-permute-done.67 = f32[16,64,128]{2,1,0:T(8,128)S(1)} collective-permute-done((f32[16,64,128]{2,1,0:T(8,128)S(1)}, f32[16,64,128]{2,1,0:T(8,128)S(1)}, u32[]{:S(2)}, u32[]{:S(2)}) %collective-permute-start.67) | collective-permute-done | bytes 524320 | tf_op jit(solution)/shard_map/ppermute | solution.py:320
  148.4 3.9 %collective-permute-start.69 = (f32[16,16,128]{2,1,0:T(8,128)S(1)}, f32[16,16,128]{2,1,0:T(8,128)S(1)}, u32[]{:S(2)}, u32[]{:S(2)}) collective-permute-start(f32[16,16,128]{2,1,0:T(8,128)S(1)} %get-tuple-element.178), channel_id=1, source_target_pairs={{16,0},{32,16},{48,32},{64,48},{80,64},{96,80},{112,96},{128,112},... | collective-permute-start | bytes 393224 | tf_op jit(solution)/shard_map/ppermute | solution.py:334
  153.4 5.7 %collective-permute-done.69 = f32[16,16,128]{2,1,0:T(8,128)S(1)} collective-permute-done((f32[16,16,128]{2,1,0:T(8,128)S(1)}, f32[16,16,128]{2,1,0:T(8,128)S(1)}, u32[]{:S(2)}, u32[]{:S(2)}) %collective-permute-start.69) | collective-permute-done | bytes 131104 | tf_op jit(solution)/shard_map/ppermute | solution.py:334
  (44 shorter events, 15.3 us)
Async XLA Ops:
  1.0 11.1 %collective-permute-start.62 = (f32[16,16,128]{2,1,0:T(8,128)S(1)}, f32[16,16,128]{2,1,0:T(8,128)S(1)}, u32[]{:S(2)}, u32[]{:S(2)}) collective-permute-start(f32[16,16,128]{2,1,0:T(8,128)S(1)} %get-tuple-element.180), channel_id=1, source_target_pairs={{0,16},{16,32},{32,48},{48,64},{64,80},{80,96},{96,112},{112,128},... | collective-permute-start | bytes 393224 | tf_op jit(solution)/shard_map/ppermute | solution.py:268
  6.3 10.9 %collective-permute-start.63 = (f32[16,16,128]{2,1,0:T(8,128)S(1)}, f32[16,16,128]{2,1,0:T(8,128)S(1)}, u32[]{:S(2)}, u32[]{:S(2)}) collective-permute-start(f32[16,16,128]{2,1,0:T(8,128)S(1)} %get-tuple-element.179), channel_id=1, source_target_pairs={{16,0},{32,16},{48,32},{64,48},{80,64},{96,80},{112,96},{128,112},... | collective-permute-start | bytes 393224 | tf_op jit(solution)/shard_map/ppermute | solution.py:269
  8.2 1.4 copy-start
  12.1 18.2 %copy-start.10 = (f32[16,32,128]{2,1,0:T(8,128)S(1)}, f32[16,32,128]{2,1,0:T(8,128)}, u32[]{:S(2)}) copy-start(f32[16,32,128]{2,1,0:T(8,128)} %param.69) | copy-start | bytes 786436
  17.2 59.8 %all-to-all-start = ((f32[32,4,16,128]{3,2,1,0:T(8,128)}), f32[32,4,16,128]{3,2,1,0:T(8,128)S(1)}, u32[]{:S(2)}, u32[]{:S(2)}) async-start(f32[32,4,16,128]{3,2,1,0:T(8,128)} %get-tuple-element.159), calls=%async_computation | async-start | bytes 2097152 | tf_op jit(solution)/shard_map/all_to_all | solution.py:271
  30.4 46.6 %collective-permute-start.64 = (f32[16,64,128]{2,1,0:T(8,128)S(1)}, f32[16,64,128]{2,1,0:T(8,128)S(1)}, u32[]{:S(2)}, u32[]{:S(2)}) collective-permute-start(f32[16,64,128]{2,1,0:T(8,128)S(1)} %constant_dynamic-update-slice_fusion.mid_ref), channel_id=1, source_target_pairs={{0,1},{1,2},{2,3},{3,4},{4,5},{5,6},{6,7},{7,8},{8,9},{9,10},{10,1... | collective-permute-start | bytes 1572872 | tf_op jit(solution)/shard_map/ppermute | solution.py:273
  32.3 44.7 %collective-permute-start.65 = (f32[16,64,128]{2,1,0:T(8,128)S(1)}, f32[16,64,128]{2,1,0:T(8,128)S(1)}, u32[]{:S(2)}, u32[]{:S(2)}) collective-permute-start(f32[16,64,128]{2,1,0:T(8,128)S(1)} %constant_dynamic-update-slice_fusion.mid_ref), channel_id=1, source_target_pairs={{1,0},{2,1},{3,2},{4,3},{5,4},{6,5},{7,6},{8,7},{9,8},{10,9},{11,1... | collective-permute-start | bytes 1572872 | tf_op jit(solution)/shard_map/ppermute | solution.py:274
  38.1 27.2 %collective-permute-start.30 = (f32[16,32,128]{2,1,0:T(8,128)S(1)}, f32[16,32,128]{2,1,0:T(8,128)S(1)}, u32[]{:S(2)}, u32[]{:S(2)}) collective-permute-start(f32[16,32,128]{2,1,0:T(8,128)S(1)} %param.31), channel_id=1, source_target_pairs={{0,496},{16,0},{32,16},{48,32},{64,48},{80,64},{96,80},{112,96},{1... | collective-permute-start | bytes 786440 | tf_op jit(solution)/shard_map/cond/branch_31_fun/ppermute | solution.py:290
  65.4 13.6 %copy-start.12 = (f32[16,32,128]{2,1,0:T(8,128)}, f32[16,32,128]{2,1,0:T(8,128)S(1)}, u32[]{:S(2)}) copy-start(f32[16,32,128]{2,1,0:T(8,128)S(1)} %get-tuple-element.183.refs_1_) | copy-start | bytes 786436
  77.0 2.0 %copy-start.3 = (f32[16,64,128]{2,1,0:T(8,128)}, f32[16,64,128]{2,1,0:T(8,128)S(1)}, u32[]{:S(2)}) copy-start(f32[16,64,128]{2,1,0:T(8,128)S(1)} %collective-permute-done.64.low_ref) | copy-start | bytes 1572868
  77.0 2.0 %copy-start.5 = (f32[16,64,128]{2,1,0:T(8,128)}, f32[16,64,128]{2,1,0:T(8,128)S(1)}, u32[]{:S(2)}) copy-start(f32[16,64,128]{2,1,0:T(8,128)S(1)} %collective-permute-done.65.high_ref) | copy-start | bytes 1572868
  79.0 7.1 %copy-start.7 = (f32[6,3,31]{2,1,0:T(4,128)S(1)}, f32[6,3,31]{2,1,0:T(4,128)}, u32[]{:S(2)}) copy-start(f32[6,3,31]{2,1,0:T(4,128)} %taps_ref.7) | copy-start | bytes 6700
  79.0 45.8 %all-to-all-start.1 = ((f32[32,4,16,128]{3,2,1,0:T(8,128)}), f32[32,4,16,128]{3,2,1,0:T(8,128)S(1)}, u32[]{:S(2)}, u32[]{:S(2)}) async-start(f32[32,4,16,128]{3,2,1,0:T(8,128)} %turn.1), calls=%async_computation.1 | async-start | bytes 2097152 | tf_op jit(solution)/shard_map/all_to_all | solution.py:295
  87.7 0.9 copy-start.1
  89.3 1.0 copy-start.4
  90.3 1.0 copy-start.6
  96.9 28.0 %copy-start.2 = (bf16[6,256,256]{2,1,0:T(8,128)(2,1)S(1)}, bf16[6,256,256]{2,1,0:T(8,128)(2,1)}, u32[]{:S(2)}) copy-start(bf16[6,256,256]{2,1,0:T(8,128)(2,1)} %copy-done.1) | copy-start | bytes 2359300
  96.9 28.0 %copy-start.9 = (s32[6,1]{0,1:T(1,128)S(1)}, s32[6,1]{0,1:T(1,128)}, u32[]{:S(2)}) copy-start(s32[6,1]{0,1:T(1,128)} %param.73) | copy-start | bytes 76
  97.0 27.2 %collective-permute-start.61 = (f32[16,32,128]{2,1,0:T(8,128)}, f32[16,32,128]{2,1,0:T(8,128)S(1)}, u32[]{:S(2)}, u32[]{:S(2)}) collective-permute-start(f32[16,32,128]{2,1,0:T(8,128)} %param.63), channel_id=1, source_target_pairs={{0,496},{16,0},{32,16},{48,32},{64,48},{80,64},{96,80},{112,96},{1... | collective-permute-start | bytes 786440 | tf_op jit(solution)/shard_map/cond/branch_31_fun/ppermute | solution.py:290
  129.0 12.4 %collective-permute-start.66 = (f32[16,64,128]{2,1,0:T(8,128)S(1)}, f32[16,64,128]{2,1,0:T(8,128)S(1)}, u32[]{:S(2)}, u32[]{:S(2)}) collective-permute-start(f32[16,64,128]{2,1,0:T(8,128)S(1)} %get-tuple-element.175), channel_id=1, source_target_pairs={{1,0},{2,1},{3,2},{4,3},{5,4},{6,5},{7,6},{8,7},{9,8},{10,9},{11,1... | collective-permute-start | bytes 1572872 | tf_op jit(solution)/shard_map/ppermute | solution.py:319
  130.9 15.5 %collective-permute-start.67 = (f32[16,64,128]{2,1,0:T(8,128)S(1)}, f32[16,64,128]{2,1,0:T(8,128)S(1)}, u32[]{:S(2)}, u32[]{:S(2)}) collective-permute-start(f32[16,64,128]{2,1,0:T(8,128)S(1)} %get-tuple-element.176), channel_id=1, source_target_pairs={{0,1},{1,2},{2,3},{3,4},{4,5},{5,6},{6,7},{7,8},{8,9},{9,10},{10,1... | collective-permute-start | bytes 1572872 | tf_op jit(solution)/shard_map/ppermute | solution.py:320
  133.4 25.7 %copy-start.11 = (f32[16,32,128]{2,1,0:T(8,128)S(1)}, f32[16,32,128]{2,1,0:T(8,128)}, u32[]{:S(2)}) copy-start(f32[16,32,128]{2,1,0:T(8,128)} %param.69) | copy-start | bytes 786436
  146.5 6.9 %collective-permute-start.68 = (f32[16,16,128]{2,1,0:T(8,128)S(1)}, f32[16,16,128]{2,1,0:T(8,128)S(1)}, u32[]{:S(2)}, u32[]{:S(2)}) collective-permute-start(f32[16,16,128]{2,1,0:T(8,128)S(1)} %get-tuple-element.177), channel_id=1, source_target_pairs={{0,16},{16,32},{32,48},{48,64},{64,80},{80,96},{96,112},{112,128},... | collective-permute-start | bytes 393224 | tf_op jit(solution)/shard_map/ppermute | solution.py:335
  148.4 10.6 %collective-permute-start.69 = (f32[16,16,128]{2,1,0:T(8,128)S(1)}, f32[16,16,128]{2,1,0:T(8,128)S(1)}, u32[]{:S(2)}, u32[]{:S(2)}) collective-permute-start(f32[16,16,128]{2,1,0:T(8,128)S(1)} %get-tuple-element.178), channel_id=1, source_target_pairs={{16,0},{32,16},{48,32},{64,48},{80,64},{96,80},{112,96},{128,112},... | collective-permute-start | bytes 393224 | tf_op jit(solution)/shard_map/ppermute | solution.py:334
  (1 other events, 0.7 us)
